TPU v7x, 32 devices: a whole 2x2x4 slice. The times are simulated.
32 devices in a mesh: batch: 4 (over x, core), seq: 8 (over z, y).
Axes of the slice: x: 2, y: 2, z: 4, core: 2. Of those that a mesh axis runs over, the one named last changes fastest.
Arguments:
- inputs: bfloat16 [4, 1024, 768], P('batch', 'seq'), may hold values from -6 to 6
- pre_gain: bfloat16 [768], replicated, may hold values from 0.5 to 1.5
- pre_bias: bfloat16 [768], replicated, may hold values from -1.75 to 1.75
- in_weight: bfloat16 [768, 2304], replicated, may hold values from -0.21875 to 0.21875
- input_projection_bias: bfloat16 [2304], replicated, may hold values from -1.75 to 1.75
- short_weight: bfloat16 [3, 2304], replicated, may hold values from -3.5 to 3.5
- short_bias: bfloat16 [2304], replicated, may hold values from -1.75 to 1.75
- pos_weight: bfloat16 [33, 64], replicated, may hold values from -1 to 1
- pos_bias: bfloat16 [64], replicated, may hold values from -3 to 3
- inner_weight: bfloat16 [64, 64], replicated, may hold values from -0.75 to 0.75
- inner_bias: bfloat16 [64], replicated, may hold values from -3 to 3
- filter_third_weight: bfloat16 [64, 64], replicated, may hold values from -0.75 to 0.75
- third_bias: bfloat16 [64], replicated, may hold values from -3 to 3
- sine_freq: bfloat16 [64], replicated, may hold values from 0.5 to 1.5
- filter_weight: bfloat16 [2, 64, 768], replicated, may hold values from -0.09375 to 0.09375
- decay_rates: float32 [2, 768], replicated, may hold values from 0.5 to 32
- skip_gains: bfloat16 [2, 768], replicated, may hold values from -6 to 6
- out_weight: bfloat16 [768, 768], replicated, may hold values from -0.21875 to 0.21875
- out_bias: bfloat16 [768], replicated, may hold values from -1.75 to 1.75
- post_gain: bfloat16 [768], replicated, may hold values from 0.5 to 1.5
- post_bias: bfloat16 [768], replicated, may hold values from -1.75 to 1.75
- up_weight: bfloat16 [768, 3072], replicated, may hold values from -0.21875 to 0.21875
- up_bias: bfloat16 [3072], replicated, may hold values from -1.75 to 1.75
- down_weight: bfloat16 [3072, 768], replicated, may hold values from -0.109375 to 0.109375
- down_bias: bfloat16 [768], replicated, may hold values from -1.75 to 1.75
- cotangent: bfloat16 [4, 1024, 768], P('batch', 'seq'), may hold values from -6 to 6
Outputs:
- outputs: float32 [4, 1024, 768], P('batch', 'seq')
- grad_inputs: float32 [4, 1024, 768], P('batch', 'seq')
- grad_pre_gain: float32 [768], replicated
- grad_pre_bias: float32 [768], replicated
- grad_in_weight: float32 [768, 2304], P('seq')
- grad_in_bias: float32 [2304], replicated
- grad_short_weight: float32 [3, 2304], replicated
- grad_short_bias: float32 [2304], replicated
- grad_pos_weight: float32 [33, 64], replicated
- grad_pos_bias: float32 [64], replicated
- grad_inner_weight: float32 [64, 64], replicated
- grad_inner_bias: float32 [64], replicated
- grad_third_weight: float32 [64, 64], replicated
- grad_third_bias: float32 [64], replicated
- grad_sine_freq: float32 [64], replicated
- grad_filter_weight: float32 [2, 64, 768], P(None, None, 'seq')
- grad_decay_rates: float32 [2, 768], P(None, 'seq')
- grad_skip_gains: float32 [2, 768], P(None, 'seq')
- grad_out_weight: float32 [768, 768], P('seq')
- grad_out_bias: float32 [768], replicated
- grad_post_gain: float32 [768], replicated
- grad_post_bias: float32 [768], replicated
- up_weight_gradient: float32 [768, 3072], P('seq')
- grad_up_bias: float32 [3072], replicated
- grad_down_weight: float32 [3072, 768], P('seq')
- grad_down_bias: float32 [768], replicated
All inputs are finite; a program needn't handle non-finite values.
Results may differ from a plain program's by a relative error of at most 0.013.
Values may be sent and summed in bfloat16 or wider, within the bound.
No kernel may reach another device: no remote copies, remote signals or barrier semaphores. Data moves between devices by JAX's collectives and lax.ppermute only.
A program may use at most 192 MiB of HBM per device.

v0:
```python
import math

import jax
import jax.numpy as jnp
from jax import lax
from jax.sharding import PartitionSpec as P

epsilon = 1e-05
highest_accuracy = lax.Precision.HIGHEST


def passed_along(value, axis, steps):
    count = lax.axis_size(axis)
    initial, last = (max(0, -steps), min(count, count - steps))
    return lax.ppermute(value, axis, [(source, source + steps) for source in range(initial, last)])


def plain_dot(left_side, right_side):
    return jnp.dot(left_side, right_side, preferred_element_type=jnp.float32)


def exact_tdot(left_side, right_side):
    return lax.dot_general(
        left_side,
        right_side,
        (((0,), (0,)), ((), ())),
        precision=highest_accuracy,
        preferred_element_type=jnp.float32,
    )


def left_dot(left_side, right_side):
    return lax.dot_general(
        left_side, right_side, (((0,), (0,)), ((), ())), preferred_element_type=jnp.float32
    )


def right_dot(left_side, right_side):
    return lax.dot_general(
        left_side, right_side, (((1,), (1,)), ((), ())), preferred_element_type=jnp.float32
    )


def rounded(values):
    return lax.optimization_barrier(values.astype(jnp.bfloat16)).astype(jnp.float32)


def norm_forward(values, gain_vec, shift_vec):
    centre = values - jnp.mean(values, axis=-1, keepdims=True)
    inv_std = lax.rsqrt(jnp.mean(centre * centre, axis=-1, keepdims=True) + epsilon)
    unit_rows = centre * inv_std
    return (unit_rows * gain_vec + shift_vec, unit_rows, inv_std)


def norm_backward(grad_out, unit_rows, inv_std, gain_vec):
    grad_unit = grad_out * gain_vec
    grad_values = inv_std * (
        grad_unit
        - jnp.mean(grad_unit, axis=-1, keepdims=True)
        - unit_rows * jnp.mean(grad_unit * unit_rows, axis=-1, keepdims=True)
    )
    return (grad_values, jnp.sum(grad_out * unit_rows, axis=0), jnp.sum(grad_out, axis=0))


def position_rows(length, feat_count):
    steps_pos = jnp.arange(length, dtype=jnp.float32)
    time_steps = steps_pos / (length - 1)
    band_count = (feat_count - 1) // 2
    frequency = jnp.linspace(0.0001, band_count - 1, band_count, dtype=jnp.float32)
    angles = frequency[:, None] * (steps_pos * (2.0 * math.pi / length))[None, :]
    features_t = jnp.concatenate([time_steps[None, :], jnp.cos(angles), -jnp.sin(angles)], axis=0)
    return (features_t, time_steps)


def body_filters(
    features_t,
    time_steps,
    pos_weight,
    pos_bias,
    inner_weight,
    inner_bias,
    filter_third_weight,
    third_bias,
    sine_freq,
    weight_local,
    rates_local,
):
    hidden = jnp.sin(sine_freq[:, None] * (exact_tdot(pos_weight, features_t) + pos_bias[:, None]))
    hidden = jnp.sin(sine_freq[:, None] * (exact_tdot(inner_weight, hidden) + inner_bias[:, None]))
    hidden = jnp.sin(
        sine_freq[:, None] * (exact_tdot(filter_third_weight, hidden) + third_bias[:, None])
    )
    first_kernel = exact_tdot(weight_local[0], hidden) * jnp.exp(
        -rates_local[0][:, None] * time_steps[None, :]
    )
    second_kernel = exact_tdot(weight_local[1], hidden) * jnp.exp(
        -rates_local[1][:, None] * time_steps[None, :]
    )
    return (first_kernel, second_kernel)


def split_sizes(extent):
    outer_size = math.gcd(extent // 2, 1 << (extent.bit_length() - 1) // 2)
    return (outer_size, extent // outer_size)


def dft_rect(row_count, col_count, modulus, direction):
    row_ids = jnp.arange(row_count, dtype=jnp.int32)[:, None]
    col_ids = jnp.arange(col_count, dtype=jnp.int32)[None, :]
    angles = (row_ids * col_ids % modulus).astype(jnp.float32) * (2.0 * math.pi / modulus)
    return (jnp.cos(angles), direction * jnp.sin(angles))


def first_section(block_groups, lookup_grid):
    return jnp.einsum(
        "cij,ik->ckj",
        block_groups,
        lookup_grid,
        precision=highest_accuracy,
        preferred_element_type=jnp.float32,
    )


def second_section(block_groups, lookup_grid):
    return jnp.einsum(
        "dhq,qn->dnh",
        block_groups,
        lookup_grid,
        precision=highest_accuracy,
        preferred_element_type=jnp.float32,
    )


def padded_spectrum(signal):
    channels, length = signal.shape
    extent = 2 * length
    outer_size, inner_size = split_sizes(extent)
    block_groups = signal.reshape(channels, inner_size // 2, outer_size)
    cos_inner, sin_inner = dft_rect(inner_size // 2, inner_size, inner_size, -1.0)
    section_real = first_section(block_groups, cos_inner)
    section_imag = first_section(block_groups, sin_inner)
    twist_cos, rotation_sine = dft_rect(inner_size, outer_size, extent, -1.0)
    turned_real = section_real * twist_cos - section_imag * rotation_sine
    turned_imag = section_real * rotation_sine + section_imag * twist_cos
    cos_outer, sin_outer = dft_rect(outer_size, outer_size, outer_size, -1.0)
    out_real = second_section(turned_real, cos_outer) - second_section(turned_imag, sin_outer)
    out_imag = second_section(turned_real, sin_outer) + second_section(turned_imag, cos_outer)
    return (out_real.reshape(channels, extent), out_imag.reshape(channels, extent))


def inverse_real(spec_real, spec_imag):
    channels, extent = spec_real.shape
    outer_size, inner_size = split_sizes(extent)
    blocks_real = spec_real.reshape(channels, inner_size, outer_size)
    blocks_imag = spec_imag.reshape(channels, inner_size, outer_size)
    cos_inner, sin_inner = dft_rect(inner_size, inner_size, inner_size, 1.0)
    section_real = first_section(blocks_real, cos_inner) - first_section(blocks_imag, sin_inner)
    section_imag = first_section(blocks_real, sin_inner) + first_section(blocks_imag, cos_inner)
    twist_cos, rotation_sine = dft_rect(inner_size, outer_size, extent, 1.0)
    turned_real = section_real * twist_cos - section_imag * rotation_sine
    turned_imag = section_real * rotation_sine + section_imag * twist_cos
    cos_outer, sin_outer = dft_rect(outer_size, outer_size // 2, outer_size, 1.0)
    out_real = second_section(turned_real, cos_outer) - second_section(turned_imag, sin_outer)
    return out_real.reshape(channels, extent // 2) / extent


def times_spec(left_real, left_imag, right_real, right_imag):
    return (
        left_real * right_real - left_imag * right_imag,
        left_real * right_imag + left_imag * right_real,
    )


def times_conj(left_real, left_imag, right_real, right_imag):
    return (
        left_real * right_real + left_imag * right_imag,
        left_imag * right_real - left_real * right_imag,
    )


def per_device(
    inputs,
    pre_gain,
    pre_bias,
    in_weight,
    input_projection_bias,
    short_weight,
    short_bias,
    pos_weight,
    pos_bias,
    inner_weight,
    inner_bias,
    filter_third_weight,
    third_bias,
    sine_freq,
    filter_weight,
    decay_rates,
    skip_gains,
    out_weight,
    out_bias,
    post_gain,
    post_bias,
    up_weight,
    up_bias,
    down_weight,
    down_bias,
    cotangent,
):
    seq_parts = lax.axis_size("seq")
    seq_rank = lax.axis_index("seq")
    tokens = inputs[0]
    tok_count = tokens.shape[0]
    model_width = tokens.shape[1]
    length = tok_count * seq_parts
    channels = model_width // seq_parts
    tokens_wide = tokens.astype(jnp.float32)
    pre_gain_f = pre_gain.astype(jnp.float32)
    pre_bias_f = pre_bias.astype(jnp.float32)
    in_bias_f = input_projection_bias.astype(jnp.float32)
    short_f = short_weight.astype(jnp.float32)
    short_bias_f = short_bias.astype(jnp.float32)
    out_bias_f = out_bias.astype(jnp.float32)
    post_gain_f = post_gain.astype(jnp.float32)
    post_bias_f = post_bias.astype(jnp.float32)
    up_bias_f = up_bias.astype(jnp.float32)
    down_bias_f = down_bias.astype(jnp.float32)
    normed, unit_pre, inv_pre = norm_forward(tokens_wide, pre_gain_f, pre_bias_f)
    normed_low = normed.astype(jnp.bfloat16)
    projected = plain_dot(normed_low, in_weight) + in_bias_f
    previous = passed_along(projected[tok_count - 2 :], "seq", 1)
    extended = jnp.concatenate([previous, projected], axis=0)
    mixed_conv = (
        short_f[0] * extended[:-2]
        + short_f[1] * extended[1:-1]
        + short_f[2] * extended[2:]
        + short_bias_f
    )
    value_part = mixed_conv[:, :model_width]
    gate_one = mixed_conv[:, model_width : 2 * model_width]
    gate_two = mixed_conv[:, 2 * model_width :]
    product_low = (value_part * gate_one).astype(jnp.bfloat16)
    gate_two_low = gate_two.astype(jnp.bfloat16)
    prod_chan, gate_chan = (
        lax.all_to_all(product_low.T, "seq", split_axis=0, concat_axis=1, tiled=True),
        lax.all_to_all(gate_two_low.T, "seq", split_axis=0, concat_axis=1, tiled=True),
    )
    features_t, time_steps = position_rows(length, pos_weight.shape[0])
    chan_start = seq_rank * channels
    weight_local = lax.dynamic_slice_in_dim(
        filter_weight.astype(jnp.float32), chan_start, channels, 2
    )
    rates_local = lax.dynamic_slice_in_dim(decay_rates, chan_start, channels, 1)
    skips_local = lax.dynamic_slice_in_dim(skip_gains.astype(jnp.float32), chan_start, channels, 1)
    skip_one = skips_local[0][:, None]
    skip_two = skips_local[1][:, None]
    shared = tuple(
        (
            member.astype(jnp.float32)
            for member in (
                pos_weight,
                pos_bias,
                inner_weight,
                inner_bias,
                filter_third_weight,
                third_bias,
                sine_freq,
            )
        )
    )

    def local_filters(*params):
        return body_filters(features_t, time_steps, *params)

    (kernel_one, kernel_two), filter_pull = jax.vjp(
        local_filters, *shared, weight_local, rates_local
    )
    prod_wide = prod_chan.astype(jnp.float32)
    gate_wide = gate_chan.astype(jnp.float32)
    prod_real, prod_imag = padded_spectrum(prod_wide)
    kone_real, kone_imag = padded_spectrum(kernel_one)
    convolved_real_part, conv_imag = times_spec(prod_real, prod_imag, kone_real, kone_imag)
    after_one = rounded(inverse_real(convolved_real_part, conv_imag) + skip_one * prod_wide)
    gated_low = rounded(after_one * gate_wide)
    gated_real, gated_imag = padded_spectrum(gated_low)
    ktwo_real, ktwo_imag = padded_spectrum(kernel_two)
    convolved_real_part, conv_imag = times_spec(gated_real, gated_imag, ktwo_real, ktwo_imag)
    mixer_chan = (inverse_real(convolved_real_part, conv_imag) + skip_two * gated_low).astype(
        jnp.bfloat16
    )
    mixer_tok = lax.all_to_all(mixer_chan, "seq", split_axis=1, concat_axis=0, tiled=True).T
    branch = plain_dot(mixer_tok, out_weight) + out_bias_f
    residual = tokens_wide + branch
    normed_two, unit_post, inv_post = norm_forward(residual, post_gain_f, post_bias_f)
    normed_two_low = normed_two.astype(jnp.bfloat16)
    upper_pre = plain_dot(normed_two_low, up_weight) + up_bias_f
    activated = jax.nn.gelu(upper_pre, approximate=False).astype(jnp.bfloat16)
    outputs = residual + plain_dot(activated, down_weight) + down_bias_f
    grad_top = cotangent[0]
    grad_top_wide = grad_top.astype(jnp.float32)
    grad_act = right_dot(grad_top, down_weight)
    grad_down = left_dot(activated, grad_top)
    grad_down_bias = jnp.sum(grad_top_wide, axis=0)
    gelu_slope = (
        0.5 * (1.0 + lax.erf(upper_pre * 0.7071067811865476))
        + upper_pre * jnp.exp(-0.5 * upper_pre * upper_pre) * 0.3989422804014327
    )
    grad_upper = (grad_act * gelu_slope).astype(jnp.bfloat16)
    grad_up = left_dot(normed_two_low, grad_upper)
    grad_up_bias = jnp.sum(grad_upper.astype(jnp.float32), axis=0)
    grad_normed_two = right_dot(grad_upper, up_weight)
    grad_resid_norm, grad_post_gain, grad_post_bias = norm_backward(
        grad_normed_two, unit_post, inv_post, post_gain_f
    )
    grad_residual = grad_top_wide + grad_resid_norm
    grad_branch = grad_residual.astype(jnp.bfloat16)
    grad_out = left_dot(mixer_tok, grad_branch)
    grad_out_bias = jnp.sum(grad_branch.astype(jnp.float32), axis=0)
    grad_mixer = right_dot(grad_branch, out_weight).astype(jnp.bfloat16)
    grad_mixer_chan = lax.all_to_all(
        grad_mixer.T, "seq", split_axis=0, concat_axis=1, tiled=True
    ).astype(jnp.float32)
    gmix_real, gmix_imag = padded_spectrum(grad_mixer_chan)
    corr_real, corr_imag = times_conj(gmix_real, gmix_imag, ktwo_real, ktwo_imag)
    grad_gated = rounded(inverse_real(corr_real, corr_imag) + skip_two * grad_mixer_chan)
    corr_real, corr_imag = times_conj(gmix_real, gmix_imag, gated_real, gated_imag)
    grad_kernel_two = inverse_real(corr_real, corr_imag)
    grad_skip_two = jnp.sum(grad_mixer_chan * gated_low, axis=1)
    grad_after = rounded(grad_gated * gate_wide)
    grad_gate_two = (grad_gated * after_one).astype(jnp.bfloat16)
    gaft_real, gaft_imag = padded_spectrum(grad_after)
    corr_real, corr_imag = times_conj(gaft_real, gaft_imag, kone_real, kone_imag)
    grad_product = (inverse_real(corr_real, corr_imag) + skip_one * grad_after).astype(jnp.bfloat16)
    corr_real, corr_imag = times_conj(gaft_real, gaft_imag, prod_real, prod_imag)
    grad_kernel_one = inverse_real(corr_real, corr_imag)
    grad_skip_one = jnp.sum(grad_after * prod_wide, axis=1)
    filter_grads = filter_pull((grad_kernel_one, grad_kernel_two))
    grad_prod_back, grad_gate_back = (
        lax.all_to_all(grad_product, "seq", split_axis=1, concat_axis=0, tiled=True),
        lax.all_to_all(grad_gate_two, "seq", split_axis=1, concat_axis=0, tiled=True),
    )
    grad_prod_wide = grad_prod_back.T.astype(jnp.float32)
    grad_mixed = jnp.concatenate(
        [
            grad_prod_wide * gate_one,
            grad_prod_wide * value_part,
            grad_gate_back.T.astype(jnp.float32),
        ],
        axis=1,
    )
    grad_short_bias = jnp.sum(grad_mixed, axis=0)
    grad_short = jnp.stack(
        [
            jnp.sum(grad_mixed * extended[0:tok_count], axis=0),
            jnp.sum(grad_mixed * extended[1 : tok_count + 1], axis=0),
            jnp.sum(grad_mixed * extended[2 : tok_count + 2], axis=0),
        ]
    )
    zero_rows = jnp.zeros((2, 3 * model_width), jnp.float32)
    padded_grad = jnp.concatenate([zero_rows, grad_mixed, zero_rows], axis=0)
    grad_extended = (
        short_f[0] * padded_grad[2:]
        + short_f[1] * padded_grad[1:-1]
        + short_f[2] * padded_grad[:-2]
    )
    from_next = passed_along(grad_extended[:2], "seq", -1)
    grad_projected = grad_extended[2:].at[tok_count - 2 :].add(from_next)
    grad_proj_low = grad_projected.astype(jnp.bfloat16)
    grad_in = left_dot(normed_low, grad_proj_low)
    grad_in_bias = jnp.sum(grad_proj_low.astype(jnp.float32), axis=0)
    grad_normed = right_dot(grad_proj_low, in_weight)
    grad_tokens_norm, grad_pre_gain, grad_pre_bias = norm_backward(
        grad_normed, unit_pre, inv_pre, pre_gain_f
    )
    grad_inputs = grad_residual + grad_tokens_norm
    shared_sums = lax.psum(
        (
            grad_pre_gain,
            grad_pre_bias,
            grad_in_bias,
            grad_short,
            grad_short_bias,
            filter_grads[0],
            filter_grads[1],
            filter_grads[2],
            filter_grads[3],
            filter_grads[4],
            filter_grads[5],
            filter_grads[6],
            grad_out_bias,
            grad_post_gain,
            grad_post_bias,
            grad_up_bias,
            grad_down_bias,
        ),
        ("batch", "seq"),
    )
    skip_grads = jnp.stack([grad_skip_one, grad_skip_two])
    weight_shards = (
        lax.psum_scatter(grad_in, "seq", scatter_dimension=0, tiled=True),
        lax.psum_scatter(grad_out, "seq", scatter_dimension=0, tiled=True),
        lax.psum_scatter(grad_up, "seq", scatter_dimension=0, tiled=True),
        lax.psum_scatter(grad_down, "seq", scatter_dimension=0, tiled=True),
    )
    final_in, final_out, final_up, final_down, final_filter, final_rates, final_skips = (
        lax.psum(weight_shards[0].astype(jnp.bfloat16), "batch").astype(jnp.float32),
        lax.psum(weight_shards[1].astype(jnp.bfloat16), "batch").astype(jnp.float32),
        lax.psum(weight_shards[2].astype(jnp.bfloat16), "batch").astype(jnp.float32),
        lax.psum(weight_shards[3].astype(jnp.bfloat16), "batch").astype(jnp.float32),
        lax.psum(filter_grads[7].astype(jnp.bfloat16), "batch").astype(jnp.float32),
        lax.psum(filter_grads[8].astype(jnp.bfloat16), "batch").astype(jnp.float32),
        lax.psum(skip_grads.astype(jnp.bfloat16), "batch").astype(jnp.float32),
    )
    return (
        outputs[None],
        grad_inputs[None],
        shared_sums[0],
        shared_sums[1],
        final_in,
        shared_sums[2],
        shared_sums[3],
        shared_sums[4],
        shared_sums[5],
        shared_sums[6],
        shared_sums[7],
        shared_sums[8],
        shared_sums[9],
        shared_sums[10],
        shared_sums[11],
        final_filter,
        final_rates,
        final_skips,
        final_out,
        shared_sums[12],
        shared_sums[13],
        shared_sums[14],
        final_up,
        shared_sums[15],
        final_down,
        shared_sums[16],
    )


def solution(mesh):
    in_specs = (
        P("batch", "seq", None),
        P(),
        P(),
        P(),
        P(),
        P(),
        P(),
        P(),
        P(),
        P(),
        P(),
        P(),
        P(),
        P(),
        P(),
        P(),
        P(),
        P(),
        P(),
        P(),
        P(),
        P(),
        P(),
        P(),
        P(),
        P("batch", "seq", None),
    )
    out_specs = (
        P("batch", "seq", None),
        P("batch", "seq", None),
        P(),
        P(),
        P("seq", None),
        P(),
        P(),
        P(),
        P(),
        P(),
        P(),
        P(),
        P(),
        P(),
        P(),
        P(None, None, "seq"),
        P(None, "seq"),
        P(None, "seq"),
        P("seq", None),
        P(),
        P(),
        P(),
        P("seq", None),
        P(),
        P("seq", None),
        P(),
    )
    return jax.shard_map(
        per_device, mesh=mesh, in_specs=in_specs, out_specs=out_specs, check_vma=False
    )
```

profile of v0, /device:TPU:0, one launch (start us, length us, event | category | flops | bytes accessed | tf_op | source)
XLA Modules:
  0.0 1072.9 jit_solution(18174130229089279925)
XLA Ops:
  15.0 5.5 collective-permute-start
  33.4 3.1 fusion.170
  38.5 3.4 fusion.131
  46.3 3.4 fusion.135
  57.2 14.6 %all-to-all-start = ((bf16[8,96,128]{2,1,0:T(8,128)(2,1)}), bf16[8,96,128]{2,1,0:T(8,128)(2,1)}, u32[]{:S(2)}, u32[]{:S(2)}) async-start(bf16[8,96,128]{2,1,0:T(8,128)(2,1)} %bitcast.533), calls=%async_computation | async-start | bytes 393216 | tf_op jit(solution)/shard_map/all_to_all | solution.py:244
  76.0 3.7 all-to-all-done
  79.7 4.0 all-to-all-start.1
  89.0 4.4 add_bitcast_fusion.12
  161.2 5.9 all-to-all-start.2
  177.3 8.2 fusion.3
  194.8 4.0 all-to-all-start.3
  199.0 2.9 fusion.473
  202.0 4.6 all-to-all-done.3
  217.2 3.2 subtract_bitcast_fusion.3
  223.6 2.9 fusion.67
  276.4 4.2 add_bitcast_fusion
  288.6 4.0 all-to-all-start.4
  294.2 6.2 all-to-all-done.4
  300.4 4.0 all-to-all-start.5
  308.1 4.1 all-to-all-done.5
  321.4 4.2 collective-permute-done.1
  326.5 4.1 fusion.469
  331.3 6.5 fusion.712
  338.3 6.2 fusion.201
  345.3 4.3 fusion.32
  369.3 12.5 %all-reduce.7 = (bf16[2,64,96]{2,1,0:T(8,128)(2,1)}, bf16[2,96]{1,0:T(2,128)(2,1)}, bf16[2,96]{1,0:T(2,128)(2,1)S(1)}) all-reduce(bf16[2,64,96]{2,1,0:T(8,128)(2,1)} %add_convert_fusion.1, bf16[2,96]{1,0:T(2,128)(2,1)} %add_convert_fusion.2, bf16[2,96]{1,0:T(2,128)(2,1)} %pad_maximum_fusion.11), channel_id=1, replica_groups=mesh['batch'=4,'seq'=8] {'batch'}, use_global_device_ids=true, to_apply=%region_35.36 | all-reduce | flops 12672 | bytes 50688 | tf_op jit(solution)/shard_map/psum | solution.py:409
  401.6 56.6 %reduce-scatter.5.cloned.1.call-done = f32[96,2304]{1,0:T(8,128)} async-done(((f32[768,2304]{1,0:T(8,128)}), f32[96,2304]{1,0:T(8,128)}) %reduce-scatter.5.cloned.1.call-update) | async-done | bytes 884752 | tf_op jit(solution)/shard_map/reduce_scatter | solution.py:399
  460.2 164.6 %reduce-scatter.9.cloned.1.call-done = f32[96,3072]{1,0:T(8,128)} async-done(((f32[768,3072]{1,0:T(8,128)}), f32[96,3072]{1,0:T(8,128)}) %reduce-scatter.9.cloned.1.call-update) | async-done | bytes 1179664 | tf_op jit(solution)/shard_map/reduce_scatter | solution.py:401
  627.0 164.2 %reduce-scatter.11.cloned.1.call-done = f32[384,768]{1,0:T(8,128)} async-done(((f32[3072,768]{1,0:T(8,128)}), f32[384,768]{1,0:T(8,128)}) %reduce-scatter.11.cloned.1.call-update) | async-done | bytes 1179664 | tf_op jit(solution)/shard_map/reduce_scatter | solution.py:402
  795.1 3.8 fusion.153
  801.6 39.1 %all-reduce.14.cloned.1.call-done = (bf16[96,2304]{1,0:T(8,128)(2,1)}, bf16[96,768]{1,0:T(8,128)(2,1)}, bf16[96,3072]{1,0:T(8,128)(2,1)}, bf16[384,768]{1,0:T(8,128)(2,1)}) async-done(((bf16[96,2304]{1,0:T(8,128)(2,1)}, bf16[96,768]{1,0:T(8,128)(2,1)}, bf16[96,3072]{1,0:T(8,128)(2,1)}, bf16[384,768]{1,0:T(8,128)(2,1)}), (bf16[96,2304]{1,0:T(8,128)(2,1)}, bf16[96,768]{1,0:T(8,128)(2,1)}, ...) | async-done | bytes 1769488 | tf_op jit(solution)/shard_map/psum | solution.py:405
  845.7 198.6 %all-reduce.12.cloned.1.call-done = (f32[768]{0:T(1024)}, f32[768]{0:T(1024)}, f32[2304]{0:T(1024)}, f32[3,2304]{1,0:T(4,128)}, f32[2304]{0:T(1024)}, /*index=5*...) async-done(((f32[768]{0:T(1024)}, f32[768]{0:T(1024)}, ...) | async-done | bytes 119056 | tf_op jit(solution)/shard_map/psum | solution.py:375
  (468 shorter events, 295.5 us)
Async XLA Ops:
  11.7 9.4 copy-start.104
  11.7 9.4 copy-start.105
  11.7 10.0 copy-start.106
  11.7 10.5 copy-start.107
  15.0 37.5 %collective-permute-start = (f32[2,2304]{1,0:T(2,128)}, f32[2,2304]{1,0:T(2,128)}, u32[]{:S(2)}, u32[]{:S(2)}) collective-permute-start(f32[2,2304]{1,0:T(2,128)} %slice.104), channel_id=1, source_target_pairs={{0,1},{1,2},{2,3},{3,4},{4,5},{5,6},{6,7},{8,9},{9,10},{10,11},{11... | collective-permute-start | bytes 55304 | tf_op jit(solution)/shard_map/ppermute | solution.py:15
  21.0 15.5 %copy-start.86 = (f32[1,1024]{1,0:T(1,128)}, f32[1,1024]{1,0:T(1,128)S(1)}, u32[]{:S(2)}) copy-start(f32[1,1024]{1,0:T(1,128)S(1)} %iota_multiply_fusion.2) | copy-start | bytes 12292
  21.1 15.5 %copy-start.75 = (f32[1024]{0:T(1024)}, f32[1024]{0:T(1024)S(1)}, u32[]{:S(2)}) copy-start(f32[1024]{0:T(1024)S(1)} %iota_multiply_fusion) | copy-start | bytes 12292
  21.1 15.4 %copy-start.79 = (f32[64]{0:T(128)}, f32[64]{0:T(128)S(1)}, u32[]{:S(2)}) copy-start(f32[64]{0:T(128)S(1)} %convert_element_type.516) | copy-start | bytes 772
  23.9 9.5 copy-start.95
  23.9 9.5 copy-start.98
  57.2 22.4 %all-to-all-start = ((bf16[8,96,128]{2,1,0:T(8,128)(2,1)}), bf16[8,96,128]{2,1,0:T(8,128)(2,1)}, u32[]{:S(2)}, u32[]{:S(2)}) async-start(bf16[8,96,128]{2,1,0:T(8,128)(2,1)} %bitcast.533), calls=%async_computation | async-start | bytes 393216 | tf_op jit(solution)/shard_map/all_to_all | solution.py:244
  79.7 43.8 %all-to-all-start.1 = ((bf16[8,96,128]{2,1,0:T(8,128)(2,1)}), bf16[8,96,128]{2,1,0:T(8,128)(2,1)}, u32[]{:S(2)}, u32[]{:S(2)}) async-start(bf16[8,96,128]{2,1,0:T(8,128)(2,1)} %bitcast.530), calls=%async_computation.1 | async-start | bytes 393216 | tf_op jit(solution)/shard_map/all_to_all | solution.py:245
  161.2 13.8 %all-to-all-start.2 = ((bf16[96,8,128]{2,0,1:T(8,128)(2,1)}), bf16[96,8,128]{2,0,1:T(8,128)(2,1)}, u32[]{:S(2)}, u32[]{:S(2)}) async-start(bf16[96,8,128]{2,0,1:T(8,128)(2,1)} %copy_bitcast_fusion.2), calls=%async_computation.2 | async-start | bytes 393216 | tf_op jit(solution)/shard_map/all_to_all | solution.py:290
  175.1 10.5 slice-start.2
  175.1 12.8 %slice-start = ((s8[4718592]{0:T(1024)(128)(4,1)}), s8[4194304]{0:T(1024)(128)(4,1)S(1)}, s32[]{:S(2)}) async-start(s8[4718592]{0:T(1024)(128)(4,1)} %bitcast.506), calls=%async_computation.16 | async-start | bytes 8388608
  177.0 13.2 %copy-start.1 = (f32[128,768]{1,0:T(8,128)}, f32[128,768]{1,0:T(8,128)S(1)}, u32[]{:S(2)}) copy-start(f32[128,768]{1,0:T(8,128)S(1)} %get-tuple-element.161) | copy-start | bytes 1179652
  177.1 13.2 %copy-start.94 = (f32[128]{0:T(128)}, f32[128]{0:T(128)S(1)}, u32[]{:S(2)}) copy-start(f32[128]{0:T(128)S(1)} %broadcast_multiply_fusion.5) | copy-start | bytes 1540
  177.3 13.0 %copy-start.101 = (f32[128]{0:T(128)}, f32[128]{0:T(128)S(1)}, u32[]{:S(2)}) copy-start(f32[128]{0:T(128)S(1)} %add_rsqrt_fusion) | copy-start | bytes 1540
  177.3 8.2 slice-start.3
  177.3 8.2 copy-start.51
  177.3 10.6 slice-start.1
  194.8 11.8 %all-to-all-start.3 = ((bf16[8,96,128]{2,1,0:T(8,128)(2,1)}), bf16[8,96,128]{2,1,0:T(8,128)(2,1)}, u32[]{:S(2)}, u32[]{:S(2)}) async-start(bf16[8,96,128]{2,1,0:T(8,128)(2,1)} %bitcast.531), calls=%async_computation.3 | async-start | bytes 393216 | tf_op jit(solution)/shard_map/all_to_all | solution.py:319
  198.8 201.2 %reduce-scatter.7.cloned.1.call-start = ((), (), s32[]{:S(2)}) async-start(), calls=%async_computation.11 | async-start | bytes 2654208 | tf_op jit(solution)/shard_map/reduce_scatter | solution.py:400
  288.6 11.8 %all-to-all-start.4 = ((bf16[96,8,128]{2,0,1:T(8,128)(2,1)}), bf16[96,8,128]{2,0,1:T(8,128)(2,1)}, u32[]{:S(2)}, u32[]{:S(2)}) async-start(bf16[96,8,128]{2,0,1:T(8,128)(2,1)} %bitcast.534), calls=%async_computation.4 | async-start | bytes 393216 | tf_op jit(solution)/shard_map/all_to_all | solution.py:338
  300.4 11.8 %all-to-all-start.5 = ((bf16[96,8,128]{2,0,1:T(8,128)(2,1)}), bf16[96,8,128]{2,0,1:T(8,128)(2,1)}, u32[]{:S(2)}, u32[]{:S(2)}) async-start(bf16[96,8,128]{2,0,1:T(8,128)(2,1)} %bitcast.532), calls=%async_computation.5 | async-start | bytes 393216 | tf_op jit(solution)/shard_map/all_to_all | solution.py:339
  304.4 153.8 %reduce-scatter.5.cloned.1.call-start = ((), (), s32[]{:S(2)}) async-start(), calls=%async_computation.10 | async-start | bytes 7962624 | tf_op jit(solution)/shard_map/reduce_scatter | solution.py:399
  320.0 5.7 collective-permute-start.1
  330.6 294.2 %reduce-scatter.9.cloned.1.call-start = ((), (), s32[]{:S(2)}) async-start(), calls=%async_computation.12 | async-start | bytes 10616832 | tf_op jit(solution)/shard_map/reduce_scatter | solution.py:401
  337.9 453.3 %reduce-scatter.11.cloned.1.call-start = ((), (), s32[]{:S(2)}) async-start(), calls=%async_computation.13 | async-start | bytes 10616832 | tf_op jit(solution)/shard_map/reduce_scatter | solution.py:402
  344.6 496.1 %all-reduce.14.cloned.1.call-start = ((), (), s32[]{:S(2)}) async-start(), calls=%async_computation.15 | async-start | bytes 3538944 | tf_op jit(solution)/shard_map/psum | solution.py:405
  357.5 7.6 copy-start.80
  793.3 251.0 %all-reduce.12.cloned.1.call-start = ((), (), s32[]{:S(2)}) async-start(), calls=%async_computation.14 | async-start | bytes 372736 | tf_op jit(solution)/shard_map/psum | solution.py:375
  (94 other events, 298.1 us)
Sparse Core Ops, SparseCore 0:
  203.1 70.2 reduce-scatter.6
  330.8 127.4 reduce-scatter.4
  462.3 162.4 reduce-scatter.8
  628.7 162.4 reduce-scatter.10
  794.9 45.6 all-reduce.13
  849.2 195.0 all-reduce.11
where the time goes:
time: 1080 us; the launch traced here: 1070 us
  waiting for transfers between devices  649 us (60%)
  matrix products  202 us (19%)
  local copies, waits for them, and re-layouts  84.5 us (8%)
  other arithmetic  64.7 us (6%)
  starting transfers between devices  44.2 us (4%)
  between operations  16.3 us (2%)
  blocking collectives  12.5 us (1%)
    psum x1, waiting for transfers between devices, per_device(): lax.psum((grad_pre_gain, grad_pre_bias, grad_in_bias, grad_short, grad_sh...  199 us
    reduce_scatter x1, waiting for transfers between devices, per_device(): lax.psum_scatter(grad_up, 'seq', scatter_dimension=0, tiled=True)  165 us
    reduce_scatter x1, waiting for transfers between devices, per_device(): lax.psum_scatter(grad_down, 'seq', scatter_dimension=0, tiled=True)  164 us
    dot_general x36, matrix products, first_section(): jnp.einsum('cij,ik->ckj', block_groups, lookup_grid, precision=highest_ac...  74.6 us
    dot_general x36, matrix products, second_section(): jnp.einsum('dhq,qn->dnh', block_groups, lookup_grid, precision=highest_ac...  57.2 us
    reduce_scatter x1, waiting for transfers between devices, per_device(): lax.psum_scatter(grad_in, 'seq', scatter_dimension=0, tiled=True)  56.6 us
    psum x1, waiting for transfers between devices, per_device(): lax.psum(weight_shards[0].astype(jnp.bfloat16), 'batch').astype(jnp.float32)  39.1 us
    unnamed x241, local copies, waits for them, and re-layouts  30.5 us
  transfers between devices with their start and end apart: 14, of which 11 were waited for; matrix products, arithmetic and copies ran while one was open for 24% of the time, Pallas kernels for 0%

commit v1 on v0

--- a/solution.py
+++ b/solution.py
@@ -2,7 +2,10 @@
 
 import jax
 import jax.numpy as jnp
+import numpy as np
 from jax import lax
+from jax.experimental import pallas as pl
+from jax.experimental.pallas import tpu as pltpu
 from jax.sharding import PartitionSpec as P
 
 epsilon = 1e-05
@@ -178,7 +181,7 @@
     )
 
 
-def per_device(
+def factored_device(
     inputs,
     pre_gain,
     pre_bias,
@@ -440,6 +443,1690 @@
     )
 
 
+LANES = 128
+BLOCK = 256
+DENSE_LIMIT = 2048
+ROW_AT = {
+    "pre_gain": 0,
+    "pre_bias": 1,
+    "in_bias": 2,
+    "tap_bias": 5,
+    "taps": 8,
+    "skips": 17,
+    "post_gain": 19,
+    "post_bias": 20,
+    "out_bias": 21,
+    "down_bias": 22,
+    "up_bias": 23,
+}
+ROW_COUNT = 32
+
+
+def call_kernel(kernel, outs, args, micros, spaces="", scratch=(), limit=60, name=None):
+    places = {"v": pltpu.VMEM, "s": pltpu.SMEM, "h": pl.ANY}
+    spaces = spaces or "v" * (len(args) + len(outs))
+    specs = [pl.BlockSpec(memory_space=places[space]) for space in spaces]
+    shapes = [jax.ShapeDtypeStruct(shape, dtype) for shape, dtype in outs]
+    return pl.pallas_call(
+        kernel,
+        out_shape=shapes,
+        in_specs=specs[: len(args)],
+        out_specs=specs[len(args) :],
+        scratch_shapes=[
+            pltpu.SemaphoreType.DMA((entry,))
+            if isinstance(entry, int)
+            else pltpu.VMEM(entry[0], entry[1])
+            for entry in scratch
+        ],
+        compiler_params=pltpu.CompilerParams(vmem_limit_bytes=limit * 1024 * 1024),
+        cost_estimate=pl.CostEstimate(
+            flops=1, transcendentals=0, bytes_accessed=int(3.0e6 * micros)
+        ),
+        name=name,
+    )(*args)
+
+
+def row_chunks(source, target, sems, first, count):
+    size = source.shape[0] // count
+    return [
+        pltpu.make_async_copy(
+            source.at[pl.ds(place * size, size)],
+            target.at[pl.ds(place * size, size)],
+            sems.at[first + place],
+        )
+        for place in range(count)
+    ]
+
+
+def dense_rows(tile):
+    tokens, channels = tile.shape
+    rows = tokens * channels // LANES
+    spare = LANES - channels
+    blocks = channels // spare
+    pieces = [tile[rows:, block * spare : (block + 1) * spare] for block in range(blocks)]
+    return jnp.concatenate([tile[:rows], jnp.concatenate(pieces, axis=0)], axis=1)
+
+
+def loose_rows(tile, tokens, channels):
+    rows = tile.shape[0]
+    spare = LANES - channels
+    blocks = channels // spare
+    rest = tokens - rows
+    pieces = [tile[block * rest : (block + 1) * rest, channels:] for block in range(blocks)]
+    return jnp.concatenate([tile[:, :channels], jnp.concatenate(pieces, axis=1)], axis=0)
+
+
+def lays_dense(tokens, channels):
+    spare = LANES - channels
+    if spare <= 0 or channels % spare or tokens * channels % LANES:
+        return False
+    rows, blocks = tokens * channels // LANES, channels // spare
+    return rows % 8 == 0 and (tokens - rows) * blocks == rows and (tokens - rows) % 8 == 0
+
+
+def exact_nn(left_side, right_side):
+    return jnp.dot(
+        left_side, right_side, precision=highest_accuracy, preferred_element_type=jnp.float32
+    )
+
+
+def exact_nt(left_side, right_side):
+    return lax.dot_general(
+        left_side,
+        right_side,
+        (((1,), (1,)), ((), ())),
+        precision=highest_accuracy,
+        preferred_element_type=jnp.float32,
+    )
+
+
+def sine_pair(angle):
+    turns = jnp.round(angle * (2.0 / math.pi))
+    rest = angle - turns * 1.5703125
+    rest = rest - turns * 4.837512969970703125e-4
+    rest = rest - turns * 7.549789948768648e-8
+    square = rest * rest
+    sine = rest + rest * square * (
+        -1.6666654611e-1 + square * (8.3321608736e-3 + square * -1.9515295891e-4)
+    )
+    cosine = (
+        1.0
+        - 0.5 * square
+        + square
+        * square
+        * (4.166664568298827e-2 + square * (-1.388731625493765e-3 + square * 2.443315711809948e-5))
+    )
+    quarter = turns.astype(jnp.int32)
+    odd = (quarter & 1) == 1
+    sine_out = jnp.where(odd, cosine, sine)
+    cosine_out = jnp.where(odd, sine, cosine)
+    sine_out = jnp.where((quarter & 2) == 2, -sine_out, sine_out)
+    cosine_out = jnp.where(((quarter + 1) & 2) == 2, -cosine_out, cosine_out)
+    return sine_out, cosine_out
+
+
+def block_rows(index, size):
+    return pl.ds(pl.multiple_of(index * size, size), size)
+
+
+def wave_pair(index):
+    first = index * 2 * BLOCK
+    return (
+        pl.ds(pl.multiple_of(first, BLOCK), BLOCK),
+        pl.ds(pl.multiple_of(first + BLOCK, BLOCK), BLOCK),
+    )
+
+
+def row_of(rows, name, place=0):
+    at = ROW_AT[name] + place
+    return rows[at : at + 1, :]
+
+
+def feature_block(first, count, length, feat_count):
+    bands = (feat_count - 1) // 2
+    place = lax.broadcasted_iota(jnp.int32, (count, feat_count), 0) + first
+    lane = lax.broadcasted_iota(jnp.int32, (count, feat_count), 1)
+    steps = place.astype(jnp.float32)
+    band = jnp.where(lane > bands, lane - 1 - bands, lane - 1).astype(jnp.float32)
+    frequency = 0.0001 + band * ((bands - 1 - 0.0001) / (bands - 1))
+    sine, cosine = sine_pair(frequency * (steps * (2.0 * math.pi / length)))
+    features = jnp.where(lane > bands, -sine, cosine)
+    features = jnp.where(lane == 0, steps / (length - 1), features)
+    column = lax.broadcasted_iota(jnp.int32, (count, 1), 0) + first
+    return features, column.astype(jnp.float32) / (length - 1)
+
+
+def wave_kernel(channels, start, *refs):
+    (
+        pre_gain,
+        pre_bias,
+        in_bias,
+        tap_bias,
+        taps,
+        skips,
+        post_gain,
+        post_bias,
+        out_bias,
+        down_bias,
+        up_bias,
+        pos_bias,
+        inner_bias,
+        third_bias,
+        sine_freq,
+        filter_weight,
+        decay,
+        in_weight_in,
+        wave_out,
+        back_out,
+        rows_out,
+        in_out,
+        local_out,
+        weights_out,
+        rates_out,
+        vectors_out,
+        tables,
+        wave,
+        back,
+        in_weight,
+        sems,
+    ) = refs
+    length = wave.shape[1]
+    width = in_weight.shape[0]
+    step = tables.shape[1]
+    low, f32 = jnp.bfloat16, jnp.float32
+    load = pltpu.make_async_copy(in_weight_in, in_weight, sems.at[2])
+    load.start()
+
+    def table(which, carry):
+        first = which < 2
+        at = lax.broadcasted_iota(jnp.int32, (step, length), 0)
+        place = lax.broadcasted_iota(jnp.int32, (step, length), 1)
+        fine = jnp.where(first, 2, 1)
+        scale = jnp.where(which % 2 == 0, fine * step, fine)
+        left = at * scale + jnp.where(which == 1, 1, 0)
+        right = place * jnp.where(first, 1, 2) + jnp.where(first, 0, 1)
+        turn = (left * right) & (4 * length - 1)
+        sine, cosine = sine_pair(turn.astype(f32) * (math.pi / (2 * length)))
+        tables[2 * which] = cosine
+        tables[2 * which + 1] = sine
+        return carry
+
+    lax.fori_loop(0, 4, table, 0)
+    per_block = BLOCK // step
+
+    def fill(index, carry):
+        base = (index // per_block) * (2 * BLOCK) + (index % per_block) * step
+        upper = pl.ds(pl.multiple_of(base, step), step)
+        lower = pl.ds(pl.multiple_of(base + BLOCK, step), step)
+        one = pl.ds(index, 1)
+        cos_a, sin_a = tables[0, one, :], tables[1, one, :]
+        cos_b, sin_b = tables[2], tables[3]
+        wave[upper, :] = (cos_a * cos_b - sin_a * sin_b).astype(low)
+        wave[lower, :] = (sin_a * cos_b + cos_a * sin_b).astype(low)
+        scale = 1.0 / length
+        cos_a, sin_a = tables[4, one, :] * scale, tables[5, one, :] * scale
+        cos_b, sin_b = tables[6], tables[7]
+        cosine = (cos_a * cos_b - sin_a * sin_b).astype(low)
+        sine = (sin_a * cos_b + cos_a * sin_b).astype(low)
+        here = block_rows(index, step)
+        for part in range(length // BLOCK):
+            cols = slice(part * BLOCK, (part + 1) * BLOCK)
+            at = part * 2 * BLOCK
+            back[here, at : at + BLOCK] = cosine[:, cols]
+            back[here, at + BLOCK : at + 2 * BLOCK] = sine[:, cols]
+        return carry
+
+    lax.fori_loop(0, length // step, fill, 0)
+    sent = [
+        pltpu.make_async_copy(wave, wave_out, sems.at[0]),
+        pltpu.make_async_copy(back, back_out, sems.at[1]),
+    ]
+    for copy in sent:
+        copy.start()
+
+    rows_out[...] = jnp.zeros_like(rows_out)
+
+    def place_rows(name, vector):
+        for number in range(vector.shape[0] // width):
+            piece = vector[number * width : (number + 1) * width].astype(f32)
+            at = ROW_AT[name] + number
+            rows_out[at : at + 1, :] = piece.reshape(1, width)
+
+    for name, vector in (
+        ("pre_gain", pre_gain),
+        ("pre_bias", pre_bias),
+        ("in_bias", in_bias),
+        ("tap_bias", tap_bias),
+        ("post_gain", post_gain),
+        ("post_bias", post_bias),
+        ("out_bias", out_bias),
+        ("down_bias", down_bias),
+        ("up_bias", up_bias),
+    ):
+        place_rows(name, vector)
+    wide_taps = taps[...].astype(f32)
+    for tap in range(3):
+        for group in range(3):
+            at = ROW_AT["taps"] + 3 * tap + group
+            rows_out[at : at + 1, :] = wide_taps[tap : tap + 1, group * width : (group + 1) * width]
+    at = ROW_AT["skips"]
+    rows_out[at : at + 2, :] = skips[...].astype(f32)
+    for number, vector in enumerate((pos_bias, inner_bias, third_bias, sine_freq)):
+        row = vector[...].astype(f32).reshape(1, vector.shape[0])
+        vectors_out[number : number + 1, :] = row
+
+    source = lax.broadcasted_iota(jnp.int32, (width, LANES), 0)
+    target = lax.broadcasted_iota(jnp.int32, (width, LANES), 1)
+    chosen = (source == start[0] + target) & (target < channels)
+    select_wide = jnp.where(chosen, 1.0, 0.0)
+    select = select_wide.astype(low)
+    local_out[...] = plain_dot(rows_out[...].astype(low), select)
+    padded = jnp.concatenate([decay[...], jnp.zeros((6, width), f32)], axis=0)
+    rates = exact_nn(padded, select_wide)
+    for order in range(2):
+        cols = slice(order * LANES, (order + 1) * LANES)
+        weights_out[:, cols] = plain_dot(filter_weight[order], select)
+        rates_out[:, cols] = rates[order : order + 1]
+    load.wait()
+    for group in range(3):
+        cols = slice(group * LANES, (group + 1) * LANES)
+        whole = in_weight[:, group * width : (group + 1) * width]
+        in_out[:, cols] = plain_dot(whole, select).astype(low)
+    for copy in sent:
+        copy.wait()
+
+
+def filter_kernel(
+    pos_weight,
+    inner_weight,
+    third_weight,
+    vectors,
+    weights,
+    rates,
+    wave_in,
+    spectrum_out,
+    kernel_out,
+    waves_out,
+    high,
+    rest,
+    wave,
+    sems,
+):
+    length = wave.shape[1]
+    low, f32 = jnp.bfloat16, jnp.float32
+    blocks = length // BLOCK
+    loads = row_chunks(wave_in, wave, sems, 0, blocks)
+    for copy in loads:
+        copy.start()
+    feat_count, fhid = pos_weight.shape
+    freq = vectors[3:4, :]
+
+    def network(index, carry):
+        here = block_rows(index, BLOCK)
+        features, times = feature_block(index * BLOCK, BLOCK, length, feat_count)
+        layer_in = features
+        for layer, weight in enumerate((pos_weight, inner_weight, third_weight)):
+            inner = exact_nn(layer_in, weight[...].astype(f32)) + vectors[layer : layer + 1, :]
+            layer_in, cosine = sine_pair(freq * inner)
+            waves_out[layer, here, :] = jnp.concatenate([layer_in, cosine], axis=1)
+        kernels = exact_nn(layer_in, weights[...]) * jnp.exp(-rates[...] * times)
+        kernel_out[here, :] = kernels
+        upper = kernels.astype(low)
+        high[here, :] = upper
+        rest[here, :] = (kernels - upper.astype(f32)).astype(low)
+        return carry
+
+    lax.fori_loop(0, blocks, network, 0)
+    for copy in loads:
+        copy.wait()
+
+    def spectra(index, carry):
+        here = block_rows(index, 2 * BLOCK)
+        matrix = wave[here, :]
+        spectrum_out[here, :] = plain_dot(matrix, high[...]) + plain_dot(matrix, rest[...])
+        return carry
+
+    lax.fori_loop(0, blocks, spectra, 0)
+
+
+def shifted_down(rows, count):
+    place = lax.broadcasted_iota(jnp.int32, rows.shape, 0)
+    return jnp.where(place >= count, pltpu.roll(rows, count, 0), 0.0)
+
+
+def shifted_up(rows, count):
+    length = rows.shape[0]
+    place = lax.broadcasted_iota(jnp.int32, rows.shape, 0)
+    return jnp.where(place < length - count, pltpu.roll(rows, length - count, 0), 0.0)
+
+
+def short_mix(rows, projected, group):
+    taps = [row_of(rows, "taps", 3 * tap + group) for tap in range(3)]
+    return (
+        taps[0] * shifted_down(projected, 2)
+        + taps[1] * shifted_down(projected, 1)
+        + taps[2] * projected
+        + row_of(rows, "tap_bias", group)
+    )
+
+
+def convolve(wave, back, signal, spectrum, cols, kept, products, finish, arrived=None):
+    length = wave.shape[1]
+    low = jnp.bfloat16
+
+    def ahead(index, carry):
+        both = plain_dot(wave[block_rows(index, 2 * BLOCK), :], signal[...])
+        kept[block_rows(index, 2 * BLOCK), :] = both
+        upper, lower = wave_pair(index)
+        real, imag = times_spec(
+            both[:BLOCK], both[BLOCK:], spectrum[upper, cols], spectrum[lower, cols]
+        )
+        products[upper, :LANES] = real.astype(low)
+        products[lower, :LANES] = imag.astype(low)
+        return carry
+
+    lax.fori_loop(0, length // BLOCK, ahead, 0)
+    if arrived is not None:
+        arrived()
+
+    def behind(index, carry):
+        here = block_rows(index, 2 * BLOCK)
+        finish(here, plain_dot(back[here, :], products[:, :LANES]))
+        return carry
+
+    lax.fori_loop(0, length // (2 * BLOCK), behind, 0)
+
+
+def correlate(wave, back, signal, spectrum, cols, kept, products, finish, arriving=None, arrived=None):
+    length = wave.shape[1]
+    low = jnp.bfloat16
+
+    def ahead(index, carry):
+        if arriving is not None:
+            arriving(index)
+        both = plain_dot(wave[block_rows(index, 2 * BLOCK), :], signal[...])
+        upper, lower = wave_pair(index)
+        real, imag = both[:BLOCK], both[BLOCK:]
+        first = times_conj(real, imag, spectrum[upper, cols], spectrum[lower, cols])
+        second = times_conj(real, imag, kept[upper, :], kept[lower, :])
+        products[upper, :LANES] = first[0].astype(low)
+        products[lower, :LANES] = first[1].astype(low)
+        products[upper, LANES:] = second[0].astype(low)
+        products[lower, LANES:] = second[1].astype(low)
+        return carry
+
+    lax.fori_loop(0, length // BLOCK, ahead, 0)
+    if arrived is not None:
+        arrived()
+
+    def behind(index, carry):
+        here = block_rows(index, 2 * BLOCK)
+        both = plain_dot(back[here, :], products[...])
+        return finish(here, both[:, :LANES], both[:, LANES:], carry)
+
+    zero = jnp.zeros((1, LANES), jnp.float32)
+    return lax.fori_loop(0, length // (2 * BLOCK), behind, zero)
+
+
+def front_kernel(parts, index, *refs):
+    chunks = refs[:parts]
+    (norm_rows, weight, rows, wave_in, back_in, spectrum_in) = refs[parts : 6 + parts]
+    (
+        pair_out,
+        projected_out,
+        product_out,
+        gate_out,
+        after_out,
+        gated_out,
+        product_wave_out,
+        gated_wave_out,
+        mixer_out,
+        held,
+        products,
+        wave,
+        back,
+        spectrum,
+        pair,
+        projected,
+        product_wave,
+        gated_wave,
+        mixer,
+        sems,
+    ) = refs[6 + parts :]
+    tok_count, width = chunks[0].shape
+    length = wave.shape[1]
+    channels = width // parts
+    low, f32 = jnp.bfloat16, jnp.float32
+    loads = [
+        pltpu.make_async_copy(source, target, sems.at[place])
+        for place, (source, target) in enumerate(
+            [(wave_in, wave), (spectrum_in, spectrum), (back_in, back)]
+        )
+    ]
+    stores = [
+        pltpu.make_async_copy(source, target, sems.at[3 + place])
+        for place, (source, target) in enumerate(
+            [
+                (pair, pair_out),
+                (projected, projected_out),
+                (product_wave, product_wave_out),
+                (gated_wave, gated_wave_out),
+            ]
+        )
+    ]
+    for copy in loads:
+        copy.start()
+    for part in range(parts):
+        held[block_rows(index[0] ^ part, tok_count), :] = chunks[part][...]
+    gain = row_of(norm_rows, "pre_gain")
+    bias = row_of(norm_rows, "pre_bias")
+    in_bias = jnp.concatenate([row_of(rows, "in_bias", group) for group in range(3)], axis=1)
+
+    def project(step, carry):
+        here = block_rows(step, BLOCK)
+        normed, unit, _ = norm_forward(held[here, :].astype(f32), gain, bias)
+        normed = normed.astype(low)
+        pair[here, :width] = normed
+        pair[here, width:] = unit.astype(low)
+        projected[here, :] = plain_dot(normed, weight[...]) + in_bias
+        return carry
+
+    lax.fori_loop(0, length // BLOCK, project, 0)
+    stores[0].start()
+    stores[1].start()
+    mixed = [
+        short_mix(rows, projected[:, group * LANES : (group + 1) * LANES], group)
+        for group in range(2)
+    ]
+    product_out[...] = (mixed[0] * mixed[1]).astype(low)
+    gate_out[...] = short_mix(rows, projected[:, 2 * LANES :], 2).astype(low)
+
+    def first(here, convolved):
+        product = product_out[here, :].astype(f32)
+        after = (convolved + row_of(rows, "skips", 0) * product).astype(low)
+        after_out[here, :] = after
+        gated_out[here, :] = (after.astype(f32) * gate_out[here, :].astype(f32)).astype(low)
+
+    def second(here, convolved):
+        gated = gated_out[here, :].astype(f32)
+        mixer[here, :] = (convolved + row_of(rows, "skips", 1) * gated).astype(low)
+
+    loads[0].wait()
+    loads[1].wait()
+    cols = [slice(order * LANES, (order + 1) * LANES) for order in range(2)]
+    convolve(
+        wave,
+        back,
+        product_out,
+        spectrum,
+        cols[0],
+        product_wave,
+        products,
+        first,
+        arrived=loads[2].wait,
+    )
+    stores[2].start()
+    convolve(wave, back, gated_out, spectrum, cols[1], gated_wave, products, second)
+    stores[3].start()
+    for part in range(parts):
+        tile = mixer[part * tok_count : (part + 1) * tok_count, :channels]
+        mixer_out[part] = dense_rows(tile.astype(f32)).astype(low)
+    for copy in stores:
+        copy.wait()
+
+
+def back_kernel(
+    channels,
+    grad_mixer,
+    product_ref,
+    gate_ref,
+    after_ref,
+    gated_ref,
+    rows,
+    product_wave_in,
+    gated_wave_in,
+    spectrum_in,
+    wave_in,
+    back_in,
+    projected_in,
+    packed_out,
+    padded_out,
+    grad_kernel_out,
+    sums_out,
+    grad_mix,
+    grad_after,
+    grad_value,
+    grad_gate,
+    products,
+    wave,
+    back,
+    spectrum,
+    product_wave,
+    gated_wave,
+    projected,
+    sems,
+):
+    parts = grad_mixer.shape[0]
+    length = wave.shape[1]
+    tok_count = length // parts
+    low, f32 = jnp.bfloat16, jnp.float32
+    blocks = length // BLOCK
+    loads = [
+        (wave_in, wave, blocks),
+        (spectrum_in, spectrum, blocks),
+        (gated_wave_in, gated_wave, blocks),
+    ]
+    first_loads = []
+    place = 0
+    for source, target, count in loads:
+        first_loads.append(row_chunks(source, target, sems, place, count))
+        place += count
+    for block in range(blocks):
+        for copies in first_loads:
+            copies[block].start()
+    later = [
+        pltpu.make_async_copy(source, target, sems.at[place + number])
+        for number, (source, target) in enumerate(
+            [(back_in, back), (product_wave_in, product_wave), (projected_in, projected)]
+        )
+    ]
+    for copy in later:
+        copy.start()
+    padding = jnp.zeros((tok_count, LANES - channels), f32)
+    for part in range(parts):
+        tile = loose_rows(grad_mixer[part].astype(f32), tok_count, channels)
+        here = slice(part * tok_count, (part + 1) * tok_count)
+        grad_mix[here, :] = jnp.concatenate([tile, padding], axis=1).astype(low)
+
+    def arriving(index):
+        for number, (source, target, count) in enumerate(loads):
+            size = source.shape[0] // count
+            part = pl.ds(pl.multiple_of(index * size, size), size)
+            pltpu.make_async_copy(
+                source.at[part], target.at[part], sems.at[number * blocks + index]
+            ).wait()
+
+    def first(here, data, kernel, total):
+        grad_kernel_out[here, LANES:] = kernel
+        top = grad_mix[here, :].astype(f32)
+        grad_gated = (data + row_of(rows, "skips", 1) * top).astype(low).astype(f32)
+        grad_after[here, :] = (grad_gated * gate_ref[here, :].astype(f32)).astype(low)
+        grad_gate[here, :] = (grad_gated * after_ref[here, :].astype(f32)).astype(low)
+        return total + jnp.sum(top * gated_ref[here, :].astype(f32), axis=0, keepdims=True)
+
+    cols = [slice(order * LANES, (order + 1) * LANES) for order in range(2)]
+    skip_second = correlate(
+        wave,
+        back,
+        grad_mix,
+        spectrum,
+        cols[1],
+        gated_wave,
+        products,
+        first,
+        arriving=arriving,
+        arrived=later[0].wait,
+    )
+
+    def second(here, data, kernel, total):
+        grad_kernel_out[here, :LANES] = kernel
+        top = grad_after[here, :].astype(f32)
+        grad_value[here, :] = (data + row_of(rows, "skips", 0) * top).astype(low)
+        return total + jnp.sum(top * product_ref[here, :].astype(f32), axis=0, keepdims=True)
+
+    later[1].wait()
+    skip_first = correlate(
+        wave, back, grad_after, spectrum, cols[0], product_wave, products, second
+    )
+    sums_out[15:16, :] = skip_first
+    sums_out[16:17, :] = skip_second
+    sums_out[17:24, :] = jnp.zeros((7, LANES), f32)
+    later[2].wait()
+    for group in range(3):
+        here = slice(group * LANES, (group + 1) * LANES)
+        if group == 2:
+            grad_mixed = grad_gate[...].astype(f32)
+        else:
+            other = slice((1 - group) * LANES, (2 - group) * LANES)
+            grad_mixed = grad_value[...].astype(f32) * short_mix(
+                rows, projected[:, other], 1 - group
+            )
+        taps = [row_of(rows, "taps", 3 * tap + group) for tap in range(3)]
+        plain = projected[:, here]
+        for tap in range(3):
+            at = 3 * tap + group
+            moved = plain if tap == 2 else shifted_down(plain, 2 - tap)
+            sums_out[at : at + 1, :] = jnp.sum(grad_mixed * moved, axis=0, keepdims=True)
+        sums_out[9 + group : 10 + group, :] = jnp.sum(grad_mixed, axis=0, keepdims=True)
+        grad_projected = (
+            taps[0] * shifted_up(grad_mixed, 2)
+            + taps[1] * shifted_up(grad_mixed, 1)
+            + taps[2] * grad_mixed
+        ).astype(low)
+        padded_out[:, here] = grad_projected
+        wide = grad_projected.astype(f32)
+        sums_out[12 + group : 13 + group, :] = jnp.sum(wide, axis=0, keepdims=True)
+    dense = packed_out.shape[1] // 3
+
+    def pack(part, carry):
+        tokens = block_rows(part, tok_count)
+        for group in range(3):
+            tile = padded_out[tokens, group * LANES : group * LANES + channels]
+            packed = dense_rows(tile.astype(f32)).astype(low)
+            packed_out[part, group * dense : (group + 1) * dense, :] = packed
+        return carry
+
+    lax.fori_loop(0, parts, pack, 0)
+
+
+def store_rows(target, at, value):
+    per = target.shape[1]
+    place = 0
+    while place < value.shape[0]:
+        quarter, inside = divmod(at + place, per)
+        count = min(value.shape[0] - place, per - inside)
+        target[quarter, inside : inside + count, :] = value[place : place + count]
+        place += count
+
+
+def lane_rows(vector):
+    count = vector.shape[1] // LANES
+    return jnp.concatenate(
+        [vector[:, place * LANES : (place + 1) * LANES] for place in range(count)], axis=0
+    )
+
+
+def middle_kernel(
+    parts,
+    batch_index,
+    received,
+    tokens,
+    top,
+    rows,
+    out_in,
+    up_in,
+    down_in,
+    outputs_out,
+    residual_out,
+    sides_out,
+    send_out,
+    sums_out,
+    *refs,
+):
+    batch = len(refs) - 12
+    got_out = refs[:batch]
+    (
+        out_w,
+        up_w,
+        down_w,
+        residual,
+        total,
+        flow,
+        act,
+        upper_grad,
+        act_parts,
+        branch_parts,
+        up_rows,
+        sems,
+    ) = refs[batch:]
+    tok_count, width = tokens.shape
+    channels = width // parts
+    f32, low = jnp.float32, jnp.bfloat16
+    quarters = up_w.shape[0]
+    quarter = up_w.shape[2]
+    load_out = pltpu.make_async_copy(out_in, out_w, sems.at[0])
+    load_out.start()
+
+    def loads(place):
+        cols = pl.ds(pl.multiple_of(place * quarter, quarter), quarter)
+        return (
+            pltpu.make_async_copy(up_in.at[:, cols], up_w.at[place], sems.at[1 + place]),
+            pltpu.make_async_copy(
+                down_in.at[cols, :], down_w.at[place], sems.at[1 + quarters + place]
+            ),
+        )
+
+    for place in range(quarters):
+        for copy in loads(place):
+            copy.start()
+    tiles = [
+        loose_rows(received[part].astype(f32), tok_count, channels) for part in range(parts)
+    ]
+    mixer = jnp.concatenate(tiles, axis=1).astype(low)
+    sides_out[:, width : 2 * width] = mixer
+    load_out.wait()
+    branch = plain_dot(mixer, out_w[...]) + row_of(rows, "out_bias")
+    residual[...] = tokens[...].astype(f32) + branch
+    gain = row_of(rows, "post_gain")
+    bias = row_of(rows, "post_bias")
+    normed, _, _ = norm_forward(residual[...], gain, bias)
+    sides_out[:, :width] = normed.astype(low)
+    for place in range(quarters):
+        up_rows[place] = row_of(rows, "up_bias", place)
+    total[...] = jnp.zeros_like(total)
+    flow[...] = jnp.zeros_like(flow)
+
+    def body(place, carry):
+        for copy in loads(place):
+            copy.wait()
+        upper = plain_dot(sides_out[:, :width], up_w[place]) + up_rows[place]
+        gauss = 0.5 * (1.0 + lax.erf(upper * 0.7071067811865476))
+        active = (upper * gauss).astype(low)
+        act[place] = active
+        total[...] += plain_dot(active, down_w[place])
+        grad_act = right_dot(top[...], down_w[place])
+        slope = gauss + upper * jnp.exp(-0.5 * upper * upper) * 0.3989422804014327
+        grad_upper = (grad_act * slope).astype(low)
+        upper_grad[place] = grad_upper
+        flow[...] += right_dot(grad_upper, up_w[place])
+        return carry
+
+    lax.fori_loop(0, quarters, body, 0)
+    outputs_out[...] = residual[...] + total[...] + row_of(rows, "down_bias")
+    _, unit, inv_std = norm_forward(residual[...], gain, bias)
+    grad_norm, grad_gain, grad_bias = norm_backward(flow[...], unit, inv_std, gain)
+    grad_residual = top[...].astype(f32) + grad_norm
+    residual_out[...] = grad_residual
+    grad_branch = grad_residual.astype(low)
+    grad_mixer = right_dot(grad_branch, out_w[...])
+    for part in range(parts):
+        tile = grad_mixer[:, part * channels : (part + 1) * channels]
+        send_out[part] = dense_rows(tile).astype(low)
+    wide_branch = grad_branch.astype(f32)
+    vectors = [
+        jnp.sum(wide_branch, axis=0, keepdims=True),
+        grad_gain[None],
+        grad_bias[None],
+        jnp.sum(top[...].astype(f32), axis=0, keepdims=True),
+    ]
+    vectors += [
+        jnp.sum(upper_grad[place].astype(f32), axis=0, keepdims=True) for place in range(quarters)
+    ]
+    per = width // LANES
+    for number, vector in enumerate(vectors):
+        sums_out[number * per : (number + 1) * per, :] = lane_rows(vector)
+    piece = width // batch
+    for place in range(batch):
+        branch_parts[place] = wide_branch[:, place * piece : (place + 1) * piece].astype(low)
+    step = quarters * quarter // (parts * batch)
+    per_part = quarters * quarter // parts
+    for place in range(batch):
+        tiles = []
+        for part in range(parts):
+            at = part * per_part + place * step
+            inside = at % quarter
+            tiles.append(act[at // quarter, :, inside : inside + step].astype(f32))
+        act_parts[place] = jnp.concatenate(tiles, axis=1).astype(low)
+    for bits in range(batch):
+        place = batch_index[0] ^ bits
+        got_out[bits][:, :quarter] = upper_grad[place]
+        got_out[bits][:, quarter : quarter + parts * step] = act_parts[place]
+        got_out[bits][:, quarter + parts * step :] = branch_parts[place]
+
+
+def weight_kernel(batch, *refs):
+    sides, tops, gots = (refs[batch * place : batch * (place + 1)] for place in range(3))
+    up_out, rest_out, flipped, columns = refs[3 * batch :]
+    tok_count, width = tops[0].shape
+    quarter = up_out.shape[1]
+    for bits in range(batch):
+        here = slice(bits * tok_count, (bits + 1) * tok_count)
+        columns[here, :quarter] = gots[bits][:, :quarter]
+        columns[here, quarter : quarter + width] = tops[bits][...]
+        columns[here, quarter + width :] = gots[bits][:, quarter + width :]
+        flipped[:width, here] = sides[bits][:, :width].astype(jnp.float32).T.astype(jnp.bfloat16)
+        flipped[width : 2 * width, here] = (
+            gots[bits][:, quarter : quarter + width].astype(jnp.float32).T.astype(jnp.bfloat16)
+        )
+        flipped[2 * width :, here] = (
+            sides[bits][:, width : 2 * width].astype(jnp.float32).T.astype(jnp.bfloat16)
+        )
+    size = width // 3
+    for third in range(3):
+        rows = slice(third * size, (third + 1) * size)
+        up_out[rows, :] = plain_dot(flipped[rows, :], columns[:, :quarter])
+        middle = slice(width + third * size, width + (third + 1) * size)
+        rest_out[rows, :width] = plain_dot(
+            flipped[middle, :], columns[:, quarter : quarter + width]
+        )
+        last = slice(2 * width + third * size, 2 * width + (third + 1) * size)
+        rest_out[rows, width:] = plain_dot(flipped[last, :], columns[:, quarter + width :])
+
+
+def final_kernel(received, tokens, residual, rows, weight_in, out, weight, joined, sems):
+    parts = received.shape[0]
+    tok_count, width = tokens.shape
+    channels = width // parts
+    f32, low = jnp.float32, jnp.bfloat16
+    load = pltpu.make_async_copy(weight_in, weight, sems.at[0])
+    load.start()
+    dense = received.shape[1] // 3
+    for group in range(3):
+        tiles = [
+            loose_rows(
+                received[part, group * dense : (group + 1) * dense, :].astype(f32),
+                tok_count,
+                channels,
+            )
+            for part in range(parts)
+        ]
+        joined[:, group * width : (group + 1) * width] = jnp.concatenate(tiles, axis=1).astype(low)
+    gain = row_of(rows, "pre_gain")
+    bias = row_of(rows, "pre_bias")
+    _, unit, inv_std = norm_forward(tokens[...].astype(f32), gain, bias)
+    load.wait()
+    grad_normed = jnp.zeros((tok_count, width), f32)
+    for group in range(3):
+        cols = slice(group * width, (group + 1) * width)
+        grad_normed = grad_normed + right_dot(joined[:, cols], weight[:, cols])
+    grad_tokens, _, _ = norm_backward(grad_normed, unit, inv_std, gain)
+    out[...] = residual[...] + grad_tokens
+
+
+SHARED_ROWS = 48
+LAID_ROWS = 8
+OWN_ROWS = 40
+
+
+def chain_kernel(
+    in_local,
+    sums,
+    middle_sums,
+    pos_weight,
+    inner_weight,
+    third_weight,
+    vectors,
+    weights,
+    rates,
+    grad_kernels_in,
+    kernels_in,
+    waves_in,
+    pair_in,
+    small_out,
+    weight_total,
+    rate_total,
+    shared,
+    grad_kernels,
+    kernels,
+    waves,
+    pair_sums,
+    sems,
+):
+    length = kernels.shape[0]
+    blocks = length // BLOCK
+
+    def loads(index):
+        here = block_rows(index, BLOCK)
+        return [
+            pltpu.make_async_copy(
+                grad_kernels_in.at[here], grad_kernels.at[here], sems.at[index]
+            ),
+            pltpu.make_async_copy(kernels_in.at[here], kernels.at[here], sems.at[blocks + index]),
+            pltpu.make_async_copy(
+                waves_in.at[:, here], waves.at[:, here], sems.at[2 * blocks + index]
+            ),
+        ]
+
+    for block in range(blocks):
+        for copy in loads(block):
+            copy.start()
+    width = in_local.shape[0]
+    pair_load = pltpu.make_async_copy(
+        pair_in.at[pl.ds(width, width)], pair_sums, sems.at[3 * blocks]
+    )
+    pair_load.start()
+    feat_count, fhid = pos_weight.shape
+    f32 = jnp.float32
+    freq = vectors[3:4, :]
+    weight_total[...] = jnp.zeros_like(weight_total)
+    rate_total[...] = jnp.zeros_like(rate_total)
+    shared[...] = jnp.zeros_like(shared)
+
+    def body(index, carry):
+        here = block_rows(index, BLOCK)
+        for copy in loads(index):
+            copy.wait()
+        features, times = feature_block(index * BLOCK, BLOCK, length, feat_count)
+        grads = grad_kernels[here, :]
+        decayed = jnp.sum(grads * kernels[here, :] * times, axis=0, keepdims=True)
+        rate_total[...] = rate_total[...] - decayed
+        windowed = grads * jnp.exp(-rates[...] * times)
+        weight_total[...] = weight_total[...] + exact_tdot(waves[2, here, :fhid], windowed)
+        flow = exact_nt(windowed, weights[...])
+        at, bias_at = 0, 2 * fhid + feat_count
+        for layer in (2, 1, 0):
+            slope = flow * waves[layer, here, fhid:]
+            below = waves[layer - 1, here, :fhid] if layer else features
+            count = below.shape[1]
+            shared[at : at + count, :] = shared[at : at + count, :] + exact_tdot(below, slope)
+            at += count
+            row = slice(bias_at + layer, bias_at + layer + 1)
+            shared[row, :] = shared[row, :] + jnp.sum(slope, axis=0, keepdims=True)
+            if layer:
+                weight = inner_weight if layer == 1 else third_weight
+                flow = exact_nt(slope * freq, weight[...].astype(f32))
+        return carry
+
+    lax.fori_loop(0, blocks, body, 0)
+    grad_freq = jnp.zeros_like(freq)
+    at, bias_at = 0, 2 * fhid + feat_count
+    for layer, weight in ((2, third_weight), (1, inner_weight), (0, pos_weight)):
+        count = weight.shape[0]
+        matrix = shared[at : at + count, :]
+        row = slice(bias_at + layer, bias_at + layer + 1)
+        grad_freq = grad_freq + jnp.sum(weight[...].astype(f32) * matrix, axis=0, keepdims=True)
+        grad_freq = grad_freq + vectors[layer : layer + 1, :] * shared[row, :]
+        shared[at : at + count, :] = matrix * freq
+        shared[row, :] = shared[row, :] * freq
+        at += count
+    shared[bias_at + 3 : bias_at + 4, :] = grad_freq
+    pair_load.wait()
+    small_out[...] = jnp.zeros_like(small_out)
+    ones = jnp.ones((8, in_local.shape[1]), f32)
+    in_wide = in_local[...].astype(f32)
+    gain = exact_nt(ones, in_wide * pair_sums[...])[0:1]
+    column_sums = jnp.concatenate([sums[12 + group : 13 + group, :] for group in range(3)], axis=1)
+    bias = exact_nt(jnp.broadcast_to(column_sums, ones.shape), in_wide)[0:1]
+    everywhere = small_out.at[:, :SHARED_ROWS, :]
+    per = width // LANES
+    store_rows(everywhere, 0, lane_rows(gain))
+    store_rows(everywhere, per, lane_rows(bias))
+    at = 2 * per
+    store_rows(everywhere, at, middle_sums[...])
+    at += middle_sums.shape[0]
+    store_rows(everywhere, at, jnp.concatenate([shared[:fhid, :], shared[fhid : 2 * fhid, :]], axis=1))
+    at += fhid
+    tail = shared[2 * fhid : 2 * fhid + feat_count + 4, :]
+    store_rows(everywhere, at, jnp.concatenate([tail, jnp.zeros_like(tail)], axis=1))
+    store_rows(small_out.at[:, SHARED_ROWS : SHARED_ROWS + LAID_ROWS, :], 0, sums[:15, :])
+    own = small_out.at[:, SHARED_ROWS + LAID_ROWS :, :]
+    for order in range(2):
+        cols = slice(order * LANES, (order + 1) * LANES)
+        store_rows(own, order * fhid, weight_total[:, cols])
+        store_rows(own, 2 * fhid + order, rate_total[:, cols])
+    store_rows(own, 2 * fhid + 2, sums[15:17, :])
+
+
+def spread_kernel(in_keep, in_got, small_keep, small_got, send_out, small_out):
+    low, f32 = jnp.bfloat16, jnp.float32
+    parts = send_out.shape[0]
+    small = small_keep[...] + small_got[...]
+    small_out[...] = small
+    both = SHARED_ROWS + LAID_ROWS
+    high, rest = split_low(small[:both])
+    count = in_keep.shape[0] // parts
+    for part in range(parts):
+        here = slice(part * count, (part + 1) * count)
+        send_out[part, :count, :] = (in_keep[here, :] + in_got[here, :].astype(f32)).astype(low)
+        send_out[part, count : count + both, :] = high
+        send_out[part, count + both :, :] = rest
+
+
+def merge_kernel(received, small, out):
+    f32 = jnp.float32
+    parts = received.shape[0]
+    both = SHARED_ROWS + LAID_ROWS
+    count = received.shape[1] - 2 * both
+    total = jnp.zeros((SHARED_ROWS, LANES), f32)
+    done = parts * count
+    rows = SHARED_ROWS + parts * LAID_ROWS + OWN_ROWS
+    for part in range(parts):
+        out[part * count : (part + 1) * count, :] = received[part, :count, :]
+        high = received[part, count : count + both, :].astype(f32)
+        rest = received[part, count + both :, :].astype(f32)
+        total = total + high[:SHARED_ROWS] + rest[:SHARED_ROWS]
+        at = done + SHARED_ROWS + part * LAID_ROWS
+        laid = received[part, count : count + both, :].astype(f32)[SHARED_ROWS:]
+        out[at : at + LAID_ROWS, :] = laid.astype(jnp.bfloat16)
+        laid = received[part, count + both :, :].astype(f32)[SHARED_ROWS:]
+        out[at + rows : at + rows + LAID_ROWS, :] = laid.astype(jnp.bfloat16)
+    for at, value in ((0, total), (rows - OWN_ROWS, small[SHARED_ROWS + LAID_ROWS :, :])):
+        high, rest = split_low(value)
+        count = value.shape[0]
+        out[done + at : done + at + count, :] = high
+        out[done + rows + at : done + rows + at + count, :] = rest
+
+
+def take_rows(source, at, count):
+    per = source.shape[1]
+    pieces = []
+    while count:
+        quarter, inside = divmod(at, per)
+        size = min(count, per - inside)
+        pieces.append(source[quarter, inside : inside + size, :])
+        at += size
+        count -= size
+    return pieces[0] if len(pieces) == 1 else jnp.concatenate(pieces, axis=0)
+
+
+def lane_row(block):
+    return jnp.concatenate([block[place : place + 1] for place in range(block.shape[0])], axis=1)
+
+
+def finish_kernel(batch, channels, batch_index, *refs):
+    entries = refs[:batch]
+    (
+        in_out,
+        pre_gain_out,
+        pre_bias_out,
+        out_bias_out,
+        post_gain_out,
+        post_bias_out,
+        down_bias_out,
+        up_bias_out,
+        third_out,
+        inner_out,
+        pos_out,
+        pos_bias_out,
+        inner_bias_out,
+        third_bias_out,
+        freq_out,
+        taps_out,
+        tap_bias_out,
+        in_bias_out,
+        filter_out,
+        rates_out,
+        skips_out,
+        held,
+        small,
+    ) = refs[batch:]
+    f32 = jnp.float32
+    for bits in range(batch):
+        held[batch_index[0] ^ bits] = entries[bits][...]
+    in_rows = in_out.shape[0] // batch
+    width = pre_gain_out.shape[0]
+    parts = width // channels
+    total = parts * 3 * in_rows
+    rows = small.shape[1]
+    for place in range(batch):
+        small[place] = held[place, total : total + rows, :].astype(f32) + held[
+            place, total + rows :, :
+        ].astype(f32)
+
+    def gather(place, carry):
+        block = held[place, :total, :].astype(f32)
+        tiles = []
+        for group in range(3):
+            for part in range(parts):
+                at = (part * 3 + group) * in_rows
+                tiles.append(block[at : at + in_rows, :channels])
+        in_out[pl.ds(pl.multiple_of(place * in_rows, in_rows), in_rows), :] = jnp.concatenate(
+            tiles, axis=1
+        )
+        return carry
+
+    lax.fori_loop(0, batch, gather, 0)
+    everywhere = small.at[:, :SHARED_ROWS, :]
+    per = width // LANES
+    at = 0
+    for target in (
+        pre_gain_out,
+        pre_bias_out,
+        out_bias_out,
+        post_gain_out,
+        post_bias_out,
+        down_bias_out,
+        up_bias_out,
+    ):
+        count = target.shape[0] // LANES
+        target[...] = lane_row(take_rows(everywhere, at, count)).reshape(target.shape)
+        at += count
+    fhid = third_out.shape[0]
+    pair = take_rows(everywhere, at, fhid)
+    third_out[...] = pair[:, :fhid]
+    inner_out[...] = pair[:, fhid : 2 * fhid]
+    at += fhid
+    tail = take_rows(everywhere, at, pos_out.shape[0] + 4)
+    pos_out[...] = tail[: pos_out.shape[0], :fhid]
+    for place, target in enumerate((pos_bias_out, inner_bias_out, third_bias_out, freq_out)):
+        row = pos_out.shape[0] + place
+        target[...] = tail[row : row + 1, :fhid].reshape(target.shape)
+
+    def laid(number):
+        place, row = divmod(number, LAID_ROWS)
+        return [
+            small[place, SHARED_ROWS + part * LAID_ROWS + row :][:1, :channels]
+            for part in range(parts)
+        ]
+
+    for number in range(5):
+        tiles = [tile for group in range(3) for tile in laid(3 * number + group)]
+        row = jnp.concatenate(tiles, axis=1)
+        if number < 3:
+            taps_out[number : number + 1, :] = row
+        elif number == 3:
+            tap_bias_out[...] = row.reshape(tap_bias_out.shape)
+        else:
+            in_bias_out[...] = row.reshape(in_bias_out.shape)
+    own = small.at[:, SHARED_ROWS + parts * LAID_ROWS :, :]
+    for order in range(2):
+        filter_out[order] = take_rows(own, order * fhid, fhid)[:, :channels]
+    rates_out[...] = take_rows(own, 2 * fhid, 2)[:, :channels]
+    skips_out[...] = take_rows(own, 2 * fhid + 2, 2)[:, :channels]
+
+
+def swapped(value, axis, bits):
+    count = lax.axis_size(axis)
+    return lax.ppermute(value, axis, [(source, source ^ bits) for source in range(count)])
+
+
+def over_batch(value):
+    held = {0: value}
+    bits = lax.axis_size("batch") // 2
+    while bits:
+        held.update({place ^ bits: swapped(member, "batch", bits) for place, member in held.items()})
+        bits //= 2
+    return [held[place] for place in range(len(held))]
+
+
+def natural(entries, index):
+    stacked = jnp.stack(entries)
+    return [
+        lax.dynamic_index_in_dim(stacked, index ^ place, 0, keepdims=False)
+        for place in range(len(entries))
+    ]
+
+
+def halves(total, index, bits, left):
+    shape = total.shape[1:]
+    place = left.index(bits)
+    before = 1 << (len(left) - 1 - place)
+    after = 1 << place
+    view = total.reshape((before, 2, after) + shape)
+    bit = (index // bits) % 2
+    keep = lax.dynamic_index_in_dim(view, bit, 1, keepdims=False)
+    send = lax.dynamic_index_in_dim(view, 1 - bit, 1, keepdims=False)
+    return keep.reshape((before * after,) + shape), send.reshape((before * after,) + shape)
+
+
+def halved(total, axis, index, order):
+    count = lax.axis_size(axis)
+    left = [1 << k for k in range(count.bit_length() - 1)]
+    for bits in order:
+        keep, send = halves(total, index, bits, left)
+        got = swapped(send.astype(jnp.bfloat16), axis, bits)
+        total = keep + got.astype(jnp.float32)
+        left.remove(bits)
+    return total[0]
+
+
+def split_low(value):
+    high = value.astype(jnp.bfloat16)
+    return high, (value - high.astype(jnp.float32)).astype(jnp.bfloat16)
+
+
+def dense_device(
+    inputs,
+    pre_gain,
+    pre_bias,
+    in_weight,
+    input_projection_bias,
+    short_weight,
+    short_bias,
+    pos_weight,
+    pos_bias,
+    inner_weight,
+    inner_bias,
+    filter_third_weight,
+    third_bias,
+    sine_freq,
+    filter_weight,
+    decay_rates,
+    skip_gains,
+    out_weight,
+    out_bias,
+    post_gain,
+    post_bias,
+    up_weight,
+    up_bias,
+    down_weight,
+    down_bias,
+    cotangent,
+):
+    seq_parts = lax.axis_size("seq")
+    batch_parts = lax.axis_size("batch")
+    seq_rank = lax.axis_index("seq")
+    batch_rank = lax.axis_index("batch")
+    tokens = inputs[0]
+    tok_count, width = tokens.shape
+    length = tok_count * seq_parts
+    channels = width // seq_parts
+    hidden_units = up_weight.shape[1]
+    fhid = pos_weight.shape[1]
+    f32, low = jnp.float32, jnp.bfloat16
+    wide = 3 * LANES
+    start = seq_rank * channels
+    bit_list = [1 << k for k in range(seq_parts.bit_length() - 1)]
+    swap_list = [bit_list[1], bit_list[0]] + bit_list[2:]
+    batch_bits = [1 << k for k in range(batch_parts.bit_length() - 1)]
+
+    chunks = {0: tokens}
+    for bits in range(2, seq_parts, 2):
+        chunks[bits] = swapped(tokens, "seq", bits)
+
+    quarters = hidden_units // width
+    seq_scalar = seq_rank.astype(jnp.int32)[None]
+    batch_scalar = batch_rank.astype(jnp.int32)[None]
+    start_scalar = start.astype(jnp.int32)[None]
+    wave, back, rows, in_local, rows_local, weights_local, rates_local, vectors = call_kernel(
+        lambda *refs: wave_kernel(channels, *refs),
+        [
+            ((2 * length, length), low),
+            ((length, 2 * length), low),
+            ((ROW_COUNT, width), f32),
+            ((width, wide), low),
+            ((ROW_COUNT, LANES), f32),
+            ((fhid, 2 * LANES), f32),
+            ((1, 2 * LANES), f32),
+            ((4, fhid), f32),
+        ],
+        [
+            start_scalar,
+            pre_gain,
+            pre_bias,
+            input_projection_bias,
+            short_bias,
+            short_weight,
+            skip_gains,
+            post_gain,
+            post_bias,
+            out_bias,
+            down_bias,
+            up_bias,
+            pos_bias,
+            inner_bias,
+            third_bias,
+            sine_freq,
+            filter_weight,
+            decay_rates,
+            in_weight,
+        ],
+        micros=8.5,
+        spaces="s" + "v" * 17 + "h" + "hh" + "v" * 6,
+        scratch=[
+            ((8, 32, length), f32),
+            ((2 * length, length), low),
+            ((length, 2 * length), low),
+            ((width, 3 * width), low),
+            3,
+        ],
+        name="waves",
+    )
+    even = [chunks[bits] for bits in range(2, seq_parts, 2)]
+    wave, *even = lax.optimization_barrier((wave, *even))
+    for bits in range(0, seq_parts, 2):
+        if bits:
+            chunks[bits] = even[bits // 2 - 1]
+        chunks[bits + 1] = swapped(chunks[bits], "seq", 1)
+    spectrum, kernels, filter_waves = call_kernel(
+        filter_kernel,
+        [
+            ((2 * length, 2 * LANES), f32),
+            ((length, 2 * LANES), f32),
+            ((3, length, 2 * fhid), f32),
+        ],
+        [
+            pos_weight,
+            inner_weight,
+            filter_third_weight,
+            vectors,
+            weights_local,
+            rates_local,
+            wave,
+        ],
+        micros=13,
+        spaces="v" * 6 + "h" + "vvv",
+        scratch=[
+            ((length, 2 * LANES), low),
+            ((length, 2 * LANES), low),
+            ((2 * length, length), low),
+            length // BLOCK,
+        ],
+        name="filters",
+    )
+    grad_top = cotangent[0]
+    tops = over_batch(grad_top)
+    spectrum, *tops = lax.optimization_barrier((spectrum, *tops))
+
+    dense = tok_count * channels // LANES
+    (
+        norm_pair,
+        projected,
+        product,
+        gate,
+        after,
+        gated,
+        product_wave,
+        gated_wave,
+        mixer_chan,
+    ) = call_kernel(
+        lambda *refs: front_kernel(seq_parts, *refs),
+        [
+            ((length, 2 * width), low),
+            ((length, wide), f32),
+            ((length, LANES), low),
+            ((length, LANES), low),
+            ((length, LANES), low),
+            ((length, LANES), low),
+            ((2 * length, LANES), f32),
+            ((2 * length, LANES), f32),
+            ((seq_parts, dense, LANES), low),
+        ],
+        [seq_scalar]
+        + [chunks[part] for part in range(seq_parts)]
+        + [rows, in_local, rows_local, wave, back, spectrum],
+        micros=13,
+        spaces="s" + "v" * seq_parts + "vvvhhh" + "hhvvvvhhv",
+        scratch=[
+            ((length, width), low),
+            ((2 * length, LANES), low),
+            ((2 * length, length), low),
+            ((length, 2 * length), low),
+            ((2 * length, 2 * LANES), f32),
+            ((length, 2 * width), low),
+            ((length, wide), f32),
+            ((2 * length, LANES), f32),
+            ((2 * length, LANES), f32),
+            ((length, LANES), low),
+            7,
+        ],
+        name="front",
+    )
+    mixer_back = lax.all_to_all(mixer_chan, "seq", 0, 0, tiled=True)
+
+    quarter = hidden_units // batch_parts
+    branch_quarter = width // batch_parts
+    rows_quarter = hidden_units // (seq_parts * batch_parts)
+    assert quarter == width and seq_parts * rows_quarter == width
+    got_width = quarter + width + branch_quarter
+    outputs, grad_residual, sides, grad_mixer, middle_sums, *gots = call_kernel(
+        lambda *refs: middle_kernel(seq_parts, *refs),
+        [
+            ((tok_count, width), f32),
+            ((tok_count, width), f32),
+            ((tok_count, 2 * width), low),
+            ((seq_parts, dense, LANES), low),
+            (((4 * width + hidden_units) // LANES, LANES), f32),
+        ]
+        + [((tok_count, got_width), low)] * batch_parts,
+        [
+            batch_scalar,
+            mixer_back,
+            tokens,
+            grad_top,
+            rows,
+            out_weight,
+            up_weight,
+            down_weight,
+        ],
+        micros=11,
+        spaces="svvvvhhh" + "v" * (5 + batch_parts),
+        scratch=[
+            ((width, width), low),
+            ((quarters, width, width), low),
+            ((quarters, width, width), low),
+            ((tok_count, width), f32),
+            ((tok_count, width), f32),
+            ((tok_count, width), f32),
+            ((quarters, tok_count, width), low),
+            ((quarters, tok_count, width), low),
+            ((batch_parts, tok_count, width), low),
+            ((batch_parts, tok_count, branch_quarter), low),
+            ((quarters, 1, width), f32),
+            1 + 2 * quarters,
+        ],
+        name="middle",
+    )
+    grad_mixer_chan = lax.all_to_all(grad_mixer, "seq", 0, 0, tiled=True)
+
+    sides = over_batch(sides)
+    gots = [gots[0]] + [swapped(gots[bits], "batch", bits) for bits in range(1, batch_parts)]
+    up_part, rest_part = call_kernel(
+        lambda *refs: weight_kernel(batch_parts, *refs),
+        [((width, quarter), f32), ((width, width + branch_quarter), f32)],
+        sides + tops + gots,
+        micros=6,
+        scratch=[
+            ((3 * width, batch_parts * tok_count), low),
+            ((batch_parts * tok_count, got_width), low),
+        ],
+        name="weights",
+    )
+    blocks = length // BLOCK
+    packed, grad_proj, grad_kernels, sums = call_kernel(
+        lambda *refs: back_kernel(channels, *refs),
+        [
+            ((seq_parts, 3 * dense, LANES), low),
+            ((length, wide), low),
+            ((length, 2 * LANES), f32),
+            ((24, LANES), f32),
+        ],
+        [
+            grad_mixer_chan,
+            product,
+            gate,
+            after,
+            gated,
+            rows_local,
+            product_wave,
+            gated_wave,
+            spectrum,
+            wave,
+            back,
+            projected,
+        ],
+        micros=15,
+        spaces="v" * 6 + "h" * 6 + "vvvv",
+        scratch=[((length, LANES), low)] * 4
+        + [
+            ((2 * length, 2 * LANES), low),
+            ((2 * length, length), low),
+            ((length, 2 * length), low),
+            ((2 * length, 2 * LANES), f32),
+            ((2 * length, LANES), f32),
+            ((2 * length, LANES), f32),
+            ((length, wide), f32),
+            3 * blocks + 3,
+        ],
+        name="back",
+    )
+    proj_back = lax.all_to_all(packed, "seq", 0, 0, tiled=True)
+    pair_part = left_dot(norm_pair, grad_proj)
+    in_rows = width // (seq_parts * batch_parts)
+    in_count = 3 * in_rows
+    in_part = (
+        pair_part[:width]
+        .reshape(seq_parts, batch_parts, in_rows, 3, LANES)
+        .transpose(1, 0, 3, 2, 4)
+        .reshape(batch_parts, seq_parts * in_count, LANES)
+    )
+    small_rows = SHARED_ROWS + LAID_ROWS + OWN_ROWS
+    pair_part, in_part, up_part, rest_part = lax.optimization_barrier(
+        (pair_part, in_part, up_part, rest_part)
+    )
+    up_quarter = halved(
+        up_part.reshape(seq_parts, -1, quarter), "seq", seq_rank, bit_list
+    ).astype(low)
+    rest_quarter = halved(
+        rest_part.reshape(seq_parts, -1, width + branch_quarter), "seq", seq_rank, swap_list
+    ).astype(low)
+    weights_all = natural(
+        over_batch(jnp.concatenate([up_quarter, rest_quarter], axis=1)), batch_rank
+    )
+    final_up = jnp.concatenate([part[:, :quarter] for part in weights_all], axis=1).astype(f32)
+    final_down = jnp.concatenate(
+        [part[:, quarter : quarter + width] for part in weights_all], axis=0
+    ).astype(f32)
+    final_out = jnp.concatenate(
+        [part[:, quarter + width :] for part in weights_all], axis=1
+    ).astype(f32)
+    (small,) = call_kernel(
+        chain_kernel,
+        [((batch_parts, small_rows, LANES), f32)],
+        [
+            in_local,
+            sums,
+            middle_sums,
+            pos_weight,
+            inner_weight,
+            filter_third_weight,
+            vectors,
+            weights_local,
+            rates_local,
+            grad_kernels,
+            kernels,
+            filter_waves,
+            pair_part,
+        ],
+        micros=12,
+        spaces="v" * 9 + "hhhh" + "v",
+        scratch=[
+            ((fhid, 2 * LANES), f32),
+            ((1, 2 * LANES), f32),
+            ((2 * fhid + 40, fhid), f32),
+            ((length, 2 * LANES), f32),
+            ((length, 2 * LANES), f32),
+            ((3, length, 2 * fhid), f32),
+            ((width, wide), f32),
+            3 * blocks + 1,
+        ],
+        name="chain",
+    )
+    small, proj_back = lax.optimization_barrier((small, proj_back))
+    left = list(batch_bits)
+    for bits in batch_bits[:-1]:
+        in_keep, in_send = halves(in_part, batch_rank, bits, left)
+        small_keep, small_send = halves(small, batch_rank, bits, left)
+        in_part = in_keep + swapped(in_send.astype(low), "batch", bits).astype(f32)
+        small = small_keep + swapped(small_send, "batch", bits)
+        left.remove(bits)
+    in_keep, in_send = halves(in_part, batch_rank, batch_bits[-1], left)
+    small_keep, small_send = halves(small, batch_rank, batch_bits[-1], left)
+    shared_count = in_count + 2 * (SHARED_ROWS + LAID_ROWS)
+    mixed_send, small = call_kernel(
+        spread_kernel,
+        [((seq_parts, shared_count, LANES), low), ((small_rows, LANES), f32)],
+        [
+            in_keep[0],
+            swapped(in_send.astype(low), "batch", batch_bits[-1])[0],
+            small_keep[0],
+            swapped(small_send, "batch", batch_bits[-1])[0],
+        ],
+        micros=2,
+        name="spread",
+    )
+    mixed_send, proj_back = lax.optimization_barrier((mixed_send, proj_back))
+    mixed_got = lax.all_to_all(mixed_send, "seq", 0, 0, tiled=True)
+    (grad_inputs,) = call_kernel(
+        final_kernel,
+        [((tok_count, width), f32)],
+        [proj_back, tokens, grad_residual, rows, in_weight],
+        micros=5.5,
+        spaces="vvvvhv",
+        scratch=[((width, 3 * width), low), ((tok_count, 3 * width), low), 1],
+        name="final",
+    )
+    done_rows = SHARED_ROWS + seq_parts * LAID_ROWS + OWN_ROWS
+    (last,) = call_kernel(
+        merge_kernel,
+        [((seq_parts * in_count + 2 * done_rows, LANES), low)],
+        [mixed_got, small],
+        micros=2,
+        name="merge",
+    )
+    (
+        final_in,
+        grad_pre_gain,
+        grad_pre_bias,
+        grad_out_bias,
+        grad_post_gain,
+        grad_post_bias,
+        grad_down_bias,
+        grad_up_bias,
+        grad_third,
+        grad_inner,
+        grad_pos,
+        grad_pos_bias,
+        grad_inner_bias,
+        grad_third_bias,
+        grad_freq,
+        grad_taps,
+        grad_tap_bias,
+        grad_in_bias,
+        grad_filter,
+        grad_rates,
+        grad_skips,
+    ) = call_kernel(
+        lambda *refs: finish_kernel(batch_parts, channels, *refs),
+        [
+            ((batch_parts * in_rows, 3 * width), f32),
+            ((width,), f32),
+            ((width,), f32),
+            ((width,), f32),
+            ((width,), f32),
+            ((width,), f32),
+            ((width,), f32),
+            ((hidden_units,), f32),
+            (filter_third_weight.shape, f32),
+            (inner_weight.shape, f32),
+            (pos_weight.shape, f32),
+            ((fhid,), f32),
+            ((fhid,), f32),
+            ((fhid,), f32),
+            ((fhid,), f32),
+            ((3, 3 * width), f32),
+            ((3 * width,), f32),
+            ((3 * width,), f32),
+            ((2, fhid, channels), f32),
+            ((2, channels), f32),
+            ((2, channels), f32),
+        ],
+        [batch_scalar] + over_batch(last),
+        micros=3,
+        spaces="s" + "v" * batch_parts + "v" * 21,
+        scratch=[
+            ((batch_parts,) + last.shape, low),
+            ((batch_parts, done_rows, LANES), f32),
+        ],
+        name="finish",
+    )
+    return (
+        outputs[None],
+        grad_inputs[None],
+        grad_pre_gain,
+        grad_pre_bias,
+        final_in,
+        grad_in_bias,
+        grad_taps,
+        grad_tap_bias,
+        grad_pos,
+        grad_pos_bias,
+        grad_inner,
+        grad_inner_bias,
+        grad_third,
+        grad_third_bias,
+        grad_freq,
+        grad_filter,
+        grad_rates,
+        grad_skips,
+        final_out,
+        grad_out_bias,
+        grad_post_gain,
+        grad_post_bias,
+        final_up,
+        grad_up_bias,
+        final_down,
+        grad_down_bias,
+    )
+
+
+def per_device(*args):
+    tokens, parts = args[0].shape[1], lax.axis_size("seq")
+    channels = args[0].shape[2] // parts
+    dense = tokens * parts <= DENSE_LIMIT and lays_dense(tokens, channels)
+    return (dense_device if dense else factored_device)(*args)
+
+
 def solution(mesh):
     in_specs = (
         P("batch", "seq", None),

time: 1080 us -> 217 us (0.20)
  waiting for transfers between devices: 649 us -> 45.7 us
  matrix products: 202 us -> 3.93 us
  Pallas kernels: 0 us -> 91.6 us
  local copies, waits for them, and re-layouts: 84.5 us -> 17.4 us
  other arithmetic: 64.7 us -> 8.62 us
  between operations: 16.3 us -> 1.32 us
  blocking collectives: 12.5 us -> 0 us
    reduce_scatter x4 -> x0, waiting for transfers between devices: 385 us -> none  [the longest x1 165 us: per_device(): lax.psum_scatter(grad_up, 'seq', scatter_dimension=0, tiled=True)]
    psum x2 -> x0, waiting for transfers between devices: 238 us -> none  [the longest x1 199 us: per_device(): lax.psum((grad_pre_gain, grad_pre_bias, grad_in_bias, grad_short, grad_sh...]
    dot_general x94 -> x0, matrix products: 182 us -> none  [the longest x36 74.6 us: first_section(): jnp.einsum('cij,ik->ckj', block_groups, lookup_grid, precision=highest_ac...]
    pallas_call x0 -> x11, Pallas kernels: none -> 91.6 us  [call_kernel(): pl.pallas_call(kernel, out_shape=shapes, in_specs=specs[:len(args)], out_...]
    convert_element_type x33 -> x5, other arithmetic: 36.4 us -> 3.1 us  [the longest x1 1.11 us: dense_device(): jnp.concatenate([part[:, :quarter] for part in weights_all], axis=1)]
    ppermute x2 -> x32, waiting for transfers between devices: 4.25 us -> 32.7 us  [swapped(): lax.ppermute(value, axis, [(source, source ^ bits) for source in range(co...]
    unnamed x241 -> x50, local copies, waits for them, and re-layouts: 30.5 us -> 6.57 us
    ppermute x2 -> x32, starting transfers between devices: 6.76 us -> 29.1 us  [swapped(): lax.ppermute(value, axis, [(source, source ^ bits) for source in range(co...]
  transfers between devices with their start and end apart: 14 -> 36, of which waited for: 11 -> 7; matrix products, arithmetic and copies ran while one was open for 24% -> 9% of each run, Pallas kernels for 0% -> 31%
where the time goes in v1:
time: 217 us; the launch traced here: 216 us
  Pallas kernels  91.6 us (42%)
  starting transfers between devices  47.7 us (22%)
  waiting for transfers between devices  45.7 us (21%)
  local copies, waits for them, and re-layouts  17.4 us (8%)
  other arithmetic  8.62 us (4%)
  matrix products  3.93 us (2%)
    pallas_call x11, Pallas kernels, call_kernel(): pl.pallas_call(kernel, out_shape=shapes, in_specs=specs[:len(args)], out_...  91.6 us
    ppermute x32, waiting for transfers between devices, swapped(): lax.ppermute(value, axis, [(source, source ^ bits) for source in range(co...  32.7 us
    ppermute x32, starting transfers between devices, swapped(): lax.ppermute(value, axis, [(source, source ^ bits) for source in range(co...  29.1 us
    all_to_all x1, waiting for transfers between devices, dense_device(): mixer_back = lax.all_to_all(mixer_chan, 'seq', 0, 0, tiled=True)  7.79 us
    unnamed x50, local copies, waits for them, and re-layouts  6.57 us
    convert_element_type x6, local copies, waits for them, and re-layouts, halved(): got = swapped(send.astype(jnp.bfloat16), axis, bits)  6.25 us
    all_to_all x1, starting transfers between devices, dense_device(): mixed_got = lax.all_to_all(mixed_send, 'seq', 0, 0, tiled=True)  5.86 us
    all_to_all x1, starting transfers between devices, dense_device(): mixer_back = lax.all_to_all(mixer_chan, 'seq', 0, 0, tiled=True)  5.63 us
  transfers between devices with their start and end apart: 36, of which 7 were waited for; matrix products, arithmetic and copies ran while one was open for 9% of the time, Pallas kernels for 31%

profile of v1, /device:TPU:0, one launch (start us, length us, event | category | flops | bytes accessed | tf_op | source)
XLA Modules:
  0.0 216.3 jit_solution(11795439435894678192)
XLA Ops:
  0.7 3.1 %collective-permute-start.1 = (bf16[128,768]{1,0:T(8,128)(2,1)}, bf16[128,768]{1,0:T(8,128)(2,1)S(1)}, u32[]{:S(2)}, u32[]{:S(2)}) collective-permute-start(bf16[128,768]{1,0:T(8,128)(2,1)} %bitcast.84), channel_id=1, source_target_pairs={{0,2},{1,3},{2,0},{3,1},{4,6},{5,7},{6,4},{7,5},{8,10},{9,11},{10,... | collective-permute-start | bytes 589832 | tf_op jit(solution)/shard_map/ppermute | solution.py:1610
  3.8 2.6 %collective-permute-start.2 = (bf16[128,768]{1,0:T(8,128)(2,1)}, bf16[128,768]{1,0:T(8,128)(2,1)S(1)}, u32[]{:S(2)}, u32[]{:S(2)}) collective-permute-start(bf16[128,768]{1,0:T(8,128)(2,1)} %bitcast.85), channel_id=1, source_target_pairs={{0,4},{1,5},{2,6},{3,7},{4,0},{5,1},{6,2},{7,3},{8,12},{9,13},{10,... | collective-permute-start | bytes 589832 | tf_op jit(solution)/shard_map/ppermute | solution.py:1610
  6.4 1.7 collective-permute-start.8
  8.1 8.5 %waves.1 = (bf16[2048,1024]{1,0:T(8,128)(2,1)}, bf16[1024,2048]{1,0:T(8,128)(2,1)}, f32[32,768]{1,0:T(8,128)}, bf16[768,384]{1,0:T(8,128)(2,1)}, f32[32,128]{1,0...) custom-call(s32[1]{0:T(128)} %bitcast.3.refs_0_, bf16[768]{0:T(1024)(128)(2,1)} %refs_1_.1, ...), custom_call_target="tpu_custom_call" | custom-call | flops 1 | bytes 25500000 | tf_op jit(solution)/shard_map/waves/pallas_call | solution.py:470
  18.2 2.9 %collective-permute-done.2.refs_5_ = bf16[128,768]{1,0:T(8,128)(2,1)S(1)} collective-permute-done((bf16[128,768]{1,0:T(8,128)(2,1)}, bf16[128,768]{1,0:T(8,128)(2,1)S(1)}, u32[]{:S(2)}, u32[]{:S(2)}) %collective-permute-start.2) | collective-permute-done | bytes 196640 | tf_op jit(solution)/shard_map/ppermute | solution.py:1610
  21.2 1.6 collective-permute-start.4
  24.8 13.3 %filters.1 = (f32[2048,256]{1,0:T(8,128)}, f32[1024,256]{1,0:T(8,128)}, f32[3,1024,128]{2,1,0:T(8,128)}) custom-call(bf16[33,64]{1,0:T(8,128)(2,1)} %pos_weight.3, bf16[64,64]{1,0:T(8,128)(2,1)} %inner_weight.3, bf16[64,64]{1,0:T(8,128)(2,1)} %third_weight.3, f32[4,64]{1,0:T(4,128)} %get-tuple-element.110.vectors, f32[64,256]{1,0:T(8,128)} %get-tuple-element.111.weights, ...), custom_call_target="tpu_custom_call" | custom-call | flops 1 | bytes 39000000 | tf_op jit(solution)/shard_map/filters/pallas_call | solution.py:470
  39.2 13.4 %front.1 = (bf16[1024,1536]{1,0:T(8,128)(2,1)}, f32[1024,384]{1,0:T(8,128)}, bf16[1024,128]{1,0:T(8,128)(2,1)}, bf16[1024,128]{1,0:T(8,128)(2,1)}, bf16[1024,128...) custom-call(s32[1]{0:T(128)} %bitcast.1.refs_0_, ...), custom_call_target="tpu_custom_call" | custom-call | flops 1 | bytes 39000000 | tf_op jit(solution)/shard_map/front/pallas_call | solution.py:470
  52.6 5.6 %all-to-all-start = ((bf16[8,96,128]{2,1,0:T(8,128)(2,1)}), bf16[8,96,128]{2,1,0:T(8,128)(2,1)S(1)}, u32[]{:S(2)}, u32[]{:S(2)}) async-start(bf16[8,96,128]{2,1,0:T(8,128)(2,1)} %get-tuple-element.115), calls=%async_computation | async-start | bytes 393216 | tf_op jit(solution)/shard_map/all_to_all | solution.py:1835
  58.3 7.8 %all-to-all-done.refs_1_ = bf16[8,96,128]{2,1,0:T(8,128)(2,1)S(1)} async-done(((bf16[8,96,128]{2,1,0:T(8,128)(2,1)}), bf16[8,96,128]{2,1,0:T(8,128)(2,1)S(1)}, u32[]{:S(2)}, u32[]{:S(2)}) %all-to-all-start) | async-done | bytes 196640 | tf_op jit(solution)/shard_map/all_to_all | solution.py:1835
  66.7 11.0 %middle.1 = (f32[128,768]{1,0:T(8,128)}, f32[128,768]{1,0:T(8,128)}, bf16[128,1536]{1,0:T(8,128)(2,1)}, bf16[8,96,128]{2,1,0:T(8,128)(2,1)}, f32[48,128]{1,0:T(8...) custom-call(s32[1]{0:T(128)} %bitcast.refs_0_, ...), custom_call_target="tpu_custom_call" | custom-call | flops 1 | bytes 33000000 | tf_op jit(solution)/shard_map/middle/pallas_call | solution.py:470
  79.3 3.6 %all-to-all-start.1 = ((bf16[8,96,128]{2,1,0:T(8,128)(2,1)}), bf16[8,96,128]{2,1,0:T(8,128)(2,1)S(1)}, u32[]{:S(2)}, u32[]{:S(2)}) async-start(bf16[8,96,128]{2,1,0:T(8,128)(2,1)} %get-tuple-element.118), calls=%async_computation.1 | async-start | bytes 393216 | tf_op jit(solution)/shard_map/all_to_all | solution.py:1880
  85.2 5.3 %all-to-all-done.1.refs_0_ = bf16[8,96,128]{2,1,0:T(8,128)(2,1)S(1)} async-done(((bf16[8,96,128]{2,1,0:T(8,128)(2,1)}), bf16[8,96,128]{2,1,0:T(8,128)(2,1)S(1)}, u32[]{:S(2)}, u32[]{:S(2)}) %all-to-all-start.1) | async-done | bytes 196640 | tf_op jit(solution)/shard_map/all_to_all | solution.py:1880
  91.1 15.3 %back.1 = (bf16[8,288,128]{2,1,0:T(8,128)(2,1)}, bf16[1024,384]{1,0:T(8,128)(2,1)}, f32[1024,256]{1,0:T(8,128)}, f32[24,128]{1,0:T(8,128)}) custom-call(bf16[8,96,128]{2,1,0:T(8,128)(2,1)} %copy-done.8, bf16[1024,128]{1,0:T(8,128)(2,1)} %get-tuple-element.119.refs_1_, bf16[1024,128]{1,0:T(8,128)(2,1)} %get-tuple-element.120.refs_2_, ...), custom_call_target="tpu_custom_call" | custom-call | flops 1 | bytes 45000000 | tf_op jit(solution)/shard_map/back/pallas_call | solution.py:470
  106.4 3.5 %all-to-all-start.2 = ((bf16[8,288,128]{2,1,0:T(8,128)(2,1)}), bf16[8,288,128]{2,1,0:T(8,128)(2,1)S(1)}, u32[]{:S(2)}, u32[]{:S(2)}) async-start(bf16[8,288,128]{2,1,0:T(8,128)(2,1)} %get-tuple-element.145), calls=%async_computation.2 | async-start | bytes 1179648 | tf_op jit(solution)/shard_map/all_to_all | solution.py:1933
  110.1 3.9 %fusion.11.pair_in = f32[1536,384]{1,0:T(8,128)S(1)} fusion(bf16[1024,1536]{1,0:T(8,128)(2,1)} %get-tuple-element.117, bf16[1024,384]{1,0:T(8,128)(2,1)} %get-tuple-element.126), kind=kOutput, calls=%fused_computation.41 | convolution fusion | flops 1207959552 | bytes 6291456 | tf_op jit(solution)/shard_map/dot_general | solution.py:36
  116.2 5.9 %weights.1 = (f32[768,768]{1,0:T(8,128)}, f32[768,960]{1,0:T(8,128)}) custom-call(bf16[128,1536]{1,0:T(8,128)(2,1)} %get-tuple-element.127.refs_0_, bf16[128,1536]{1,0:T(8,128)(2,1)} %collective-permute-done.10.refs_1_, bf16[128,1536]{1,0:T(8,128)(2,1)} %collective-permute-done.11.refs_2_, bf16[128,1536]{1,0:T(8,128)(2,1)} %collective-permute-done.12.refs_3_, ...), custom_call_target="tpu_custom_call" | custom-call | flops 1 | bytes 18000000 | tf_op jit(solution)/shard_map/weights/pallas_call | solution.py:470
  122.8 2.4 %dynamic-slice_convert_fusion = bf16[2,1,2,96,960]{4,3,2,1,0:T(8,128)(2,1)} fusion(f32[2,2,2,96,960]{4,3,2,1,0:T(8,128)} %bitcast.82, s32[]{:T(128)S(6)} %select_n.126), kind=kLoop, calls=%fused_computation.1 | loop fusion | bytes 1474564 | tf_op jit(solution)/shard_map/convert_element_type | solution.py:1647
  125.2 1.9 collective-permute-start.26
  127.0 2.2 %fusion = bf16[4,96,768]{2,1,0:T(8,128)(2,1)} fusion(f32[4,2,1,96,768]{4,3,1,0,2:T(8,128)} %bitcast.91, s32[]{:T(128)S(6)} %select_n.122), kind=kLoop, calls=%fused_computation.7 | loop fusion | bytes 1179652 | tf_op jit(solution)/shard_map/convert_element_type | solution.py:1647
  130.7 12.2 %chain.1 = f32[4,96,128]{2,1,0:T(8,128)} custom-call(bf16[768,384]{1,0:T(8,128)(2,1)} %get-tuple-element.106.refs_10_.in_local, f32[24,128]{1,0:T(8,128)} %get-tuple-element.139.sums, f32[48,128]{1,0:T(8,128)} %get-tuple-element.140.middle_sums, bf16[33,64]{1,0:T(8,128)(2,1)} %pos_weight.3, bf16[64,64]{1,0:T(8,128)(2,1)} %inner_weight.3, ...), custom_call_target="tpu_custom_call" | custom-call | flops 1 | bytes 36000000 | tf_op jit(solution)/shard_map/chain/pallas_call | solution.py:470
  147.0 1.7 bitcast_add_fusion.1
  156.0 1.8 spread.1
  157.8 5.9 %all-to-all-start.3 = ((bf16[8,184,128]{2,1,0:T(8,128)(2,1)}), bf16[8,184,128]{2,1,0:T(8,128)(2,1)S(1)}, u32[]{:S(2)}, u32[]{:S(2)}) async-start(bf16[8,184,128]{2,1,0:T(8,128)(2,1)} %get-tuple-element.151), calls=%async_computation.3 | async-start | bytes 753664 | tf_op jit(solution)/shard_map/all_to_all | solution.py:2019
  164.8 3.0 %collective-permute-start.25 = (bf16[1,96,768]{2,1,0:T(8,128)(2,1)S(1)}, bf16[1,96,768]{2,1,0:T(8,128)(2,1)S(1)}, u32[]{:S(2)}, u32[]{:S(2)}) collective-permute-start(bf16[1,96,768]{2,1,0:T(8,128)(2,1)S(1)} %dynamic-slice_convert_fusion.4), channel_id=1, source_target_pairs={{0,4},{1,5},{2,6},{3,7},{4,0},{5,1},{6,2},{7,3},{8,12},{9,13},{10,... | collective-permute-start | bytes 442376 | tf_op jit(solution)/shard_map/ppermute | solution.py:1610
  168.1 18.8 %collective-permute-done.25 = bf16[1,96,768]{2,1,0:T(8,128)(2,1)S(1)} collective-permute-done((bf16[1,96,768]{2,1,0:T(8,128)(2,1)S(1)}, bf16[1,96,768]{2,1,0:T(8,128)(2,1)S(1)}, u32[]{:S(2)}, u32[]{:S(2)}) %collective-permute-start.25) | collective-permute-done | bytes 147488 | tf_op jit(solution)/shard_map/ppermute | solution.py:1610
  186.9 2.6 %collective-permute-done.28 = bf16[1,96,960]{2,1,0:T(8,128)(2,1)S(1)} collective-permute-done((bf16[1,96,960]{2,1,0:T(8,128)(2,1)S(1)}, bf16[1,96,960]{2,1,0:T(8,128)(2,1)S(1)}, u32[]{:S(2)}, u32[]{:S(2)}) %collective-permute-start.28) | collective-permute-done | bytes 184352 | tf_op jit(solution)/shard_map/ppermute | solution.py:1610
  191.0 1.7 merge.1.refs_1_
  194.2 6.4 %collective-permute-done.30 = bf16[96,1728]{1,0:T(8,128)(2,1)S(1)} collective-permute-done((bf16[96,1728]{1,0:T(8,128)(2,1)S(1)}, bf16[96,1728]{1,0:T(8,128)(2,1)S(1)}, u32[]{:S(2)}, u32[]{:S(2)}) %collective-permute-start.30) | collective-permute-done | bytes 331808 | tf_op jit(solution)/shard_map/ppermute | solution.py:1610
  201.1 1.9 collective-permute-done.21.refs_3_
  203.0 5.5 %final.1 = f32[128,768]{1,0:T(8,128)} custom-call(bf16[8,288,128]{2,1,0:T(8,128)(2,1)} %copy-done.3, bf16[128,768]{1,0:T(8,128)(2,1)} %bitcast.89, f32[128,768]{1,0:T(8,128)} %get-tuple-element.150.residual, f32[32,768]{1,0:T(8,128)} %get-tuple-element.105.refs_9_.refs_4_.rows, bf16[768,2304]{1,0:T(8,128)(2,1)} %weight_in.1), custom_call_target="tpu_custom_call" | custom-call | flops 1 | bytes 16500000 | tf_op jit(solution)/shard_map/final/pallas_call | solution.py:470
  210.0 2.9 %finish.1 = (f32[96,2304]{1,0:T(8,128)}, f32[768]{0:T(1024)}, f32[768]{0:T(1024)}, f32[768]{0:T(1024)}, f32[768]{0:T(1024)}, /*index=5*/f32[768]{0:T(1024)}, f32...) custom-call(s32[1]{0:T(128)} %bitcast.refs_0_, ...), custom_call_target="tpu_custom_call" | custom-call | flops 1 | bytes 9000000 | tf_op jit(solution)/shard_map/finish/pallas_call | solution.py:470
  (137 shorter events, 35.1 us)
Async XLA Ops:
  0.7 15.9 %collective-permute-start.1 = (bf16[128,768]{1,0:T(8,128)(2,1)}, bf16[128,768]{1,0:T(8,128)(2,1)S(1)}, u32[]{:S(2)}, u32[]{:S(2)}) collective-permute-start(bf16[128,768]{1,0:T(8,128)(2,1)} %bitcast.84), channel_id=1, source_target_pairs={{0,2},{1,3},{2,0},{3,1},{4,6},{5,7},{6,4},{7,5},{8,10},{9,11},{10,... | collective-permute-start | bytes 589832 | tf_op jit(solution)/shard_map/ppermute | solution.py:1610
  3.8 17.4 %collective-permute-start.2 = (bf16[128,768]{1,0:T(8,128)(2,1)}, bf16[128,768]{1,0:T(8,128)(2,1)S(1)}, u32[]{:S(2)}, u32[]{:S(2)}) collective-permute-start(bf16[128,768]{1,0:T(8,128)(2,1)} %bitcast.85), channel_id=1, source_target_pairs={{0,4},{1,5},{2,6},{3,7},{4,0},{5,1},{6,2},{7,3},{8,12},{9,13},{10,... | collective-permute-start | bytes 589832 | tf_op jit(solution)/shard_map/ppermute | solution.py:1610
  6.3 14.8 %collective-permute-start.3 = (bf16[128,768]{1,0:T(8,128)(2,1)}, bf16[128,768]{1,0:T(8,128)(2,1)S(1)}, u32[]{:S(2)}, u32[]{:S(2)}) collective-permute-start(bf16[128,768]{1,0:T(8,128)(2,1)} %bitcast.86), channel_id=1, source_target_pairs={{0,6},{1,7},{2,4},{3,5},{4,2},{5,3},{6,0},{7,1},{8,14},{9,15},{10,... | collective-permute-start | bytes 589832 | tf_op jit(solution)/shard_map/ppermute | solution.py:1610
  6.4 14.8 %collective-permute-start.8 = (bf16[128,768]{1,0:T(8,128)(2,1)}, bf16[128,768]{1,0:T(8,128)(2,1)S(1)}, u32[]{:S(2)}, u32[]{:S(2)}) collective-permute-start(bf16[128,768]{1,0:T(8,128)(2,1)} %bitcast.95), channel_id=1, source_target_pairs={{0,16},{8,24},{16,0},{24,8},{1,17},{9,25},{17,1},{25,9},{2,18},{10... | collective-permute-start | bytes 589832 | tf_op jit(solution)/shard_map/ppermute | solution.py:1610
  8.1 15.3 %collective-permute-start.7 = (bf16[128,768]{1,0:T(8,128)(2,1)}, bf16[128,768]{1,0:T(8,128)(2,1)S(1)}, u32[]{:S(2)}, u32[]{:S(2)}) collective-permute-start(bf16[128,768]{1,0:T(8,128)(2,1)} %bitcast.96), channel_id=1, source_target_pairs={{0,8},{8,0},{16,24},{24,16},{1,9},{9,1},{17,25},{25,17},{2,10},{10... | collective-permute-start | bytes 589832 | tf_op jit(solution)/shard_map/ppermute | solution.py:1610
  16.6 21.6 %collective-permute-start = (bf16[128,768]{1,0:T(8,128)(2,1)S(1)}, bf16[128,768]{1,0:T(8,128)(2,1)S(1)}, u32[]{:S(2)}, u32[]{:S(2)}) collective-permute-start(bf16[128,768]{1,0:T(8,128)(2,1)S(1)} %bitcast.90), channel_id=1, source_target_pairs={{0,1},{1,0},{2,3},{3,2},{4,5},{5,4},{6,7},{7,6},{8,9},{9,8},{10,11... | collective-permute-start | bytes 589832 | tf_op jit(solution)/shard_map/ppermute | solution.py:1610
  21.1 17.1 %collective-permute-start.9 = (bf16[128,768]{1,0:T(8,128)(2,1)S(1)}, bf16[128,768]{1,0:T(8,128)(2,1)S(1)}, u32[]{:S(2)}, u32[]{:S(2)}) collective-permute-start(bf16[128,768]{1,0:T(8,128)(2,1)S(1)} %collective-permute-done.8.refs_6_), channel_id=1, source_target_pairs={{0,8},{8,0},{16,24},{24,16},{1,9},{9,1},{17,25},{25,17},{2,10},{10... | collective-permute-start | bytes 589832 | tf_op jit(solution)/shard_map/ppermute | solution.py:1610
  21.2 17.0 %collective-permute-start.4 = (bf16[128,768]{1,0:T(8,128)(2,1)S(1)}, bf16[128,768]{1,0:T(8,128)(2,1)S(1)}, u32[]{:S(2)}, u32[]{:S(2)}) collective-permute-start(bf16[128,768]{1,0:T(8,128)(2,1)S(1)} %collective-permute-done.1.refs_3_), channel_id=1, source_target_pairs={{0,1},{1,0},{2,3},{3,2},{4,5},{5,4},{6,7},{7,6},{8,9},{9,8},{10,11... | collective-permute-start | bytes 589832 | tf_op jit(solution)/shard_map/ppermute | solution.py:1610
  22.8 15.5 %collective-permute-start.5 = (bf16[128,768]{1,0:T(8,128)(2,1)S(1)}, bf16[128,768]{1,0:T(8,128)(2,1)S(1)}, u32[]{:S(2)}, u32[]{:S(2)}) collective-permute-start(bf16[128,768]{1,0:T(8,128)(2,1)S(1)} %collective-permute-done.2.refs_5_), channel_id=1, source_target_pairs={{0,1},{1,0},{2,3},{3,2},{4,5},{5,4},{6,7},{7,6},{8,9},{9,8},{10,11... | collective-permute-start | bytes 589832 | tf_op jit(solution)/shard_map/ppermute | solution.py:1610
  23.3 15.0 %collective-permute-start.6 = (bf16[128,768]{1,0:T(8,128)(2,1)S(1)}, bf16[128,768]{1,0:T(8,128)(2,1)S(1)}, u32[]{:S(2)}, u32[]{:S(2)}) collective-permute-start(bf16[128,768]{1,0:T(8,128)(2,1)S(1)} %collective-permute-done.3.refs_7_), channel_id=1, source_target_pairs={{0,1},{1,0},{2,3},{3,2},{4,5},{5,4},{6,7},{7,6},{8,9},{9,8},{10,11... | collective-permute-start | bytes 589832 | tf_op jit(solution)/shard_map/ppermute | solution.py:1610
  52.6 13.4 %all-to-all-start = ((bf16[8,96,128]{2,1,0:T(8,128)(2,1)}), bf16[8,96,128]{2,1,0:T(8,128)(2,1)S(1)}, u32[]{:S(2)}, u32[]{:S(2)}) async-start(bf16[8,96,128]{2,1,0:T(8,128)(2,1)} %get-tuple-element.115), calls=%async_computation | async-start | bytes 393216 | tf_op jit(solution)/shard_map/all_to_all | solution.py:1835
  77.8 32.2 %collective-permute-start.11 = (bf16[128,1536]{1,0:T(8,128)(2,1)}, bf16[128,1536]{1,0:T(8,128)(2,1)}, u32[]{:S(2)}, u32[]{:S(2)}) collective-permute-start(bf16[128,1536]{1,0:T(8,128)(2,1)} %get-tuple-element.127.refs_0_), channel_id=1, source_target_pairs={{0,16},{8,24},{16,0},{24,8},{1,17},{9,25},{17,1},{25,9},{2,18},{10... | collective-permute-start | bytes 1179656 | tf_op jit(solution)/shard_map/ppermute | solution.py:1610
  79.3 11.1 %all-to-all-start.1 = ((bf16[8,96,128]{2,1,0:T(8,128)(2,1)}), bf16[8,96,128]{2,1,0:T(8,128)(2,1)S(1)}, u32[]{:S(2)}, u32[]{:S(2)}) async-start(bf16[8,96,128]{2,1,0:T(8,128)(2,1)} %get-tuple-element.118), calls=%async_computation.1 | async-start | bytes 393216 | tf_op jit(solution)/shard_map/all_to_all | solution.py:1880
  82.9 33.3 %collective-permute-start.13 = (bf16[128,1728]{1,0:T(8,128)(2,1)}, bf16[128,1728]{1,0:T(8,128)(2,1)}, u32[]{:S(2)}, u32[]{:S(2)}) collective-permute-start(bf16[128,1728]{1,0:T(8,128)(2,1)} %get-tuple-element.133), channel_id=1, source_target_pairs={{0,8},{8,0},{16,24},{24,16},{1,9},{9,1},{17,25},{25,17},{2,10},{10... | collective-permute-start | bytes 1327112 | tf_op jit(solution)/shard_map/ppermute | solution.py:1610
  83.0 33.2 %collective-permute-start.14 = (bf16[128,1728]{1,0:T(8,128)(2,1)}, bf16[128,1728]{1,0:T(8,128)(2,1)}, u32[]{:S(2)}, u32[]{:S(2)}) collective-permute-start(bf16[128,1728]{1,0:T(8,128)(2,1)} %get-tuple-element.134), channel_id=1, source_target_pairs={{0,16},{8,24},{16,0},{24,8},{1,17},{9,25},{17,1},{25,9},{2,18},{10... | collective-permute-start | bytes 1327112 | tf_op jit(solution)/shard_map/ppermute | solution.py:1610
  83.6 32.7 %collective-permute-start.15 = (bf16[128,1728]{1,0:T(8,128)(2,1)}, bf16[128,1728]{1,0:T(8,128)(2,1)}, u32[]{:S(2)}, u32[]{:S(2)}) collective-permute-start(bf16[128,1728]{1,0:T(8,128)(2,1)} %get-tuple-element.135), channel_id=1, source_target_pairs={{0,24},{8,16},{16,8},{24,0},{1,25},{9,17},{17,9},{25,1},{2,26},{10... | collective-permute-start | bytes 1327112 | tf_op jit(solution)/shard_map/ppermute | solution.py:1610
  84.8 31.4 %collective-permute-start.10 = (bf16[128,1536]{1,0:T(8,128)(2,1)}, bf16[128,1536]{1,0:T(8,128)(2,1)}, u32[]{:S(2)}, u32[]{:S(2)}) collective-permute-start(bf16[128,1536]{1,0:T(8,128)(2,1)} %get-tuple-element.127.refs_0_), channel_id=1, source_target_pairs={{0,8},{8,0},{16,24},{24,16},{1,9},{9,1},{17,25},{25,17},{2,10},{10... | collective-permute-start | bytes 1179656 | tf_op jit(solution)/shard_map/ppermute | solution.py:1610
  106.4 40.4 %all-to-all-start.2 = ((bf16[8,288,128]{2,1,0:T(8,128)(2,1)}), bf16[8,288,128]{2,1,0:T(8,128)(2,1)S(1)}, u32[]{:S(2)}, u32[]{:S(2)}) async-start(bf16[8,288,128]{2,1,0:T(8,128)(2,1)} %get-tuple-element.145), calls=%async_computation.2 | async-start | bytes 1179648 | tf_op jit(solution)/shard_map/all_to_all | solution.py:1933
  122.2 22.2 %collective-permute-start.16 = (bf16[2,576,128]{2,1,0:T(8,128)(2,1)S(1)}, bf16[2,576,128]{2,1,0:T(8,128)(2,1)}, u32[]{:S(2)}, u32[]{:S(2)}) collective-permute-start(bf16[2,576,128]{2,1,0:T(8,128)(2,1)S(1)} %fusion.3), channel_id=1, source_target_pairs={{0,8},{8,0},{16,24},{24,16},{1,9},{9,1},{17,25},{25,17},{2,10},{10... | collective-permute-start | bytes 884744 | tf_op jit(solution)/shard_map/ppermute | solution.py:1610
  125.2 27.0 %collective-permute-start.26 = (bf16[4,96,960]{2,1,0:T(8,128)(2,1)}, bf16[4,96,960]{2,1,0:T(8,128)(2,1)}, u32[]{:S(2)}, u32[]{:S(2)}) collective-permute-start(bf16[4,96,960]{2,1,0:T(8,128)(2,1)} %bitcast.28), channel_id=1, source_target_pairs={{0,2},{1,3},{2,0},{3,1},{4,6},{5,7},{6,4},{7,5},{8,10},{9,11},{10,... | collective-permute-start | bytes 2211848 | tf_op jit(solution)/shard_map/ppermute | solution.py:1610
  129.2 17.8 %collective-permute-start.23 = (bf16[4,96,768]{2,1,0:T(8,128)(2,1)}, bf16[4,96,768]{2,1,0:T(8,128)(2,1)}, u32[]{:S(2)}, u32[]{:S(2)}) collective-permute-start(bf16[4,96,768]{2,1,0:T(8,128)(2,1)} %fusion), channel_id=1, source_target_pairs={{0,1},{1,0},{2,3},{3,2},{4,5},{5,4},{6,7},{7,6},{8,9},{9,8},{10,11... | collective-permute-start | bytes 1769480 | tf_op jit(solution)/shard_map/ppermute | solution.py:1610
  146.3 9.1 %collective-permute-start.17 = (bf16[1,576,128]{2,1,0:T(8,128)(2,1)}, bf16[1,576,128]{2,1,0:T(8,128)(2,1)}, u32[]{:S(2)}, u32[]{:S(2)}) collective-permute-start(bf16[1,576,128]{2,1,0:T(8,128)(2,1)} %dynamic-slice_convert_fusion.5), channel_id=1, source_target_pairs={{0,16},{8,24},{16,0},{24,8},{1,17},{9,25},{17,1},{25,9},{2,18},{10... | collective-permute-start | bytes 442376 | tf_op jit(solution)/shard_map/ppermute | solution.py:1610
  149.5 14.2 %collective-permute-start.24 = (bf16[2,96,768]{2,1,0:T(8,128)(2,1)}, bf16[2,96,768]{2,1,0:T(8,128)(2,1)}, u32[]{:S(2)}, u32[]{:S(2)}) collective-permute-start(bf16[2,96,768]{2,1,0:T(8,128)(2,1)} %fusion.2), channel_id=1, source_target_pairs={{0,2},{1,3},{2,0},{3,1},{4,6},{5,7},{6,4},{7,5},{8,10},{9,11},{10,... | collective-permute-start | bytes 884744 | tf_op jit(solution)/shard_map/ppermute | solution.py:1610
  154.5 13.3 %collective-permute-start.27 = (bf16[2,96,960]{2,1,0:T(8,128)(2,1)}, bf16[2,96,960]{2,1,0:T(8,128)(2,1)S(1)}, u32[]{:S(2)}, u32[]{:S(2)}) collective-permute-start(bf16[2,96,960]{2,1,0:T(8,128)(2,1)} %fusion.1), channel_id=1, source_target_pairs={{0,1},{1,0},{2,3},{3,2},{4,5},{5,4},{6,7},{7,6},{8,9},{9,8},{10,11... | collective-permute-start | bytes 1105928 | tf_op jit(solution)/shard_map/ppermute | solution.py:1610
  157.8 32.4 %all-to-all-start.3 = ((bf16[8,184,128]{2,1,0:T(8,128)(2,1)}), bf16[8,184,128]{2,1,0:T(8,128)(2,1)S(1)}, u32[]{:S(2)}, u32[]{:S(2)}) async-start(bf16[8,184,128]{2,1,0:T(8,128)(2,1)} %get-tuple-element.151), calls=%async_computation.3 | async-start | bytes 753664 | tf_op jit(solution)/shard_map/all_to_all | solution.py:2019
  164.8 22.1 %collective-permute-start.25 = (bf16[1,96,768]{2,1,0:T(8,128)(2,1)S(1)}, bf16[1,96,768]{2,1,0:T(8,128)(2,1)S(1)}, u32[]{:S(2)}, u32[]{:S(2)}) collective-permute-start(bf16[1,96,768]{2,1,0:T(8,128)(2,1)S(1)} %dynamic-slice_convert_fusion.4), channel_id=1, source_target_pairs={{0,4},{1,5},{2,6},{3,7},{4,0},{5,1},{6,2},{7,3},{8,12},{9,13},{10,... | collective-permute-start | bytes 442376 | tf_op jit(solution)/shard_map/ppermute | solution.py:1610
  167.9 21.6 %collective-permute-start.28 = (bf16[1,96,960]{2,1,0:T(8,128)(2,1)S(1)}, bf16[1,96,960]{2,1,0:T(8,128)(2,1)S(1)}, u32[]{:S(2)}, u32[]{:S(2)}) collective-permute-start(bf16[1,96,960]{2,1,0:T(8,128)(2,1)S(1)} %dynamic-slice_convert_fusion.3), channel_id=1, source_target_pairs={{0,4},{1,5},{2,6},{3,7},{4,0},{5,1},{6,2},{7,3},{8,12},{9,13},{10,... | collective-permute-start | bytes 552968 | tf_op jit(solution)/shard_map/ppermute | solution.py:1610
  189.6 11.0 %collective-permute-start.30 = (bf16[96,1728]{1,0:T(8,128)(2,1)S(1)}, bf16[96,1728]{1,0:T(8,128)(2,1)S(1)}, u32[]{:S(2)}, u32[]{:S(2)}) collective-permute-start(bf16[96,1728]{1,0:T(8,128)(2,1)S(1)} %get-tuple-element.189), channel_id=1, source_target_pairs={{0,16},{8,24},{16,0},{24,8},{1,17},{9,25},{17,1},{25,9},{2,18},{10... | collective-permute-start | bytes 995336 | tf_op jit(solution)/shard_map/ppermute | solution.py:1610
  192.7 10.3 %collective-permute-start.21 = (bf16[880,128]{1,0:T(8,128)(2,1)}, bf16[880,128]{1,0:T(8,128)(2,1)S(1)}, u32[]{:S(2)}, u32[]{:S(2)}) collective-permute-start(bf16[880,128]{1,0:T(8,128)(2,1)} %merge.1.refs_1_), channel_id=1, source_target_pairs={{0,16},{8,24},{16,0},{24,8},{1,17},{9,25},{17,1},{25,9},{2,18},{10... | collective-permute-start | bytes 675848 | tf_op jit(solution)/shard_map/ppermute | solution.py:1610
  194.2 18.6 %collective-permute-start.29 = (bf16[96,1728]{1,0:T(8,128)(2,1)S(1)}, bf16[96,1728]{1,0:T(8,128)(2,1)S(1)}, u32[]{:S(2)}, u32[]{:S(2)}) collective-permute-start(bf16[96,1728]{1,0:T(8,128)(2,1)S(1)} %get-tuple-element.189), channel_id=1, source_target_pairs={{0,8},{8,0},{16,24},{24,16},{1,9},{9,1},{17,25},{25,17},{2,10},{10... | collective-permute-start | bytes 995336 | tf_op jit(solution)/shard_map/ppermute | solution.py:1610
  200.6 12.2 %collective-permute-start.31 = (bf16[96,1728]{1,0:T(8,128)(2,1)S(1)}, bf16[96,1728]{1,0:T(8,128)(2,1)S(1)}, u32[]{:S(2)}, u32[]{:S(2)}) collective-permute-start(bf16[96,1728]{1,0:T(8,128)(2,1)S(1)} %collective-permute-done.30), channel_id=1, source_target_pairs={{0,8},{8,0},{16,24},{24,16},{1,9},{9,1},{17,25},{25,17},{2,10},{10... | collective-permute-start | bytes 995336 | tf_op jit(solution)/shard_map/ppermute | solution.py:1610
  200.6 8.0 %collective-permute-start.20 = (bf16[880,128]{1,0:T(8,128)(2,1)}, bf16[880,128]{1,0:T(8,128)(2,1)S(1)}, u32[]{:S(2)}, u32[]{:S(2)}) collective-permute-start(bf16[880,128]{1,0:T(8,128)(2,1)} %merge.1.refs_1_), channel_id=1, source_target_pairs={{0,8},{8,0},{16,24},{24,16},{1,9},{9,1},{17,25},{25,17},{2,10},{10... | collective-permute-start | bytes 675848 | tf_op jit(solution)/shard_map/ppermute | solution.py:1610
  (29 other events, 167.3 us)

commit v2 on v1

--- a/solution.py
+++ b/solution.py
@@ -445,6 +445,8 @@
 
 LANES = 128
 BLOCK = 256
+WAVE_BLOCK = 256
+PAD = 8
 DENSE_LIMIT = 2048
 ROW_AT = {
     "pre_gain": 0,
@@ -570,10 +572,10 @@
 
 
 def wave_pair(index):
-    first = index * 2 * BLOCK
+    first = index * 2 * WAVE_BLOCK
     return (
-        pl.ds(pl.multiple_of(first, BLOCK), BLOCK),
-        pl.ds(pl.multiple_of(first + BLOCK, BLOCK), BLOCK),
+        pl.ds(pl.multiple_of(first, WAVE_BLOCK), WAVE_BLOCK),
+        pl.ds(pl.multiple_of(first + WAVE_BLOCK, WAVE_BLOCK), WAVE_BLOCK),
     )
 
 
@@ -584,8 +586,11 @@
 
 def feature_block(first, count, length, feat_count):
     bands = (feat_count - 1) // 2
-    place = lax.broadcasted_iota(jnp.int32, (count, feat_count), 0) + first
-    lane = lax.broadcasted_iota(jnp.int32, (count, feat_count), 1)
+    place = lax.broadcasted_iota(jnp.int32, (count, 2 * feat_count), 0) + first
+    lane = lax.broadcasted_iota(jnp.int32, (count, 2 * feat_count), 1)
+    later = lane >= feat_count
+    place = jnp.where(later, 2 * place + 1, 2 * place)
+    lane = jnp.where(later, lane - feat_count, lane)
     steps = place.astype(jnp.float32)
     band = jnp.where(lane > bands, lane - 1 - bands, lane - 1).astype(jnp.float32)
     frequency = 0.0001 + band * ((bands - 1 - 0.0001) / (bands - 1))
@@ -593,7 +598,23 @@
     features = jnp.where(lane > bands, -sine, cosine)
     features = jnp.where(lane == 0, steps / (length - 1), features)
     column = lax.broadcasted_iota(jnp.int32, (count, 1), 0) + first
-    return features, column.astype(jnp.float32) / (length - 1)
+    times = [(2 * column + odd).astype(jnp.float32) / (length - 1) for odd in (0, 1)]
+    return features, times
+
+
+def norm_kernel(tokens, top, gain, bias, tokens_out, top_out, normed_out, held):
+    low, f32 = jnp.bfloat16, jnp.float32
+    count = tokens.shape[0] // 2
+    for source, target in ((top, top_out), (tokens, tokens_out)):
+        for place in range(held.shape[0]):
+            cols = slice(place * LANES, (place + 1) * LANES)
+            held[place] = source[:, cols].astype(f32)
+            for odd in range(2):
+                rows = held[place, pl.ds(odd, count, stride=2), :]
+                target[odd * count : (odd + 1) * count, cols] = rows.astype(low)
+    rows = [vector[...].astype(f32).reshape(1, vector.shape[0]) for vector in (gain, bias)]
+    normed, _, _ = norm_forward(tokens_out[...].astype(f32), *rows)
+    normed_out[...] = normed.astype(low)
 
 
 def wave_kernel(channels, start, *refs):
@@ -617,7 +638,7 @@
         decay,
         in_weight_in,
         wave_out,
-        back_out,
+        turn_out,
         rows_out,
         in_out,
         local_out,
@@ -626,64 +647,56 @@
         vectors_out,
         tables,
         wave,
-        back,
         in_weight,
         sems,
     ) = refs
-    length = wave.shape[1]
+    half = wave.shape[1]
     width = in_weight.shape[0]
     step = tables.shape[1]
     low, f32 = jnp.bfloat16, jnp.float32
-    load = pltpu.make_async_copy(in_weight_in, in_weight, sems.at[2])
+    load = pltpu.make_async_copy(in_weight_in, in_weight, sems.at[1])
     load.start()
 
+    unit = math.pi / (4 * half)
+
     def table(which, carry):
-        first = which < 2
-        at = lax.broadcasted_iota(jnp.int32, (step, length), 0)
-        place = lax.broadcasted_iota(jnp.int32, (step, length), 1)
-        fine = jnp.where(first, 2, 1)
-        scale = jnp.where(which % 2 == 0, fine * step, fine)
-        left = at * scale + jnp.where(which == 1, 1, 0)
-        right = place * jnp.where(first, 1, 2) + jnp.where(first, 0, 1)
-        turn = (left * right) & (4 * length - 1)
-        sine, cosine = sine_pair(turn.astype(f32) * (math.pi / (2 * length)))
+        at = lax.broadcasted_iota(jnp.int32, (step, half), 0)
+        place = lax.broadcasted_iota(jnp.int32, (step, half), 1)
+        left = jnp.where(which == 0, 2 * step * at, 2 * at + 1)
+        turn = (left * (2 * place + 1)) & (8 * half - 1)
+        sine, cosine = sine_pair(turn.astype(f32) * unit)
         tables[2 * which] = cosine
         tables[2 * which + 1] = sine
         return carry
 
-    lax.fori_loop(0, 4, table, 0)
-    per_block = BLOCK // step
+    lax.fori_loop(0, 2, table, 0)
+    per_block = WAVE_BLOCK // step
 
     def fill(index, carry):
-        base = (index // per_block) * (2 * BLOCK) + (index % per_block) * step
+        base = (index // per_block) * (2 * WAVE_BLOCK) + (index % per_block) * step
         upper = pl.ds(pl.multiple_of(base, step), step)
-        lower = pl.ds(pl.multiple_of(base + BLOCK, step), step)
+        lower = pl.ds(pl.multiple_of(base + WAVE_BLOCK, step), step)
         one = pl.ds(index, 1)
         cos_a, sin_a = tables[0, one, :], tables[1, one, :]
         cos_b, sin_b = tables[2], tables[3]
         wave[upper, :] = (cos_a * cos_b - sin_a * sin_b).astype(low)
         wave[lower, :] = (sin_a * cos_b + cos_a * sin_b).astype(low)
-        scale = 1.0 / length
-        cos_a, sin_a = tables[4, one, :] * scale, tables[5, one, :] * scale
-        cos_b, sin_b = tables[6], tables[7]
-        cosine = (cos_a * cos_b - sin_a * sin_b).astype(low)
-        sine = (sin_a * cos_b + cos_a * sin_b).astype(low)
-        here = block_rows(index, step)
-        for part in range(length // BLOCK):
-            cols = slice(part * BLOCK, (part + 1) * BLOCK)
-            at = part * 2 * BLOCK
-            back[here, at : at + BLOCK] = cosine[:, cols]
-            back[here, at + BLOCK : at + 2 * BLOCK] = sine[:, cols]
         return carry
 
-    lax.fori_loop(0, length // step, fill, 0)
-    sent = [
-        pltpu.make_async_copy(wave, wave_out, sems.at[0]),
-        pltpu.make_async_copy(back, back_out, sems.at[1]),
-    ]
+    lax.fori_loop(0, half // step, fill, 0)
+    sent = [pltpu.make_async_copy(wave, wave_out, sems.at[0])]
     for copy in sent:
         copy.start()
 
+    def turn(index, carry):
+        upper, lower = wave_pair(index)
+        at = lax.broadcasted_iota(jnp.int32, (WAVE_BLOCK, LANES), 0) + index * WAVE_BLOCK
+        sine, cosine = sine_pair((2 * at + 1).astype(f32) * unit)
+        turn_out[upper, :] = cosine
+        turn_out[lower, :] = sine
+        return carry
+
+    lax.fori_loop(0, half // WAVE_BLOCK, turn, 0)
     rows_out[...] = jnp.zeros_like(rows_out)
 
     def place_rows(name, vector):
@@ -736,6 +749,17 @@
         copy.wait()
 
 
+def doubled(weight):
+    zero = jnp.zeros_like(weight)
+    return jnp.concatenate(
+        [jnp.concatenate([weight, zero], axis=1), jnp.concatenate([zero, weight], axis=1)], axis=0
+    )
+
+
+def twice(row):
+    return jnp.concatenate([row, row], axis=1)
+
+
 def filter_kernel(
     pos_weight,
     inner_weight,
@@ -743,6 +767,7 @@
     vectors,
     weights,
     rates,
+    turn,
     wave_in,
     spectrum_out,
     kernel_out,
@@ -752,127 +777,168 @@
     wave,
     sems,
 ):
-    length = wave.shape[1]
+    half = wave.shape[1]
+    length = 2 * half
     low, f32 = jnp.bfloat16, jnp.float32
-    blocks = length // BLOCK
-    loads = row_chunks(wave_in, wave, sems, 0, blocks)
+    loads = row_chunks(wave_in, wave, sems, 0, 1)
     for copy in loads:
         copy.start()
-    feat_count, fhid = pos_weight.shape
-    freq = vectors[3:4, :]
+    feat_count = pos_weight.shape[0]
+    freq = twice(vectors[3:4, :])
 
     def network(index, carry):
         here = block_rows(index, BLOCK)
-        features, times = feature_block(index * BLOCK, BLOCK, length, feat_count)
-        layer_in = features
+        there = pl.ds(pl.multiple_of(index * BLOCK + half, BLOCK), BLOCK)
+        layer_in, times = feature_block(index * BLOCK, BLOCK, length, feat_count)
         for layer, weight in enumerate((pos_weight, inner_weight, third_weight)):
-            inner = exact_nn(layer_in, weight[...].astype(f32)) + vectors[layer : layer + 1, :]
+            matrix = doubled(weight[...].astype(f32))
+            inner = exact_nn(layer_in, matrix) + twice(vectors[layer : layer + 1, :])
             layer_in, cosine = sine_pair(freq * inner)
             waves_out[layer, here, :] = jnp.concatenate([layer_in, cosine], axis=1)
-        kernels = exact_nn(layer_in, weights[...]) * jnp.exp(-rates[...] * times)
-        kernel_out[here, :] = kernels
-        upper = kernels.astype(low)
-        high[here, :] = upper
-        rest[here, :] = (kernels - upper.astype(f32)).astype(low)
+        both = exact_nn(layer_in, doubled(weights[...]))
+        cols = 2 * LANES
+        for part, rows in enumerate((here, there)):
+            kernels = both[:, part * cols : (part + 1) * cols]
+            kernels = kernels * jnp.exp(-rates[...] * times[part])
+            kernel_out[rows, :] = kernels
+            upper = kernels.astype(low)
+            high[rows, :] = upper
+            rest[rows, :] = (kernels - upper.astype(f32)).astype(low)
         return carry
 
-    lax.fori_loop(0, blocks, network, 0)
+    lax.fori_loop(0, half // BLOCK, network, 0)
     for copy in loads:
         copy.wait()
 
     def spectra(index, carry):
-        here = block_rows(index, 2 * BLOCK)
-        matrix = wave[here, :]
-        spectrum_out[here, :] = plain_dot(matrix, high[...]) + plain_dot(matrix, rest[...])
+        matrix = wave[block_rows(index, 2 * WAVE_BLOCK), :]
+        even, odd = (
+            plain_dot(matrix, high[rows, :]) + plain_dot(matrix, rest[rows, :])
+            for rows in (slice(0, half), slice(half, length))
+        )
+        upper, lower = wave_pair(index)
+        for order in range(2):
+            cols = slice(order * LANES, (order + 1) * LANES)
+            parts = butterfly(even[:, cols], odd[:, cols], turn, upper, lower)
+            for side, (real, imag) in enumerate(parts):
+                spectrum_out[side, upper, cols] = real * (1.0 / length)
+                spectrum_out[side, lower, cols] = imag * (1.0 / length)
         return carry
 
-    lax.fori_loop(0, blocks, spectra, 0)
-
-
-def shifted_down(rows, count):
-    place = lax.broadcasted_iota(jnp.int32, rows.shape, 0)
-    return jnp.where(place >= count, pltpu.roll(rows, count, 0), 0.0)
-
-
-def shifted_up(rows, count):
-    length = rows.shape[0]
-    place = lax.broadcasted_iota(jnp.int32, rows.shape, 0)
-    return jnp.where(place < length - count, pltpu.roll(rows, length - count, 0), 0.0)
+    lax.fori_loop(0, half // WAVE_BLOCK, spectra, 0)
+
+
+def butterfly(even, odd, turn, upper, lower):
+    cosine, sine = turn[upper, :], turn[lower, :]
+    even_real, even_imag = even[:WAVE_BLOCK], even[WAVE_BLOCK:]
+    odd_real, odd_imag = odd[:WAVE_BLOCK], odd[WAVE_BLOCK:]
+    real = even_real * cosine + even_imag * sine
+    imag = even_imag * cosine - even_real * sine
+    return (real + odd_real, imag + odd_imag), (real - odd_real, odd_imag - imag)
+
+
+def unbutterfly(first, second, turn, upper, lower):
+    cosine, sine = turn[upper, :], turn[lower, :]
+    real, imag = first[0] + second[0], first[1] - second[1]
+    even = (real * cosine - imag * sine, imag * cosine + real * sine)
+    return even, (first[0] - second[0], first[1] + second[1])
 
 
 def short_mix(rows, projected, group):
+    cols = slice(group * LANES, (group + 1) * LANES)
+    length = projected.shape[1] - PAD
+    now, last = slice(PAD, PAD + length), slice(PAD - 1, PAD - 1 + length)
     taps = [row_of(rows, "taps", 3 * tap + group) for tap in range(3)]
-    return (
-        taps[0] * shifted_down(projected, 2)
-        + taps[1] * shifted_down(projected, 1)
-        + taps[2] * projected
-        + row_of(rows, "tap_bias", group)
-    )
-
-
-def convolve(wave, back, signal, spectrum, cols, kept, products, finish, arrived=None):
-    length = wave.shape[1]
-    low = jnp.bfloat16
+    shift = row_of(rows, "tap_bias", group)
+    odd_last = projected[1, last, cols]
+    even_now = projected[0, now, cols]
+    even = taps[0] * projected[0, last, cols] + taps[1] * odd_last + taps[2] * even_now + shift
+    odd = taps[0] * odd_last + taps[1] * even_now + taps[2] * projected[1, now, cols] + shift
+    return even, odd
+
+
+def spread_rows(tile, held, target):
+    count = tile.shape[0] // 2
+    for place in range(held.shape[0]):
+        cols = slice(place * LANES, (place + 1) * LANES)
+        for odd in range(2):
+            rows = tile[odd * count : (odd + 1) * count, cols]
+            held[place, pl.ds(odd, count, stride=2), :] = rows
+        target[:, cols] = held[place]
+
+
+def inverse_block(wave, reals, imags, index):
+    upper, lower = wave_pair(index)
+    return plain_dot(wave[upper, :], reals[...]) + plain_dot(wave[lower, :], imags[...])
+
+
+def store_inverse(reals, imags, here, at, parts):
+    for place, (real, imag) in enumerate(parts):
+        cols = slice((at + place) * LANES, (at + place + 1) * LANES)
+        reals[here, cols] = real.astype(jnp.bfloat16)
+        imags[here, cols] = imag.astype(jnp.bfloat16)
+
+
+def convolve(wave, turn, signal, spectrum, cols, kept, reals, imags, finish):
+    half = wave.shape[1]
 
     def ahead(index, carry):
-        both = plain_dot(wave[block_rows(index, 2 * BLOCK), :], signal[...])
-        kept[block_rows(index, 2 * BLOCK), :] = both
+        both = plain_dot(wave[block_rows(index, 2 * WAVE_BLOCK), :], signal[...])
         upper, lower = wave_pair(index)
-        real, imag = times_spec(
-            both[:BLOCK], both[BLOCK:], spectrum[upper, cols], spectrum[lower, cols]
-        )
-        products[upper, :LANES] = real.astype(low)
-        products[lower, :LANES] = imag.astype(low)
+        sides = butterfly(both[:, :LANES], both[:, LANES:], turn, upper, lower)
+        outs = []
+        for side, (real, imag) in enumerate(sides):
+            kept[side, upper, :], kept[side, lower, :] = real, imag
+            outs.append(
+                times_spec(real, imag, spectrum[side, upper, cols], spectrum[side, lower, cols])
+            )
+        parts = unbutterfly(*outs, turn, upper, lower)
+        store_inverse(reals, imags, block_rows(index, WAVE_BLOCK), 0, parts)
         return carry
 
-    lax.fori_loop(0, length // BLOCK, ahead, 0)
-    if arrived is not None:
-        arrived()
+    lax.fori_loop(0, half // WAVE_BLOCK, ahead, 0)
 
     def behind(index, carry):
-        here = block_rows(index, 2 * BLOCK)
-        finish(here, plain_dot(back[here, :], products[:, :LANES]))
+        finish(block_rows(index, WAVE_BLOCK), inverse_block(wave, reals, imags, index))
         return carry
 
-    lax.fori_loop(0, length // (2 * BLOCK), behind, 0)
-
-
-def correlate(wave, back, signal, spectrum, cols, kept, products, finish, arriving=None, arrived=None):
-    length = wave.shape[1]
-    low = jnp.bfloat16
+    lax.fori_loop(0, half // WAVE_BLOCK, behind, 0)
+
+
+def correlate(wave, turn, signal, spectrum, cols, kept, reals, imags, finish):
+    half = wave.shape[1]
+    wide = 2 * LANES
 
     def ahead(index, carry):
-        if arriving is not None:
-            arriving(index)
-        both = plain_dot(wave[block_rows(index, 2 * BLOCK), :], signal[...])
+        both = plain_dot(wave[block_rows(index, 2 * WAVE_BLOCK), :], signal[...])
         upper, lower = wave_pair(index)
-        real, imag = both[:BLOCK], both[BLOCK:]
-        first = times_conj(real, imag, spectrum[upper, cols], spectrum[lower, cols])
-        second = times_conj(real, imag, kept[upper, :], kept[lower, :])
-        products[upper, :LANES] = first[0].astype(low)
-        products[lower, :LANES] = first[1].astype(low)
-        products[upper, LANES:] = second[0].astype(low)
-        products[lower, LANES:] = second[1].astype(low)
+        sides = butterfly(both[:, :LANES], both[:, LANES:], turn, upper, lower)
+        here = block_rows(index, WAVE_BLOCK)
+        for number, (other, columns) in enumerate(((spectrum, cols), (kept, slice(0, LANES)))):
+            outs = [
+                times_conj(*pair, other[side, upper, columns], other[side, lower, columns])
+                for side, pair in enumerate(sides)
+            ]
+            parts = unbutterfly(*outs, turn, upper, lower)
+            store_inverse(reals, imags, here, 2 * number, parts)
         return carry
 
-    lax.fori_loop(0, length // BLOCK, ahead, 0)
-    if arrived is not None:
-        arrived()
+    lax.fori_loop(0, half // WAVE_BLOCK, ahead, 0)
 
     def behind(index, carry):
-        here = block_rows(index, 2 * BLOCK)
-        both = plain_dot(back[here, :], products[...])
-        return finish(here, both[:, :LANES], both[:, LANES:], carry)
-
-    zero = jnp.zeros((1, LANES), jnp.float32)
-    return lax.fori_loop(0, length // (2 * BLOCK), behind, zero)
+        both = inverse_block(wave, reals, imags, index)
+        kernel = both[:, wide:] * (0.5 / half)
+        return finish(block_rows(index, WAVE_BLOCK), both[:, :wide], kernel, carry)
+
+    zero = jnp.zeros((1, wide), jnp.float32)
+    return lax.fori_loop(0, half // WAVE_BLOCK, behind, zero)
 
 
 def front_kernel(parts, index, *refs):
     chunks = refs[:parts]
-    (norm_rows, weight, rows, wave_in, back_in, spectrum_in) = refs[parts : 6 + parts]
+    (weight, rows, wave_in, turn_in, spectrum_in) = refs[parts : 5 + parts]
     (
-        pair_out,
+        normed_out,
         projected_out,
         product_out,
         gate_out,
@@ -882,32 +948,32 @@
         gated_wave_out,
         mixer_out,
         held,
-        products,
+        reals,
+        imags,
         wave,
-        back,
+        turn,
         spectrum,
-        pair,
         projected,
         product_wave,
         gated_wave,
         mixer,
         sems,
-    ) = refs[6 + parts :]
+    ) = refs[5 + parts :]
     tok_count, width = chunks[0].shape
-    length = wave.shape[1]
+    half = wave.shape[1]
     channels = width // parts
     low, f32 = jnp.bfloat16, jnp.float32
     loads = [
         pltpu.make_async_copy(source, target, sems.at[place])
         for place, (source, target) in enumerate(
-            [(wave_in, wave), (spectrum_in, spectrum), (back_in, back)]
+            [(wave_in, wave), (turn_in, turn), (spectrum_in, spectrum)]
         )
     ]
     stores = [
         pltpu.make_async_copy(source, target, sems.at[3 + place])
         for place, (source, target) in enumerate(
             [
-                (pair, pair_out),
+                (held, normed_out),
                 (projected, projected_out),
                 (product_wave, product_wave_out),
                 (gated_wave, gated_wave_out),
@@ -916,61 +982,50 @@
     ]
     for copy in loads:
         copy.start()
+    count = tok_count // 2
     for part in range(parts):
-        held[block_rows(index[0] ^ part, tok_count), :] = chunks[part][...]
-    gain = row_of(norm_rows, "pre_gain")
-    bias = row_of(norm_rows, "pre_bias")
+        place = index[0] ^ part
+        for odd in range(2):
+            at = pl.ds(pl.multiple_of(odd * half + place * count, count), count)
+            held[at, :] = chunks[part][odd * count : (odd + 1) * count, :]
+    stores[0].start()
     in_bias = jnp.concatenate([row_of(rows, "in_bias", group) for group in range(3)], axis=1)
-
-    def project(step, carry):
-        here = block_rows(step, BLOCK)
-        normed, unit, _ = norm_forward(held[here, :].astype(f32), gain, bias)
-        normed = normed.astype(low)
-        pair[here, :width] = normed
-        pair[here, width:] = unit.astype(low)
-        projected[here, :] = plain_dot(normed, weight[...]) + in_bias
+    projected[:, :PAD, :] = jnp.zeros((2, PAD, projected.shape[2]), f32)
+
+    def project(odd, carry):
+        projected[odd, PAD:, :] = plain_dot(held[block_rows(odd, half), :], weight[...]) + in_bias
         return carry
 
-    lax.fori_loop(0, length // BLOCK, project, 0)
-    stores[0].start()
+    lax.fori_loop(0, 2, project, 0)
     stores[1].start()
-    mixed = [
-        short_mix(rows, projected[:, group * LANES : (group + 1) * LANES], group)
-        for group in range(2)
-    ]
-    product_out[...] = (mixed[0] * mixed[1]).astype(low)
-    gate_out[...] = short_mix(rows, projected[:, 2 * LANES :], 2).astype(low)
+    mixed = [short_mix(rows, projected, group) for group in range(3)]
+    for odd in range(2):
+        cols = slice(odd * LANES, (odd + 1) * LANES)
+        product_out[:, cols] = (mixed[0][odd] * mixed[1][odd]).astype(low)
+        gate_out[:, cols] = mixed[2][odd].astype(low)
+    skips = [twice(row_of(rows, "skips", order)) for order in range(2)]
 
     def first(here, convolved):
         product = product_out[here, :].astype(f32)
-        after = (convolved + row_of(rows, "skips", 0) * product).astype(low)
+        after = (convolved + skips[0] * product).astype(low)
         after_out[here, :] = after
         gated_out[here, :] = (after.astype(f32) * gate_out[here, :].astype(f32)).astype(low)
 
     def second(here, convolved):
         gated = gated_out[here, :].astype(f32)
-        mixer[here, :] = (convolved + row_of(rows, "skips", 1) * gated).astype(low)
-
-    loads[0].wait()
-    loads[1].wait()
+        mixer[here, :] = (convolved + skips[1] * gated).astype(low)
+
+    for copy in loads:
+        copy.wait()
     cols = [slice(order * LANES, (order + 1) * LANES) for order in range(2)]
-    convolve(
-        wave,
-        back,
-        product_out,
-        spectrum,
-        cols[0],
-        product_wave,
-        products,
-        first,
-        arrived=loads[2].wait,
-    )
+    convolve(wave, turn, product_out, spectrum, cols[0], product_wave, reals, imags, first)
     stores[2].start()
-    convolve(wave, back, gated_out, spectrum, cols[1], gated_wave, products, second)
+    convolve(wave, turn, gated_out, spectrum, cols[1], gated_wave, reals, imags, second)
     stores[3].start()
     for part in range(parts):
-        tile = mixer[part * tok_count : (part + 1) * tok_count, :channels]
-        mixer_out[part] = dense_rows(tile.astype(f32)).astype(low)
+        at = slice(part * count, (part + 1) * count)
+        tiles = [mixer[at, odd * LANES : odd * LANES + channels].astype(f32) for odd in range(2)]
+        mixer_out[part] = dense_rows(jnp.concatenate(tiles, axis=0)).astype(low)
     for copy in stores:
         copy.wait()
 
@@ -983,11 +1038,11 @@
     after_ref,
     gated_ref,
     rows,
+    turn,
     product_wave_in,
     gated_wave_in,
     spectrum_in,
     wave_in,
-    back_in,
     projected_in,
     packed_out,
     padded_out,
@@ -997,122 +1052,123 @@
     grad_after,
     grad_value,
     grad_gate,
-    products,
+    reals,
+    imags,
     wave,
-    back,
     spectrum,
     product_wave,
     gated_wave,
     projected,
+    shifted,
     sems,
 ):
     parts = grad_mixer.shape[0]
-    length = wave.shape[1]
-    tok_count = length // parts
+    half = wave.shape[1]
+    count = half // parts
     low, f32 = jnp.bfloat16, jnp.float32
-    blocks = length // BLOCK
     loads = [
-        (wave_in, wave, blocks),
-        (spectrum_in, spectrum, blocks),
-        (gated_wave_in, gated_wave, blocks),
-    ]
-    first_loads = []
-    place = 0
-    for source, target, count in loads:
-        first_loads.append(row_chunks(source, target, sems, place, count))
-        place += count
-    for block in range(blocks):
-        for copies in first_loads:
-            copies[block].start()
-    later = [
-        pltpu.make_async_copy(source, target, sems.at[place + number])
-        for number, (source, target) in enumerate(
-            [(back_in, back), (product_wave_in, product_wave), (projected_in, projected)]
+        pltpu.make_async_copy(source, target, sems.at[place])
+        for place, (source, target) in enumerate(
+            [
+                (wave_in, wave),
+                (spectrum_in, spectrum),
+                (gated_wave_in, gated_wave),
+                (product_wave_in, product_wave),
+                (projected_in, projected),
+            ]
         )
     ]
-    for copy in later:
+    for copy in loads:
         copy.start()
-    padding = jnp.zeros((tok_count, LANES - channels), f32)
+    padding = jnp.zeros((count, LANES - channels), f32)
     for part in range(parts):
-        tile = loose_rows(grad_mixer[part].astype(f32), tok_count, channels)
-        here = slice(part * tok_count, (part + 1) * tok_count)
-        grad_mix[here, :] = jnp.concatenate([tile, padding], axis=1).astype(low)
-
-    def arriving(index):
-        for number, (source, target, count) in enumerate(loads):
-            size = source.shape[0] // count
-            part = pl.ds(pl.multiple_of(index * size, size), size)
-            pltpu.make_async_copy(
-                source.at[part], target.at[part], sems.at[number * blocks + index]
-            ).wait()
+        tile = loose_rows(grad_mixer[part].astype(f32), 2 * count, channels)
+        here = slice(part * count, (part + 1) * count)
+        pieces = [tile[:count], padding, tile[count:], padding]
+        grad_mix[here, :] = jnp.concatenate(pieces, axis=1).astype(low)
+    skips = [twice(row_of(rows, "skips", order)) for order in range(2)]
+
+    def store_kernel(here, order, kernel):
+        cols = slice(order * LANES, (order + 1) * LANES)
+        grad_kernel_out[0, here, cols] = kernel[:, :LANES]
+        grad_kernel_out[1, here, cols] = kernel[:, LANES:]
 
     def first(here, data, kernel, total):
-        grad_kernel_out[here, LANES:] = kernel
+        store_kernel(here, 1, kernel)
         top = grad_mix[here, :].astype(f32)
-        grad_gated = (data + row_of(rows, "skips", 1) * top).astype(low).astype(f32)
+        grad_gated = (data + skips[1] * top).astype(low).astype(f32)
         grad_after[here, :] = (grad_gated * gate_ref[here, :].astype(f32)).astype(low)
         grad_gate[here, :] = (grad_gated * after_ref[here, :].astype(f32)).astype(low)
         return total + jnp.sum(top * gated_ref[here, :].astype(f32), axis=0, keepdims=True)
 
+    def second(here, data, kernel, total):
+        store_kernel(here, 0, kernel)
+        top = grad_after[here, :].astype(f32)
+        grad_value[here, :] = (data + skips[0] * top).astype(low)
+        return total + jnp.sum(top * product_ref[here, :].astype(f32), axis=0, keepdims=True)
+
     cols = [slice(order * LANES, (order + 1) * LANES) for order in range(2)]
+    for copy in loads[:3]:
+        copy.wait()
     skip_second = correlate(
-        wave,
-        back,
-        grad_mix,
-        spectrum,
-        cols[1],
-        gated_wave,
-        products,
-        first,
-        arriving=arriving,
-        arrived=later[0].wait,
-    )
-
-    def second(here, data, kernel, total):
-        grad_kernel_out[here, :LANES] = kernel
-        top = grad_after[here, :].astype(f32)
-        grad_value[here, :] = (data + row_of(rows, "skips", 0) * top).astype(low)
-        return total + jnp.sum(top * product_ref[here, :].astype(f32), axis=0, keepdims=True)
-
-    later[1].wait()
+        wave, turn, grad_mix, spectrum, cols[1], gated_wave, reals, imags, first
+    )
+    loads[3].wait()
     skip_first = correlate(
-        wave, back, grad_after, spectrum, cols[0], product_wave, products, second
-    )
-    sums_out[15:16, :] = skip_first
-    sums_out[16:17, :] = skip_second
+        wave, turn, grad_after, spectrum, cols[0], product_wave, reals, imags, second
+    )
+    sums_out[15:16, :] = skip_first[:, :LANES] + skip_first[:, LANES:]
+    sums_out[16:17, :] = skip_second[:, :LANES] + skip_second[:, LANES:]
     sums_out[17:24, :] = jnp.zeros((7, LANES), f32)
-    later[2].wait()
+    loads[4].wait()
+    now, last, after = slice(PAD, PAD + half), slice(PAD - 1, PAD - 1 + half), slice(1, 1 + half)
+
+    def total(value):
+        return jnp.sum(value, axis=0, keepdims=True)
+
+    shifted[:, half:, :] = jnp.zeros((2, PAD, LANES), f32)
     for group in range(3):
         here = slice(group * LANES, (group + 1) * LANES)
+        sides = [slice(odd * LANES, (odd + 1) * LANES) for odd in range(2)]
         if group == 2:
-            grad_mixed = grad_gate[...].astype(f32)
+            mixed = [grad_gate[:, side].astype(f32) for side in sides]
         else:
-            other = slice((1 - group) * LANES, (2 - group) * LANES)
-            grad_mixed = grad_value[...].astype(f32) * short_mix(
-                rows, projected[:, other], 1 - group
-            )
+            others = short_mix(rows, projected, 1 - group)
+            mixed = [grad_value[:, side].astype(f32) * other for side, other in zip(sides, others)]
+        shifted[0, :half, :], shifted[1, :half, :] = mixed
+        even, odd = mixed
         taps = [row_of(rows, "taps", 3 * tap + group) for tap in range(3)]
-        plain = projected[:, here]
+        odd_last, even_now = projected[1, last, here], projected[0, now, here]
+        moved = (
+            total(even * projected[0, last, here] + odd * odd_last),
+            total(even * odd_last + odd * even_now),
+            total(even * even_now + odd * projected[1, now, here]),
+        )
         for tap in range(3):
             at = 3 * tap + group
-            moved = plain if tap == 2 else shifted_down(plain, 2 - tap)
-            sums_out[at : at + 1, :] = jnp.sum(grad_mixed * moved, axis=0, keepdims=True)
-        sums_out[9 + group : 10 + group, :] = jnp.sum(grad_mixed, axis=0, keepdims=True)
-        grad_projected = (
-            taps[0] * shifted_up(grad_mixed, 2)
-            + taps[1] * shifted_up(grad_mixed, 1)
-            + taps[2] * grad_mixed
-        ).astype(low)
-        padded_out[:, here] = grad_projected
-        wide = grad_projected.astype(f32)
-        sums_out[12 + group : 13 + group, :] = jnp.sum(wide, axis=0, keepdims=True)
+            sums_out[at : at + 1, :] = moved[tap]
+        sums_out[9 + group : 10 + group, :] = total(even + odd)
+        even_next, odd_next = shifted[0, after, :], shifted[1, after, :]
+        grads = (
+            taps[0] * even_next + taps[1] * odd + taps[2] * even,
+            taps[0] * odd_next + taps[1] * even_next + taps[2] * odd,
+        )
+        grads = [grad.astype(low) for grad in grads]
+        for place, grad in enumerate(grads):
+            padded_out[place * half : (place + 1) * half, here] = grad
+        sums_out[12 + group : 13 + group, :] = total(grads[0].astype(f32) + grads[1].astype(f32))
     dense = packed_out.shape[1] // 3
 
     def pack(part, carry):
-        tokens = block_rows(part, tok_count)
         for group in range(3):
-            tile = padded_out[tokens, group * LANES : group * LANES + channels]
-            packed = dense_rows(tile.astype(f32)).astype(low)
+            cols = slice(group * LANES, group * LANES + channels)
+            tiles = [
+                padded_out[
+                    pl.ds(pl.multiple_of(odd * half + part * count, count), count), cols
+                ].astype(f32)
+                for odd in range(2)
+            ]
+            packed = dense_rows(jnp.concatenate(tiles, axis=0)).astype(low)
             packed_out[part, group * dense : (group + 1) * dense, :] = packed
         return carry
 
@@ -1148,13 +1204,12 @@
     down_in,
     outputs_out,
     residual_out,
-    sides_out,
     send_out,
     sums_out,
     *refs,
 ):
-    batch = len(refs) - 12
-    got_out = refs[:batch]
+    batch = len(refs) - 14
+    sides, parts_out = refs[0], refs[1 : 1 + batch]
     (
         out_w,
         up_w,
@@ -1167,8 +1222,9 @@
         act_parts,
         branch_parts,
         up_rows,
+        held,
         sems,
-    ) = refs[batch:]
+    ) = refs[1 + batch :]
     tok_count, width = tokens.shape
     channels = width // parts
     f32, low = jnp.float32, jnp.bfloat16
@@ -1193,14 +1249,14 @@
         loose_rows(received[part].astype(f32), tok_count, channels) for part in range(parts)
     ]
     mixer = jnp.concatenate(tiles, axis=1).astype(low)
-    sides_out[:, width : 2 * width] = mixer
     load_out.wait()
     branch = plain_dot(mixer, out_w[...]) + row_of(rows, "out_bias")
     residual[...] = tokens[...].astype(f32) + branch
     gain = row_of(rows, "post_gain")
     bias = row_of(rows, "post_bias")
     normed, _, _ = norm_forward(residual[...], gain, bias)
-    sides_out[:, :width] = normed.astype(low)
+    sides[:, :width] = normed.astype(low)
+    sides[:, width:] = mixer
     for place in range(quarters):
         up_rows[place] = row_of(rows, "up_bias", place)
     total[...] = jnp.zeros_like(total)
@@ -1209,7 +1265,7 @@
     def body(place, carry):
         for copy in loads(place):
             copy.wait()
-        upper = plain_dot(sides_out[:, :width], up_w[place]) + up_rows[place]
+        upper = plain_dot(sides[:, :width], up_w[place]) + up_rows[place]
         gauss = 0.5 * (1.0 + lax.erf(upper * 0.7071067811865476))
         active = (upper * gauss).astype(low)
         act[place] = active
@@ -1222,7 +1278,7 @@
         return carry
 
     lax.fori_loop(0, quarters, body, 0)
-    outputs_out[...] = residual[...] + total[...] + row_of(rows, "down_bias")
+    spread_rows(residual[...] + total[...] + row_of(rows, "down_bias"), held, outputs_out)
     _, unit, inv_std = norm_forward(residual[...], gain, bias)
     grad_norm, grad_gain, grad_bias = norm_backward(flow[...], unit, inv_std, gain)
     grad_residual = top[...].astype(f32) + grad_norm
@@ -1247,7 +1303,10 @@
         sums_out[number * per : (number + 1) * per, :] = lane_rows(vector)
     piece = width // batch
     for place in range(batch):
-        branch_parts[place] = wide_branch[:, place * piece : (place + 1) * piece].astype(low)
+        part = wide_branch[:, place * piece : (place + 1) * piece]
+        spare = branch_parts.shape[2] - piece
+        part = jnp.concatenate([part, jnp.zeros((tok_count, spare), f32)], axis=1)
+        branch_parts[place] = part.astype(low)
     step = quarters * quarter // (parts * batch)
     per_part = quarters * quarter // parts
     for place in range(batch):
@@ -1259,41 +1318,74 @@
         act_parts[place] = jnp.concatenate(tiles, axis=1).astype(low)
     for bits in range(batch):
         place = batch_index[0] ^ bits
-        got_out[bits][:, :quarter] = upper_grad[place]
-        got_out[bits][:, quarter : quarter + parts * step] = act_parts[place]
-        got_out[bits][:, quarter + parts * step :] = branch_parts[place]
-
-
-def weight_kernel(batch, *refs):
+        parts_out[bits][:, :quarter] = upper_grad[place]
+        parts_out[bits][:, quarter : 2 * quarter] = act_parts[place]
+        parts_out[bits][:, 2 * quarter :] = branch_parts[place]
+
+
+def store_halves(part, bit, bits, keep_out, send_out):
+    count = keep_out.shape[0]
+    size = keep_out.shape[1]
+    for entry in range(count):
+        lower, upper = entry % bits, entry // bits
+        base = upper * 2 * bits + lower
+        mine = pl.ds(pl.multiple_of((base + bit * bits) * size, size), size)
+        other = pl.ds(pl.multiple_of((base + (1 - bit) * bits) * size, size), size)
+        keep_out[entry] = part[mine, :]
+        send_out[entry] = part[other, :].astype(jnp.bfloat16)
+
+
+def flip(tile):
+    return tile.astype(jnp.float32).T.astype(jnp.bfloat16)
+
+
+def weight_kernel(batch, orders, index, *refs):
     sides, tops, gots = (refs[batch * place : batch * (place + 1)] for place in range(3))
-    up_out, rest_out, flipped, columns = refs[3 * batch :]
+    up_keep, up_send, rest_keep, rest_send, flipped, columns, part, rest = refs[3 * batch :]
     tok_count, width = tops[0].shape
-    quarter = up_out.shape[1]
-    for bits in range(batch):
-        here = slice(bits * tok_count, (bits + 1) * tok_count)
-        columns[here, :quarter] = gots[bits][:, :quarter]
-        columns[here, quarter : quarter + width] = tops[bits][...]
-        columns[here, quarter + width :] = gots[bits][:, quarter + width :]
-        flipped[:width, here] = sides[bits][:, :width].astype(jnp.float32).T.astype(jnp.bfloat16)
-        flipped[width : 2 * width, here] = (
-            gots[bits][:, quarter : quarter + width].astype(jnp.float32).T.astype(jnp.bfloat16)
-        )
-        flipped[2 * width :, here] = (
-            sides[bits][:, width : 2 * width].astype(jnp.float32).T.astype(jnp.bfloat16)
-        )
-    size = width // 3
-    for third in range(3):
-        rows = slice(third * size, (third + 1) * size)
-        up_out[rows, :] = plain_dot(flipped[rows, :], columns[:, :quarter])
-        middle = slice(width + third * size, width + (third + 1) * size)
-        rest_out[rows, :width] = plain_dot(
-            flipped[middle, :], columns[:, quarter : quarter + width]
-        )
-        last = slice(2 * width + third * size, 2 * width + (third + 1) * size)
-        rest_out[rows, width:] = plain_dot(flipped[last, :], columns[:, quarter + width :])
-
-
-def final_kernel(received, tokens, residual, rows, weight_in, out, weight, joined, sems):
+    for entry in range(batch):
+        here = slice(entry * tok_count, (entry + 1) * tok_count)
+        columns[here, :width] = gots[entry][:, :width]
+        columns[here, width : 2 * width] = tops[entry][...]
+        columns[here, 2 * width :] = gots[entry][:, 2 * width :]
+        flipped[:width, here] = flip(sides[entry][:, :width])
+        flipped[width : 2 * width, here] = flip(gots[entry][:, width : 2 * width])
+        flipped[2 * width :, here] = flip(sides[entry][:, width:])
+    part[...] = plain_dot(flipped[:width, :], columns[:, :width])
+    store_halves(part, index[0], orders[0], up_keep, up_send)
+    rest[:, :width] = plain_dot(flipped[width : 2 * width, :], columns[:, width : 2 * width])
+    last = plain_dot(flipped[2 * width :, :], columns[:, 2 * width :])
+    rest[:, width:] = last[:, : rest.shape[1] - width]
+    store_halves(rest, index[1], orders[1], rest_keep, rest_send)
+
+
+def fold_kernel(bits, bit, keep, got, keep_out, send_out):
+    for entry in range(keep_out.shape[0]):
+        lower, upper = entry % bits, entry // bits
+        base = upper * 2 * bits + lower
+        mine, other = base + bit[0] * bits, base + (1 - bit[0]) * bits
+        keep_out[entry] = keep[mine] + got[mine].astype(jnp.float32)
+        send_out[entry] = (keep[other] + got[other].astype(jnp.float32)).astype(jnp.bfloat16)
+
+
+def collect_kernel(batch, batch_index, *refs):
+    entries = refs[:batch]
+    down_out, up_out, out_out, held = refs[batch:]
+    rows, total = entries[0].shape
+    width = down_out.shape[1]
+    piece = width // batch
+    f32 = jnp.float32
+    for entry in range(batch):
+        held[batch_index[0] ^ entry] = entries[entry][...]
+    for place in range(batch):
+        up_out[:, place * width : (place + 1) * width] = held[place, :, :width].astype(f32)
+        down = held[place, :, width : 2 * width].astype(f32)
+        down_out[place * rows : (place + 1) * rows, :] = down
+    tiles = [held[place, :, 2 * width : 2 * width + piece].astype(f32) for place in range(batch)]
+    out_out[...] = jnp.concatenate(tiles, axis=1)
+
+
+def final_kernel(received, tokens, residual, rows, weight_in, out, weight, joined, held, sems):
     parts = received.shape[0]
     tok_count, width = tokens.shape
     channels = width // parts
@@ -1320,7 +1412,7 @@
         cols = slice(group * width, (group + 1) * width)
         grad_normed = grad_normed + right_dot(joined[:, cols], weight[:, cols])
     grad_tokens, _, _ = norm_backward(grad_normed, unit, inv_std, gain)
-    out[...] = residual[...] + grad_tokens
+    spread_rows(residual[...] + grad_tokens, held, out)
 
 
 SHARED_ROWS = 48
@@ -1329,6 +1421,7 @@
 
 
 def chain_kernel(
+    norm_rows,
     in_local,
     sums,
     middle_sums,
@@ -1346,6 +1439,7 @@
     weight_total,
     rate_total,
     shared,
+    pairs,
     grad_kernels,
     kernels,
     waves,
@@ -1357,67 +1451,75 @@
 
     def loads(index):
         here = block_rows(index, BLOCK)
+        later = pl.ds(pl.multiple_of(index * BLOCK + length // 2, BLOCK), BLOCK)
+        pieces = [
+            (source.at[rows], target.at[rows])
+            for source, target in ((grad_kernels_in, grad_kernels), (kernels_in, kernels))
+            for rows in (here, later)
+        ]
+        pieces.append((waves_in.at[:, here], waves.at[:, here]))
         return [
-            pltpu.make_async_copy(
-                grad_kernels_in.at[here], grad_kernels.at[here], sems.at[index]
-            ),
-            pltpu.make_async_copy(kernels_in.at[here], kernels.at[here], sems.at[blocks + index]),
-            pltpu.make_async_copy(
-                waves_in.at[:, here], waves.at[:, here], sems.at[2 * blocks + index]
-            ),
+            pltpu.make_async_copy(source, target, sems.at[number * (blocks // 2) + index])
+            for number, (source, target) in enumerate(pieces)
         ]
 
-    for block in range(blocks):
+    for block in range(blocks // 2):
         for copy in loads(block):
             copy.start()
     width = in_local.shape[0]
-    pair_load = pltpu.make_async_copy(
-        pair_in.at[pl.ds(width, width)], pair_sums, sems.at[3 * blocks]
-    )
+    pair_load = pltpu.make_async_copy(pair_in, pair_sums, sems.at[5 * (blocks // 2)])
     pair_load.start()
     feat_count, fhid = pos_weight.shape
     f32 = jnp.float32
     freq = vectors[3:4, :]
     weight_total[...] = jnp.zeros_like(weight_total)
     rate_total[...] = jnp.zeros_like(rate_total)
-    shared[...] = jnp.zeros_like(shared)
+    pairs[...] = jnp.zeros_like(pairs)
+
+    half = length // 2
+    cols = 2 * LANES
+    weight_pair = doubled(weights[...])
+    freq_pair = twice(freq)
 
     def body(index, carry):
         here = block_rows(index, BLOCK)
+        there = pl.ds(pl.multiple_of(index * BLOCK + half, BLOCK), BLOCK)
         for copy in loads(index):
             copy.wait()
         features, times = feature_block(index * BLOCK, BLOCK, length, feat_count)
-        grads = grad_kernels[here, :]
-        decayed = jnp.sum(grads * kernels[here, :] * times, axis=0, keepdims=True)
-        rate_total[...] = rate_total[...] - decayed
-        windowed = grads * jnp.exp(-rates[...] * times)
-        weight_total[...] = weight_total[...] + exact_tdot(waves[2, here, :fhid], windowed)
-        flow = exact_nt(windowed, weights[...])
-        at, bias_at = 0, 2 * fhid + feat_count
+        windowed = []
+        for rows, time in zip((here, there), times):
+            grads = grad_kernels[rows, :]
+            decayed = jnp.sum(grads * kernels[rows, :] * time, axis=0, keepdims=True)
+            rate_total[...] = rate_total[...] - decayed
+            windowed.append(grads * jnp.exp(-rates[...] * time))
+        windowed = jnp.concatenate(windowed, axis=1)
+        weight_total[...] = weight_total[...] + exact_tdot(waves[2, here, :LANES], windowed)
+        flow = exact_nt(windowed, weight_pair)
         for layer in (2, 1, 0):
-            slope = flow * waves[layer, here, fhid:]
-            below = waves[layer - 1, here, :fhid] if layer else features
+            slope = flow * waves[layer, here, LANES:]
+            below = waves[layer - 1, here, :LANES] if layer else features
             count = below.shape[1]
-            shared[at : at + count, :] = shared[at : at + count, :] + exact_tdot(below, slope)
-            at += count
-            row = slice(bias_at + layer, bias_at + layer + 1)
-            shared[row, :] = shared[row, :] + jnp.sum(slope, axis=0, keepdims=True)
+            pairs[layer, :count, :] = pairs[layer, :count, :] + exact_tdot(below, slope)
+            row = slice(LANES, LANES + 1)
+            pairs[layer, row, :] = pairs[layer, row, :] + jnp.sum(slope, axis=0, keepdims=True)
             if layer:
                 weight = inner_weight if layer == 1 else third_weight
-                flow = exact_nt(slope * freq, weight[...].astype(f32))
+                flow = exact_nt(slope * freq_pair, doubled(weight[...].astype(f32)))
         return carry
 
-    lax.fori_loop(0, blocks, body, 0)
+    lax.fori_loop(0, blocks // 2, body, 0)
     grad_freq = jnp.zeros_like(freq)
     at, bias_at = 0, 2 * fhid + feat_count
     for layer, weight in ((2, third_weight), (1, inner_weight), (0, pos_weight)):
         count = weight.shape[0]
-        matrix = shared[at : at + count, :]
-        row = slice(bias_at + layer, bias_at + layer + 1)
+        matrix = pairs[layer, :count, :fhid] + pairs[layer, count : 2 * count, fhid:]
+        both = pairs[layer, LANES : LANES + 1, :]
+        vector = both[:, :fhid] + both[:, fhid:]
         grad_freq = grad_freq + jnp.sum(weight[...].astype(f32) * matrix, axis=0, keepdims=True)
-        grad_freq = grad_freq + vectors[layer : layer + 1, :] * shared[row, :]
+        grad_freq = grad_freq + vectors[layer : layer + 1, :] * vector
         shared[at : at + count, :] = matrix * freq
-        shared[row, :] = shared[row, :] * freq
+        shared[bias_at + layer : bias_at + layer + 1, :] = vector * freq
         at += count
     shared[bias_at + 3 : bias_at + 4, :] = grad_freq
     pair_load.wait()
@@ -1429,6 +1531,7 @@
     bias = exact_nt(jnp.broadcast_to(column_sums, ones.shape), in_wide)[0:1]
     everywhere = small_out.at[:, :SHARED_ROWS, :]
     per = width // LANES
+    gain = (gain - row_of(norm_rows, "pre_bias") * bias) / row_of(norm_rows, "pre_gain")
     store_rows(everywhere, 0, lane_rows(gain))
     store_rows(everywhere, per, lane_rows(bias))
     at = 2 * per
@@ -1441,9 +1544,11 @@
     store_rows(small_out.at[:, SHARED_ROWS : SHARED_ROWS + LAID_ROWS, :], 0, sums[:15, :])
     own = small_out.at[:, SHARED_ROWS + LAID_ROWS :, :]
     for order in range(2):
-        cols = slice(order * LANES, (order + 1) * LANES)
-        store_rows(own, order * fhid, weight_total[:, cols])
-        store_rows(own, 2 * fhid + order, rate_total[:, cols])
+        first = slice(order * LANES, (order + 1) * LANES)
+        second = slice(cols + order * LANES, cols + (order + 1) * LANES)
+        both = weight_total[:fhid, first] + weight_total[fhid:, second]
+        store_rows(own, order * fhid, both)
+        store_rows(own, 2 * fhid + order, rate_total[:, first])
     store_rows(own, 2 * fhid + 2, sums[15:17, :])
 
 
@@ -1501,6 +1606,15 @@
 
 def lane_row(block):
     return jnp.concatenate([block[place : place + 1] for place in range(block.shape[0])], axis=1)
+
+
+def last_fold_kernel(up_keep, up_got, rest_keep, rest_got, out):
+    f32, low = jnp.float32, jnp.bfloat16
+    width = up_keep.shape[2]
+    wide = width + rest_keep.shape[2]
+    out[:, :width] = (up_keep[0] + up_got[0].astype(f32)).astype(low)
+    out[:, width:wide] = (rest_keep[0] + rest_got[0].astype(f32)).astype(low)
+    out[:, wide:] = jnp.zeros((out.shape[0], out.shape[1] - wide), low)
 
 
 def finish_kernel(batch, channels, batch_index, *refs):
@@ -1700,19 +1814,28 @@
     swap_list = [bit_list[1], bit_list[0]] + bit_list[2:]
     batch_bits = [1 << k for k in range(batch_parts.bit_length() - 1)]
 
-    chunks = {0: tokens}
+    tokens, grad_top, own_normed = call_kernel(
+        norm_kernel,
+        [((tok_count, width), low)] * 3,
+        [tokens, cotangent[0], pre_gain, pre_bias],
+        micros=1,
+        scratch=[((width // LANES, tok_count, LANES), f32)],
+        name="norm",
+    )
+    chunks = {0: own_normed}
     for bits in range(2, seq_parts, 2):
-        chunks[bits] = swapped(tokens, "seq", bits)
+        chunks[bits] = swapped(own_normed, "seq", bits)
 
     quarters = hidden_units // width
+    half = length // 2
     seq_scalar = seq_rank.astype(jnp.int32)[None]
     batch_scalar = batch_rank.astype(jnp.int32)[None]
     start_scalar = start.astype(jnp.int32)[None]
-    wave, back, rows, in_local, rows_local, weights_local, rates_local, vectors = call_kernel(
+    wave, turn, rows, in_local, rows_local, weights_local, rates_local, vectors = call_kernel(
         lambda *refs: wave_kernel(channels, *refs),
         [
-            ((2 * length, length), low),
-            ((length, 2 * length), low),
+            ((length, half), low),
+            ((length, LANES), f32),
             ((ROW_COUNT, width), f32),
             ((width, wide), low),
             ((ROW_COUNT, LANES), f32),
@@ -1742,13 +1865,12 @@
             in_weight,
         ],
         micros=8.5,
-        spaces="s" + "v" * 17 + "h" + "hh" + "v" * 6,
+        spaces="s" + "v" * 17 + "h" + "h" + "v" * 7,
         scratch=[
-            ((8, 32, length), f32),
-            ((2 * length, length), low),
-            ((length, 2 * length), low),
+            ((4, 32, half), f32),
+            ((length, half), low),
             ((width, 3 * width), low),
-            3,
+            2,
         ],
         name="waves",
     )
@@ -1761,9 +1883,9 @@
     spectrum, kernels, filter_waves = call_kernel(
         filter_kernel,
         [
-            ((2 * length, 2 * LANES), f32),
+            ((2, length, 2 * LANES), f32),
             ((length, 2 * LANES), f32),
-            ((3, length, 2 * fhid), f32),
+            ((3, half, 4 * fhid), f32),
         ],
         [
             pos_weight,
@@ -1772,25 +1894,25 @@
             vectors,
             weights_local,
             rates_local,
+            turn,
             wave,
         ],
         micros=13,
-        spaces="v" * 6 + "h" + "vvv",
+        spaces="v" * 7 + "h" + "vvv",
         scratch=[
             ((length, 2 * LANES), low),
             ((length, 2 * LANES), low),
-            ((2 * length, length), low),
-            length // BLOCK,
+            ((length, half), low),
+            1,
         ],
         name="filters",
     )
-    grad_top = cotangent[0]
     tops = over_batch(grad_top)
     spectrum, *tops = lax.optimization_barrier((spectrum, *tops))
 
     dense = tok_count * channels // LANES
     (
-        norm_pair,
+        normed,
         projected,
         product,
         gate,
@@ -1802,32 +1924,32 @@
     ) = call_kernel(
         lambda *refs: front_kernel(seq_parts, *refs),
         [
-            ((length, 2 * width), low),
-            ((length, wide), f32),
-            ((length, LANES), low),
-            ((length, LANES), low),
-            ((length, LANES), low),
-            ((length, LANES), low),
-            ((2 * length, LANES), f32),
-            ((2 * length, LANES), f32),
+            ((length, width), low),
+            ((2, PAD + half, wide), f32),
+            ((half, 2 * LANES), low),
+            ((half, 2 * LANES), low),
+            ((half, 2 * LANES), low),
+            ((half, 2 * LANES), low),
+            ((2, length, LANES), f32),
+            ((2, length, LANES), f32),
             ((seq_parts, dense, LANES), low),
         ],
         [seq_scalar]
         + [chunks[part] for part in range(seq_parts)]
-        + [rows, in_local, rows_local, wave, back, spectrum],
+        + [in_local, rows_local, wave, turn, spectrum],
         micros=13,
-        spaces="s" + "v" * seq_parts + "vvvhhh" + "hhvvvvhhv",
+        spaces="s" + "v" * seq_parts + "vvhhh" + "hhvvvvhhv",
         scratch=[
             ((length, width), low),
-            ((2 * length, LANES), low),
-            ((2 * length, length), low),
-            ((length, 2 * length), low),
-            ((2 * length, 2 * LANES), f32),
-            ((length, 2 * width), low),
-            ((length, wide), f32),
-            ((2 * length, LANES), f32),
-            ((2 * length, LANES), f32),
-            ((length, LANES), low),
+            ((half, 2 * LANES), low),
+            ((half, 2 * LANES), low),
+            ((length, half), low),
+            ((length, LANES), f32),
+            ((2, length, 2 * LANES), f32),
+            ((2, PAD + half, wide), f32),
+            ((2, length, LANES), f32),
+            ((2, length, LANES), f32),
+            ((half, 2 * LANES), low),
             7,
         ],
         name="front",
@@ -1838,17 +1960,19 @@
     branch_quarter = width // batch_parts
     rows_quarter = hidden_units // (seq_parts * batch_parts)
     assert quarter == width and seq_parts * rows_quarter == width
-    got_width = quarter + width + branch_quarter
-    outputs, grad_residual, sides, grad_mixer, middle_sums, *gots = call_kernel(
+    up_width = quarter + branch_quarter
+    padded = quarter + -(-branch_quarter // LANES) * LANES
+    message = padded + width
+    outputs, grad_residual, grad_mixer, middle_sums, sides, *gots = call_kernel(
         lambda *refs: middle_kernel(seq_parts, *refs),
         [
             ((tok_count, width), f32),
             ((tok_count, width), f32),
-            ((tok_count, 2 * width), low),
             ((seq_parts, dense, LANES), low),
             (((4 * width + hidden_units) // LANES, LANES), f32),
         ]
-        + [((tok_count, got_width), low)] * batch_parts,
+        + [((tok_count, 2 * width), low)]
+        + [((tok_count, message), low)] * batch_parts,
         [
             batch_scalar,
             mixer_back,
@@ -1871,34 +1995,43 @@
             ((quarters, tok_count, width), low),
             ((quarters, tok_count, width), low),
             ((batch_parts, tok_count, width), low),
-            ((batch_parts, tok_count, branch_quarter), low),
+            ((batch_parts, tok_count, padded - quarter), low),
             ((quarters, 1, width), f32),
+            ((width // LANES, tok_count, LANES), f32),
             1 + 2 * quarters,
         ],
         name="middle",
     )
     grad_mixer_chan = lax.all_to_all(grad_mixer, "seq", 0, 0, tiled=True)
 
+    def bit_of(bits):
+        return ((seq_rank // bits) % 2).astype(jnp.int32)[None]
+
+    def fold(keep, got, bits, left):
+        size = keep.shape[0] // 2
+        block = keep.shape[1:]
+        place = left.index(bits)
+        return call_kernel(
+            lambda *refs: fold_kernel(1 << place, *refs),
+            [((size,) + block, f32), ((size,) + block, low)],
+            [bit_of(bits), keep, got],
+            micros=1,
+            spaces="svvvv",
+            name="fold",
+        )
+
+    grad_mixer_chan = lax.all_to_all(grad_mixer, "seq", 0, 0, tiled=True)
     sides = over_batch(sides)
     gots = [gots[0]] + [swapped(gots[bits], "batch", bits) for bits in range(1, batch_parts)]
-    up_part, rest_part = call_kernel(
-        lambda *refs: weight_kernel(batch_parts, *refs),
-        [((width, quarter), f32), ((width, width + branch_quarter), f32)],
-        sides + tops + gots,
-        micros=6,
-        scratch=[
-            ((3 * width, batch_parts * tok_count), low),
-            ((batch_parts * tok_count, got_width), low),
-        ],
-        name="weights",
-    )
+    rows_each = width // seq_parts
+
     blocks = length // BLOCK
     packed, grad_proj, grad_kernels, sums = call_kernel(
         lambda *refs: back_kernel(channels, *refs),
         [
             ((seq_parts, 3 * dense, LANES), low),
             ((length, wide), low),
-            ((length, 2 * LANES), f32),
+            ((2, half, 2 * LANES), f32),
             ((24, LANES), f32),
         ],
         [
@@ -1908,62 +2041,70 @@
             after,
             gated,
             rows_local,
+            turn,
             product_wave,
             gated_wave,
             spectrum,
             wave,
-            back,
             projected,
         ],
         micros=15,
-        spaces="v" * 6 + "h" * 6 + "vvvv",
-        scratch=[((length, LANES), low)] * 4
+        spaces="v" * 7 + "h" * 5 + "vvvv",
+        scratch=[((half, 2 * LANES), low)] * 4
         + [
-            ((2 * length, 2 * LANES), low),
-            ((2 * length, length), low),
-            ((length, 2 * length), low),
-            ((2 * length, 2 * LANES), f32),
-            ((2 * length, LANES), f32),
-            ((2 * length, LANES), f32),
-            ((length, wide), f32),
-            3 * blocks + 3,
+            ((half, 4 * LANES), low),
+            ((half, 4 * LANES), low),
+            ((length, half), low),
+            ((2, length, 2 * LANES), f32),
+            ((2, length, LANES), f32),
+            ((2, length, LANES), f32),
+            ((2, PAD + half, wide), f32),
+            ((2, half + PAD, LANES), f32),
+            5,
         ],
         name="back",
     )
     proj_back = lax.all_to_all(packed, "seq", 0, 0, tiled=True)
-    pair_part = left_dot(norm_pair, grad_proj)
+    orders = (bit_list, swap_list)
+    halves_of = [
+        ((seq_parts // 2, rows_each, columns), dtype)
+        for columns in (width, width + branch_quarter)
+        for dtype in (f32, low)
+    ]
+    up_keep, up_send, rest_keep, rest_send = call_kernel(
+        lambda *refs: weight_kernel(batch_parts, (orders[0][0], orders[1][0]), *refs),
+        halves_of,
+        [jnp.concatenate([bit_of(order[0]) for order in orders])] + sides + tops + gots,
+        micros=6,
+        spaces="s" + "v" * (3 * batch_parts + 4),
+        scratch=[
+            ((3 * width, batch_parts * tok_count), low),
+            ((batch_parts * tok_count, width + padded), low),
+            ((width, width), f32),
+            ((width, width + branch_quarter), f32),
+        ],
+        name="weights",
+    )
+    up_got = swapped(up_send, "seq", orders[0][0])
+    rest_got = swapped(rest_send, "seq", orders[1][0])
+
+    pair_part = left_dot(normed, grad_proj)
     in_rows = width // (seq_parts * batch_parts)
     in_count = 3 * in_rows
     in_part = (
-        pair_part[:width]
-        .reshape(seq_parts, batch_parts, in_rows, 3, LANES)
+        pair_part.reshape(seq_parts, batch_parts, in_rows, 3, LANES)
         .transpose(1, 0, 3, 2, 4)
         .reshape(batch_parts, seq_parts * in_count, LANES)
     )
     small_rows = SHARED_ROWS + LAID_ROWS + OWN_ROWS
-    pair_part, in_part, up_part, rest_part = lax.optimization_barrier(
-        (pair_part, in_part, up_part, rest_part)
-    )
-    up_quarter = halved(
-        up_part.reshape(seq_parts, -1, quarter), "seq", seq_rank, bit_list
-    ).astype(low)
-    rest_quarter = halved(
-        rest_part.reshape(seq_parts, -1, width + branch_quarter), "seq", seq_rank, swap_list
-    ).astype(low)
-    weights_all = natural(
-        over_batch(jnp.concatenate([up_quarter, rest_quarter], axis=1)), batch_rank
-    )
-    final_up = jnp.concatenate([part[:, :quarter] for part in weights_all], axis=1).astype(f32)
-    final_down = jnp.concatenate(
-        [part[:, quarter : quarter + width] for part in weights_all], axis=0
-    ).astype(f32)
-    final_out = jnp.concatenate(
-        [part[:, quarter + width :] for part in weights_all], axis=1
-    ).astype(f32)
+    in_part, pair_part, up_keep, rest_keep = lax.optimization_barrier(
+        (in_part, pair_part, up_keep, rest_keep)
+    )
     (small,) = call_kernel(
         chain_kernel,
         [((batch_parts, small_rows, LANES), f32)],
         [
+            rows,
             in_local,
             sums,
             middle_sums,
@@ -1973,26 +2114,32 @@
             vectors,
             weights_local,
             rates_local,
-            grad_kernels,
+            grad_kernels.reshape(length, 2 * LANES),
             kernels,
             filter_waves,
             pair_part,
         ],
         micros=12,
-        spaces="v" * 9 + "hhhh" + "v",
+        spaces="v" * 10 + "hhhh" + "v",
         scratch=[
-            ((fhid, 2 * LANES), f32),
+            ((2 * fhid, 4 * LANES), f32),
             ((1, 2 * LANES), f32),
             ((2 * fhid + 40, fhid), f32),
+            ((3, LANES + 8, 2 * fhid), f32),
             ((length, 2 * LANES), f32),
             ((length, 2 * LANES), f32),
-            ((3, length, 2 * fhid), f32),
+            ((3, length // 2, 4 * fhid), f32),
             ((width, wide), f32),
-            3 * blocks + 1,
+            5 * (blocks // 2) + 1,
         ],
         name="chain",
     )
     small, proj_back = lax.optimization_barrier((small, proj_back))
+
+    def next_fold(keep, got, order, step):
+        left = [bits for bits in bit_list if bits not in order[:step]]
+        return fold(keep, got, order[step], left)
+
     left = list(batch_bits)
     for bits in batch_bits[:-1]:
         in_keep, in_send = halves(in_part, batch_rank, bits, left)
@@ -2015,6 +2162,10 @@
         micros=2,
         name="spread",
     )
+    up_keep, up_send = next_fold(up_keep, up_got, orders[0], 1)
+    rest_keep, rest_send = next_fold(rest_keep, rest_got, orders[1], 1)
+    up_got = swapped(up_send, "seq", orders[0][1])
+    rest_got = swapped(rest_send, "seq", orders[1][1])
     mixed_send, proj_back = lax.optimization_barrier((mixed_send, proj_back))
     mixed_got = lax.all_to_all(mixed_send, "seq", 0, 0, tiled=True)
     (grad_inputs,) = call_kernel(
@@ -2023,7 +2174,12 @@
         [proj_back, tokens, grad_residual, rows, in_weight],
         micros=5.5,
         spaces="vvvvhv",
-        scratch=[((width, 3 * width), low), ((tok_count, 3 * width), low), 1],
+        scratch=[
+            ((width, 3 * width), low),
+            ((tok_count, 3 * width), low),
+            ((width // LANES, tok_count, LANES), f32),
+            1,
+        ],
         name="final",
     )
     done_rows = SHARED_ROWS + seq_parts * LAID_ROWS + OWN_ROWS
@@ -2033,6 +2189,33 @@
         [mixed_got, small],
         micros=2,
         name="merge",
+    )
+    up_keep, up_send = next_fold(up_keep, up_got, orders[0], 2)
+    rest_keep, rest_send = next_fold(rest_keep, rest_got, orders[1], 2)
+    up_got = swapped(up_send, "seq", orders[0][2])
+    rest_got = swapped(rest_send, "seq", orders[1][2])
+    lasts = over_batch(last)
+    up_got, grad_inputs, last = lax.optimization_barrier((up_got, grad_inputs, last))
+    total = -(-(2 * width + branch_quarter) // LANES) * LANES
+    (weights_done,) = call_kernel(
+        last_fold_kernel,
+        [((rows_each, total), low)],
+        [up_keep, up_got, rest_keep, rest_got],
+        micros=1,
+        name="last_fold",
+    )
+    final_down, final_up, final_out = call_kernel(
+        lambda *refs: collect_kernel(batch_parts, *refs),
+        [
+            ((batch_parts * rows_each, width), f32),
+            ((rows_each, hidden_units), f32),
+            ((rows_each, width), f32),
+        ],
+        [batch_scalar] + over_batch(weights_done),
+        micros=3,
+        spaces="s" + "v" * (batch_parts + 3),
+        scratch=[((batch_parts, rows_each, total), low)],
+        name="collect",
     )
     (
         final_in,
@@ -2081,7 +2264,7 @@
             ((2, channels), f32),
             ((2, channels), f32),
         ],
-        [batch_scalar] + over_batch(last),
+        [batch_scalar] + lasts,
         micros=3,
         spaces="s" + "v" * batch_parts + "v" * 21,
         scratch=[

time: 217 us -> 208 us (0.959)
  other arithmetic: 8.62 us -> 1.65 us
  local copies, waits for them, and re-layouts: 17.4 us -> 12.7 us
  waiting for transfers between devices: 45.7 us -> 49.4 us
    convert_element_type x6 -> x0, local copies, waits for them, and re-layouts: 6.25 us -> none  [halved(): got = swapped(send.astype(jnp.bfloat16), axis, bits)]
    add x4 -> x0, other arithmetic: 4.23 us -> none  [halved(): total = keep + got.astype(jnp.float32)]
    ppermute x32, waiting for transfers between devices: 32.7 us -> 36.3 us  [swapped(): lax.ppermute(value, axis, [(source, source ^ bits) for source in range(co...]
    convert_element_type x5 -> x0, other arithmetic: 3.1 us -> none  [the longest x1 1.11 us: dense_device(): jnp.concatenate([part[:, :quarter] for part in weights_all], axis=1)]
    all_to_all x1, starting transfers between devices: 5.86 us -> 3.67 us  [dense_device(): mixed_got = lax.all_to_all(mixed_send, 'seq', 0, 0, tiled=True)]
    unnamed x50 -> x64, local copies, waits for them, and re-layouts: 6.57 us -> 8.61 us
    pallas_call x11 -> x18, Pallas kernels: 91.6 us -> 91.7 us  [call_kernel(): pl.pallas_call(kernel, out_shape=shapes, in_specs=specs[:len(args)], out_...]
  transfers between devices with their start and end apart: 36 -> 36, of which waited for: 7 -> 12; matrix products, arithmetic and copies ran while one was open for 9% -> 4% of each run, Pallas kernels for 31% -> 31%
where the time goes in v2:
time: 208 us; the launch traced here: 207 us
  Pallas kernels  91.7 us (44%)
  waiting for transfers between devices  49.4 us (24%)
  starting transfers between devices  48.1 us (23%)
  local copies, waits for them, and re-layouts  12.7 us (6%)
  matrix products  2.13 us (1%)
    pallas_call x18, Pallas kernels, call_kernel(): pl.pallas_call(kernel, out_shape=shapes, in_specs=specs[:len(args)], out_...  91.7 us
    ppermute x32, waiting for transfers between devices, swapped(): lax.ppermute(value, axis, [(source, source ^ bits) for source in range(co...  36.3 us
    ppermute x32, starting transfers between devices, swapped(): lax.ppermute(value, axis, [(source, source ^ bits) for source in range(co...  30.8 us
    unnamed x64, local copies, waits for them, and re-layouts  8.61 us
    all_to_all x1, waiting for transfers between devices, dense_device(): mixer_back = lax.all_to_all(mixer_chan, 'seq', 0, 0, tiled=True)  7.78 us
    all_to_all x1, starting transfers between devices, dense_device(): mixer_back = lax.all_to_all(mixer_chan, 'seq', 0, 0, tiled=True)  6.59 us
    all_to_all x1, waiting for transfers between devices, dense_device(): grad_mixer_chan = lax.all_to_all(grad_mixer, 'seq', 0, 0, tiled=True)  5.25 us
  transfers between devices with their start and end apart: 36, of which 12 were waited for; matrix products, arithmetic and copies ran while one was open for 4% of the time, Pallas kernels for 31%

profile of v2, /device:TPU:0, one launch (start us, length us, event | category | flops | bytes accessed | tf_op | source)
XLA Modules:
  0.0 206.9 jit_solution(8903582173506175542)
XLA Ops:
  0.7 2.1 norm.1
  2.7 3.0 %collective-permute-start.1 = (bf16[128,768]{1,0:T(8,128)(2,1)}, bf16[128,768]{1,0:T(8,128)(2,1)S(1)}, u32[]{:S(2)}, u32[]{:S(2)}) collective-permute-start(bf16[128,768]{1,0:T(8,128)(2,1)} %get-tuple-element.119.refs_1_), channel_id=1, source_target_pairs={{0,2},{1,3},{2,0},{3,1},{4,6},{5,7},{6,4},{7,5},{8,10},{9,11},{10,... | collective-permute-start | bytes 589832 | tf_op jit(solution)/shard_map/ppermute | solution.py:1724
  5.7 2.6 %collective-permute-start.2 = (bf16[128,768]{1,0:T(8,128)(2,1)}, bf16[128,768]{1,0:T(8,128)(2,1)S(1)}, u32[]{:S(2)}, u32[]{:S(2)}) collective-permute-start(bf16[128,768]{1,0:T(8,128)(2,1)} %get-tuple-element.119.refs_1_), channel_id=1, source_target_pairs={{0,4},{1,5},{2,6},{3,7},{4,0},{5,1},{6,2},{7,3},{8,12},{9,13},{10,... | collective-permute-start | bytes 589832 | tf_op jit(solution)/shard_map/ppermute | solution.py:1724
  10.1 5.6 %waves.1 = (bf16[1024,512]{1,0:T(8,128)(2,1)}, f32[1024,128]{1,0:T(8,128)}, f32[32,768]{1,0:T(8,128)}, bf16[768,384]{1,0:T(8,128)(2,1)}, f32[32,128]{1,0:T(8,128...) custom-call(s32[1]{0:T(128)} %bitcast.4.refs_0_, bf16[768]{0:T(1024)(128)(2,1)} %refs_1_.1, ...), custom_call_target="tpu_custom_call" | custom-call | flops 1 | bytes 25500000 | tf_op jit(solution)/shard_map/waves/pallas_call | solution.py:472
  17.3 5.8 %collective-permute-done.2.refs_5_ = bf16[128,768]{1,0:T(8,128)(2,1)S(1)} collective-permute-done((bf16[128,768]{1,0:T(8,128)(2,1)}, bf16[128,768]{1,0:T(8,128)(2,1)S(1)}, u32[]{:S(2)}, u32[]{:S(2)}) %collective-permute-start.2) | collective-permute-done | bytes 196640 | tf_op jit(solution)/shard_map/ppermute | solution.py:1724
  26.8 8.6 %filters.1 = (f32[2,1024,256]{2,1,0:T(8,128)}, f32[1024,256]{1,0:T(8,128)}, f32[3,512,256]{2,1,0:T(8,128)}) custom-call(bf16[33,64]{1,0:T(8,128)(2,1)} %pos_weight.3, bf16[64,64]{1,0:T(8,128)(2,1)} %inner_weight.3, bf16[64,64]{1,0:T(8,128)(2,1)} %third_weight.3, f32[4,64]{1,0:T(4,128)} %get-tuple-element.128.vectors, f32[64,256]{1,0:T(8,128)} %get-tuple-element.129.weights, ...), custom_call_target="tpu_custom_call" | custom-call | flops 1 | bytes 39000000 | tf_op jit(solution)/shard_map/filters/pallas_call | solution.py:472
  35.5 3.4 %collective-permute-done.6.refs_8_ = bf16[128,768]{1,0:T(8,128)(2,1)S(1)} collective-permute-done((bf16[128,768]{1,0:T(8,128)(2,1)S(1)}, bf16[128,768]{1,0:T(8,128)(2,1)S(1)}, u32[]{:S(2)}, u32[]{:S(2)}) %collective-permute-start.6) | collective-permute-done | bytes 196640 | tf_op jit(solution)/shard_map/ppermute | solution.py:1724
  39.7 9.5 %front.1 = (bf16[1024,768]{1,0:T(8,128)(2,1)}, f32[2,520,384]{2,1,0:T(8,128)}, bf16[512,256]{1,0:T(8,128)(2,1)}, bf16[512,256]{1,0:T(8,128)(2,1)}, bf16[512,256]...) custom-call(s32[1]{0:T(128)} %bitcast.1.refs_0_, ...), custom_call_target="tpu_custom_call" | custom-call | flops 1 | bytes 39000000 | tf_op jit(solution)/shard_map/front/pallas_call | solution.py:472
  49.2 6.6 %all-to-all-start = ((bf16[8,96,128]{2,1,0:T(8,128)(2,1)}), bf16[8,96,128]{2,1,0:T(8,128)(2,1)S(1)}, u32[]{:S(2)}, u32[]{:S(2)}) async-start(bf16[8,96,128]{2,1,0:T(8,128)(2,1)} %get-tuple-element.134), calls=%async_computation | async-start | bytes 393216 | tf_op jit(solution)/shard_map/all_to_all | solution.py:1957
  55.8 7.8 %all-to-all-done.refs_1_ = bf16[8,96,128]{2,1,0:T(8,128)(2,1)S(1)} async-done(((bf16[8,96,128]{2,1,0:T(8,128)(2,1)}), bf16[8,96,128]{2,1,0:T(8,128)(2,1)S(1)}, u32[]{:S(2)}, u32[]{:S(2)}) %all-to-all-start) | async-done | bytes 196640 | tf_op jit(solution)/shard_map/all_to_all | solution.py:1957
  64.2 11.0 %middle.1 = (f32[128,768]{1,0:T(8,128)}, f32[128,768]{1,0:T(8,128)}, bf16[8,96,128]{2,1,0:T(8,128)(2,1)}, f32[48,128]{1,0:T(8,128)}, bf16[128,1536]{1,0:T(8,128)...) custom-call(s32[1]{0:T(128)} %bitcast.refs_0_, ...), custom_call_target="tpu_custom_call" | custom-call | flops 1 | bytes 33000000 | tf_op jit(solution)/shard_map/middle/pallas_call | solution.py:472
  76.8 3.6 %all-to-all-start.1 = ((bf16[8,96,128]{2,1,0:T(8,128)(2,1)}), bf16[8,96,128]{2,1,0:T(8,128)(2,1)S(1)}, u32[]{:S(2)}, u32[]{:S(2)}) async-start(bf16[8,96,128]{2,1,0:T(8,128)(2,1)} %get-tuple-element.139), calls=%async_computation.1 | async-start | bytes 393216 | tf_op jit(solution)/shard_map/all_to_all | solution.py:2023
  82.7 5.3 %all-to-all-done.1.refs_0_ = bf16[8,96,128]{2,1,0:T(8,128)(2,1)S(1)} async-done(((bf16[8,96,128]{2,1,0:T(8,128)(2,1)}), bf16[8,96,128]{2,1,0:T(8,128)(2,1)S(1)}, u32[]{:S(2)}, u32[]{:S(2)}) %all-to-all-start.1) | async-done | bytes 196640 | tf_op jit(solution)/shard_map/all_to_all | solution.py:2023
  88.6 12.4 %back.1 = (bf16[8,288,128]{2,1,0:T(8,128)(2,1)}, bf16[1024,384]{1,0:T(8,128)(2,1)}, f32[2,512,256]{2,1,0:T(8,128)}, f32[24,128]{1,0:T(8,128)}) custom-call(bf16[8,96,128]{2,1,0:T(8,128)(2,1)} %copy-done.6, bf16[512,256]{1,0:T(8,128)(2,1)} %get-tuple-element.140.refs_1_, bf16[512,256]{1,0:T(8,128)(2,1)} %get-tuple-element.141.refs_2_, ...), custom_call_target="tpu_custom_call" | custom-call | flops 1 | bytes 45000000 | tf_op jit(solution)/shard_map/back/pallas_call | solution.py:472
  101.0 3.5 %all-to-all-start.2 = ((bf16[8,288,128]{2,1,0:T(8,128)(2,1)}), bf16[8,288,128]{2,1,0:T(8,128)(2,1)S(1)}, u32[]{:S(2)}, u32[]{:S(2)}) async-start(bf16[8,288,128]{2,1,0:T(8,128)(2,1)} %get-tuple-element.171), calls=%async_computation.2 | async-start | bytes 1179648 | tf_op jit(solution)/shard_map/all_to_all | solution.py:2067
  105.2 2.1 %fusion.1.pair_in = f32[768,384]{1,0:T(8,128)S(1)} fusion(bf16[1024,768]{1,0:T(8,128)(2,1)S(1)} %copy-done.31, bf16[1024,384]{1,0:T(8,128)(2,1)} %get-tuple-element.147), kind=kOutput, calls=%fused_computation.10 | convolution fusion | flops 603979776 | bytes 3538944 | tf_op jit(solution)/shard_map/dot_general | solution.py:36
  109.1 5.5 %weights.1 = (f32[4,96,768]{2,1,0:T(8,128)}, bf16[4,96,768]{2,1,0:T(8,128)(2,1)}, f32[4,96,960]{2,1,0:T(8,128)}, bf16[4,96,960]{2,1,0:T(8,128)(2,1)}) custom-call(s32[2]{0:T(128)} %pad_add_fusion.refs_0_, bf16[128,1536]{1,0:T(8,128)(2,1)} %get-tuple-element.148.refs_1_, bf16[128,1536]{1,0:T(8,128)(2,1)} %collective-permute-done.10.refs_2_, ...), custom_call_target="tpu_custom_call" | custom-call | flops 1 | bytes 18000000 | tf_op jit(solution)/shard_map/weights/pallas_call | solution.py:472
  118.5 10.9 %chain.1 = f32[4,96,128]{2,1,0:T(8,128)} custom-call(f32[32,768]{1,0:T(8,128)} %get-tuple-element.136.refs_4_.norm_rows.rows, bf16[768,384]{1,0:T(8,128)(2,1)} %get-tuple-element.124.refs_9_.in_local, f32[24,128]{1,0:T(8,128)} %get-tuple-element.165.sums, f32[48,128]{1,0:T(8,128)} %get-tuple-element.166.middle_sums, bf16[33,64]{1,0:T(8,128)(2,1)} %pos_weight.3, ...), custom_call_target="tpu_custom_call" | custom-call | flops 1 | bytes 36000000 | tf_op jit(solution)/shard_map/chain/pallas_call | solution.py:472
  135.1 3.2 %collective-permute-done.20 = bf16[1,576,128]{2,1,0:T(8,128)(2,1)S(1)} collective-permute-done((bf16[1,576,128]{2,1,0:T(8,128)(2,1)S(1)}, bf16[1,576,128]{2,1,0:T(8,128)(2,1)S(1)}, u32[]{:S(2)}, u32[]{:S(2)}) %collective-permute-start.20) | collective-permute-done | bytes 147488 | tf_op jit(solution)/shard_map/ppermute | solution.py:1724
  141.4 3.7 %all-to-all-start.3 = ((bf16[8,184,128]{2,1,0:T(8,128)(2,1)}), bf16[8,184,128]{2,1,0:T(8,128)(2,1)S(1)}, u32[]{:S(2)}, u32[]{:S(2)}) async-start(bf16[8,184,128]{2,1,0:T(8,128)(2,1)} %get-tuple-element.177), calls=%async_computation.3 | async-start | bytes 753664 | tf_op jit(solution)/shard_map/all_to_all | solution.py:2170
  146.0 2.7 %fold.6 = (f32[2,96,960]{2,1,0:T(8,128)}, bf16[2,96,960]{2,1,0:T(8,128)(2,1)}) custom-call(s32[1]{0:T(128)} %bitcast.10.refs_0_, f32[4,96,960]{2,1,0:T(8,128)} %get-tuple-element.198.refs_1_, bf16[4,96,960]{2,1,0:T(8,128)(2,1)} %copy-done.5), custom_call_target="tpu_custom_call" | custom-call | flops 1 | bytes 3000000 | tf_op jit(solution)/shard_map/fold/pallas_call | solution.py:472
  148.7 2.0 collective-permute-start.27
  150.7 2.4 %fold.4 = (f32[2,96,768]{2,1,0:T(8,128)}, bf16[2,96,768]{2,1,0:T(8,128)(2,1)}) custom-call(s32[1]{0:T(128)} %bitcast.7.refs_0_, f32[4,96,768]{2,1,0:T(8,128)} %get-tuple-element.159.refs_1_, bf16[4,96,768]{2,1,0:T(8,128)(2,1)} %collective-permute-done.16.refs_2_), custom_call_target="tpu_custom_call" | custom-call | flops 1 | bytes 3000000 | tf_op jit(solution)/shard_map/fold/pallas_call | solution.py:472
  154.6 6.2 %collective-permute-done.27.refs_2_ = bf16[2,96,960]{2,1,0:T(8,128)(2,1)S(1)} collective-permute-done((bf16[2,96,960]{2,1,0:T(8,128)(2,1)}, bf16[2,96,960]{2,1,0:T(8,128)(2,1)S(1)}, u32[]{:S(2)}, u32[]{:S(2)}) %collective-permute-start.27) | collective-permute-done | bytes 368672 | tf_op jit(solution)/shard_map/ppermute | solution.py:1724
  161.6 2.1 %fold.7 = (f32[1,96,960]{2,1,0:T(8,128)}, bf16[1,96,960]{2,1,0:T(8,128)(2,1)}) custom-call(s32[1]{0:T(128)} %bitcast.6.refs_0_, f32[2,96,960]{2,1,0:T(8,128)} %get-tuple-element.200.refs_1_, bf16[2,96,960]{2,1,0:T(8,128)(2,1)} %copy-done.8), custom_call_target="tpu_custom_call" | custom-call | flops 1 | bytes 3000000 | tf_op jit(solution)/shard_map/fold/pallas_call | solution.py:472
  163.7 2.7 %collective-permute-start.28 = (bf16[1,96,960]{2,1,0:T(8,128)(2,1)}, bf16[1,96,960]{2,1,0:T(8,128)(2,1)S(1)}, u32[]{:S(2)}, u32[]{:S(2)}) collective-permute-start(bf16[1,96,960]{2,1,0:T(8,128)(2,1)} %get-tuple-element.203), channel_id=1, source_target_pairs={{0,4},{1,5},{2,6},{3,7},{4,0},{5,1},{6,2},{7,3},{8,12},{9,13},{10,... | collective-permute-start | bytes 552968 | tf_op jit(solution)/shard_map/ppermute | solution.py:1724
  169.3 5.5 %final.1 = f32[128,768]{1,0:T(8,128)} custom-call(bf16[8,288,128]{2,1,0:T(8,128)(2,1)} %copy-done.2, bf16[128,768]{1,0:T(8,128)(2,1)} %get-tuple-element.135.refs_2_.tokens, f32[128,768]{1,0:T(8,128)} %get-tuple-element.176.residual, f32[32,768]{1,0:T(8,128)} %get-tuple-element.136.refs_4_.norm_rows.rows, bf16[768,2304]{1,0:T(8,128)(2,1)} %weight_in.1), custom_call_target="tpu_custom_call" | custom-call | flops 1 | bytes 16500000 | tf_op jit(solution)/shard_map/final/pallas_call | solution.py:472
  177.3 3.7 %collective-permute-done.18.up_got = bf16[1,96,768]{2,1,0:T(8,128)(2,1)S(1)} collective-permute-done((bf16[1,96,768]{2,1,0:T(8,128)(2,1)}, bf16[1,96,768]{2,1,0:T(8,128)(2,1)S(1)}, u32[]{:S(2)}, u32[]{:S(2)}) %collective-permute-start.18) | collective-permute-done | bytes 147488 | tf_op jit(solution)/shard_map/ppermute | solution.py:1724
  181.7 2.0 last_fold.1.refs_1_
  185.8 9.2 %collective-permute-done.30.refs_3_ = bf16[96,1792]{1,0:T(8,128)(2,1)S(1)} collective-permute-done((bf16[96,1792]{1,0:T(8,128)(2,1)}, bf16[96,1792]{1,0:T(8,128)(2,1)S(1)}, u32[]{:S(2)}, u32[]{:S(2)}) %collective-permute-start.30) | collective-permute-done | bytes 344096 | tf_op jit(solution)/shard_map/ppermute | solution.py:1724
  199.6 2.9 %finish.1 = (f32[96,2304]{1,0:T(8,128)}, f32[768]{0:T(1024)}, f32[768]{0:T(1024)}, f32[768]{0:T(1024)}, f32[768]{0:T(1024)}, /*index=5*/f32[768]{0:T(1024)}, f32...) custom-call(s32[1]{0:T(128)} %bitcast.refs_0_, ...), custom_call_target="tpu_custom_call" | custom-call | flops 1 | bytes 9000000 | tf_op jit(solution)/shard_map/finish/pallas_call | solution.py:472
  203.9 3.0 %collect.1 = (f32[384,768]{1,0:T(8,128)}, f32[96,3072]{1,0:T(8,128)}, f32[96,768]{1,0:T(8,128)}) custom-call(s32[1]{0:T(128)} %bitcast.refs_0_, bf16[96,1792]{1,0:T(8,128)(2,1)} %last_fold.1.refs_1_, bf16[96,1792]{1,0:T(8,128)(2,1)} %copy-done.10, bf16[96,1792]{1,0:T(8,128)(2,1)} %copy-done.9, bf16[96,1792]{1,0:T(8,128)(2,1)} %copy-done.11), custom_call_target="tpu_custom_call" | custom-call | flops 1 | bytes 9000000 | tf_op jit(solution)/shard_map/collect/pallas_call | solution.py:472
  (133 shorter events, 45.0 us)
Async XLA Ops:
  2.7 13.0 %collective-permute-start.1 = (bf16[128,768]{1,0:T(8,128)(2,1)}, bf16[128,768]{1,0:T(8,128)(2,1)S(1)}, u32[]{:S(2)}, u32[]{:S(2)}) collective-permute-start(bf16[128,768]{1,0:T(8,128)(2,1)} %get-tuple-element.119.refs_1_), channel_id=1, source_target_pairs={{0,2},{1,3},{2,0},{3,1},{4,6},{5,7},{6,4},{7,5},{8,10},{9,11},{10,... | collective-permute-start | bytes 589832 | tf_op jit(solution)/shard_map/ppermute | solution.py:1724
  5.7 17.4 %collective-permute-start.2 = (bf16[128,768]{1,0:T(8,128)(2,1)}, bf16[128,768]{1,0:T(8,128)(2,1)S(1)}, u32[]{:S(2)}, u32[]{:S(2)}) collective-permute-start(bf16[128,768]{1,0:T(8,128)(2,1)} %get-tuple-element.119.refs_1_), channel_id=1, source_target_pairs={{0,4},{1,5},{2,6},{3,7},{4,0},{5,1},{6,2},{7,3},{8,12},{9,13},{10,... | collective-permute-start | bytes 589832 | tf_op jit(solution)/shard_map/ppermute | solution.py:1724
  8.3 14.8 %collective-permute-start.3 = (bf16[128,768]{1,0:T(8,128)(2,1)}, bf16[128,768]{1,0:T(8,128)(2,1)S(1)}, u32[]{:S(2)}, u32[]{:S(2)}) collective-permute-start(bf16[128,768]{1,0:T(8,128)(2,1)} %get-tuple-element.119.refs_1_), channel_id=1, source_target_pairs={{0,6},{1,7},{2,4},{3,5},{4,2},{5,3},{6,0},{7,1},{8,14},{9,15},{10,... | collective-permute-start | bytes 589832 | tf_op jit(solution)/shard_map/ppermute | solution.py:1724
  8.3 14.8 %collective-permute-start.8 = (bf16[128,768]{1,0:T(8,128)(2,1)}, bf16[128,768]{1,0:T(8,128)(2,1)S(1)}, u32[]{:S(2)}, u32[]{:S(2)}) collective-permute-start(bf16[128,768]{1,0:T(8,128)(2,1)} %get-tuple-element.149.refs_3_.refs_5_), channel_id=1, source_target_pairs={{0,16},{8,24},{16,0},{24,8},{1,17},{9,25},{17,1},{25,9},{2,18},{10... | collective-permute-start | bytes 589832 | tf_op jit(solution)/shard_map/ppermute | solution.py:1724
  10.1 15.3 %collective-permute-start.7 = (bf16[128,768]{1,0:T(8,128)(2,1)}, bf16[128,768]{1,0:T(8,128)(2,1)S(1)}, u32[]{:S(2)}, u32[]{:S(2)}) collective-permute-start(bf16[128,768]{1,0:T(8,128)(2,1)} %get-tuple-element.149.refs_3_.refs_5_), channel_id=1, source_target_pairs={{0,8},{8,0},{16,24},{24,16},{1,9},{9,1},{17,25},{25,17},{2,10},{10... | collective-permute-start | bytes 589832 | tf_op jit(solution)/shard_map/ppermute | solution.py:1724
  15.7 19.8 %collective-permute-start = (bf16[128,768]{1,0:T(8,128)(2,1)S(1)}, bf16[128,768]{1,0:T(8,128)(2,1)S(1)}, u32[]{:S(2)}, u32[]{:S(2)}) collective-permute-start(bf16[128,768]{1,0:T(8,128)(2,1)S(1)} %copy-done.19), channel_id=1, source_target_pairs={{0,1},{1,0},{2,3},{3,2},{4,5},{5,4},{6,7},{7,6},{8,9},{9,8},{10,11... | collective-permute-start | bytes 589832 | tf_op jit(solution)/shard_map/ppermute | solution.py:1724
  23.1 12.3 %collective-permute-start.9 = (bf16[128,768]{1,0:T(8,128)(2,1)S(1)}, bf16[128,768]{1,0:T(8,128)(2,1)S(1)}, u32[]{:S(2)}, u32[]{:S(2)}) collective-permute-start(bf16[128,768]{1,0:T(8,128)(2,1)S(1)} %collective-permute-done.8.refs_7_), channel_id=1, source_target_pairs={{0,8},{8,0},{16,24},{24,16},{1,9},{9,1},{17,25},{25,17},{2,10},{10... | collective-permute-start | bytes 589832 | tf_op jit(solution)/shard_map/ppermute | solution.py:1724
  23.2 12.3 %collective-permute-start.4 = (bf16[128,768]{1,0:T(8,128)(2,1)S(1)}, bf16[128,768]{1,0:T(8,128)(2,1)S(1)}, u32[]{:S(2)}, u32[]{:S(2)}) collective-permute-start(bf16[128,768]{1,0:T(8,128)(2,1)S(1)} %collective-permute-done.1.refs_3_), channel_id=1, source_target_pairs={{0,1},{1,0},{2,3},{3,2},{4,5},{5,4},{6,7},{7,6},{8,9},{9,8},{10,11... | collective-permute-start | bytes 589832 | tf_op jit(solution)/shard_map/ppermute | solution.py:1724
  24.8 10.7 %collective-permute-start.5 = (bf16[128,768]{1,0:T(8,128)(2,1)S(1)}, bf16[128,768]{1,0:T(8,128)(2,1)S(1)}, u32[]{:S(2)}, u32[]{:S(2)}) collective-permute-start(bf16[128,768]{1,0:T(8,128)(2,1)S(1)} %collective-permute-done.2.refs_5_), channel_id=1, source_target_pairs={{0,1},{1,0},{2,3},{3,2},{4,5},{5,4},{6,7},{7,6},{8,9},{9,8},{10,11... | collective-permute-start | bytes 589832 | tf_op jit(solution)/shard_map/ppermute | solution.py:1724
  25.3 13.6 %collective-permute-start.6 = (bf16[128,768]{1,0:T(8,128)(2,1)S(1)}, bf16[128,768]{1,0:T(8,128)(2,1)S(1)}, u32[]{:S(2)}, u32[]{:S(2)}) collective-permute-start(bf16[128,768]{1,0:T(8,128)(2,1)S(1)} %collective-permute-done.3.refs_7_), channel_id=1, source_target_pairs={{0,1},{1,0},{2,3},{3,2},{4,5},{5,4},{6,7},{7,6},{8,9},{9,8},{10,11... | collective-permute-start | bytes 589832 | tf_op jit(solution)/shard_map/ppermute | solution.py:1724
  49.2 14.4 %all-to-all-start = ((bf16[8,96,128]{2,1,0:T(8,128)(2,1)}), bf16[8,96,128]{2,1,0:T(8,128)(2,1)S(1)}, u32[]{:S(2)}, u32[]{:S(2)}) async-start(bf16[8,96,128]{2,1,0:T(8,128)(2,1)} %get-tuple-element.134), calls=%async_computation | async-start | bytes 393216 | tf_op jit(solution)/shard_map/all_to_all | solution.py:1957
  75.3 29.3 %collective-permute-start.11 = (bf16[128,1536]{1,0:T(8,128)(2,1)}, bf16[128,1536]{1,0:T(8,128)(2,1)}, u32[]{:S(2)}, u32[]{:S(2)}) collective-permute-start(bf16[128,1536]{1,0:T(8,128)(2,1)} %get-tuple-element.148.refs_1_), channel_id=1, source_target_pairs={{0,16},{8,24},{16,0},{24,8},{1,17},{9,25},{17,1},{25,9},{2,18},{10... | collective-permute-start | bytes 1179656 | tf_op jit(solution)/shard_map/ppermute | solution.py:1724
  76.8 11.1 %all-to-all-start.1 = ((bf16[8,96,128]{2,1,0:T(8,128)(2,1)}), bf16[8,96,128]{2,1,0:T(8,128)(2,1)S(1)}, u32[]{:S(2)}, u32[]{:S(2)}) async-start(bf16[8,96,128]{2,1,0:T(8,128)(2,1)} %get-tuple-element.139), calls=%async_computation.1 | async-start | bytes 393216 | tf_op jit(solution)/shard_map/all_to_all | solution.py:2023
  80.4 28.6 %collective-permute-start.13 = (bf16[128,1792]{1,0:T(8,128)(2,1)}, bf16[128,1792]{1,0:T(8,128)(2,1)}, u32[]{:S(2)}, u32[]{:S(2)}) collective-permute-start(bf16[128,1792]{1,0:T(8,128)(2,1)} %get-tuple-element.154), channel_id=1, source_target_pairs={{0,8},{8,0},{16,24},{24,16},{1,9},{9,1},{17,25},{25,17},{2,10},{10... | collective-permute-start | bytes 1376264 | tf_op jit(solution)/shard_map/ppermute | solution.py:1724
  80.5 28.6 %collective-permute-start.14 = (bf16[128,1792]{1,0:T(8,128)(2,1)}, bf16[128,1792]{1,0:T(8,128)(2,1)}, u32[]{:S(2)}, u32[]{:S(2)}) collective-permute-start(bf16[128,1792]{1,0:T(8,128)(2,1)} %get-tuple-element.155), channel_id=1, source_target_pairs={{0,16},{8,24},{16,0},{24,8},{1,17},{9,25},{17,1},{25,9},{2,18},{10... | collective-permute-start | bytes 1376264 | tf_op jit(solution)/shard_map/ppermute | solution.py:1724
  81.1 28.0 %collective-permute-start.15 = (bf16[128,1792]{1,0:T(8,128)(2,1)}, bf16[128,1792]{1,0:T(8,128)(2,1)}, u32[]{:S(2)}, u32[]{:S(2)}) collective-permute-start(bf16[128,1792]{1,0:T(8,128)(2,1)} %get-tuple-element.156), channel_id=1, source_target_pairs={{0,24},{8,16},{16,8},{24,0},{1,25},{9,17},{17,9},{25,1},{2,26},{10... | collective-permute-start | bytes 1376264 | tf_op jit(solution)/shard_map/ppermute | solution.py:1724
  82.3 26.7 %collective-permute-start.10 = (bf16[128,1536]{1,0:T(8,128)(2,1)}, bf16[128,1536]{1,0:T(8,128)(2,1)}, u32[]{:S(2)}, u32[]{:S(2)}) collective-permute-start(bf16[128,1536]{1,0:T(8,128)(2,1)} %get-tuple-element.148.refs_1_), channel_id=1, source_target_pairs={{0,8},{8,0},{16,24},{24,16},{1,9},{9,1},{17,25},{25,17},{2,10},{10... | collective-permute-start | bytes 1179656 | tf_op jit(solution)/shard_map/ppermute | solution.py:1724
  101.0 29.5 %all-to-all-start.2 = ((bf16[8,288,128]{2,1,0:T(8,128)(2,1)}), bf16[8,288,128]{2,1,0:T(8,128)(2,1)S(1)}, u32[]{:S(2)}, u32[]{:S(2)}) async-start(bf16[8,288,128]{2,1,0:T(8,128)(2,1)} %get-tuple-element.171), calls=%async_computation.2 | async-start | bytes 1179648 | tf_op jit(solution)/shard_map/all_to_all | solution.py:2067
  114.6 14.8 %collective-permute-start.19 = (bf16[2,576,128]{2,1,0:T(8,128)(2,1)S(1)}, bf16[2,576,128]{2,1,0:T(8,128)(2,1)}, u32[]{:S(2)}, u32[]{:S(2)}) collective-permute-start(bf16[2,576,128]{2,1,0:T(8,128)(2,1)S(1)} %fusion), channel_id=1, source_target_pairs={{0,8},{8,0},{16,24},{24,16},{1,9},{9,1},{17,25},{25,17},{2,10},{10... | collective-permute-start | bytes 884744 | tf_op jit(solution)/shard_map/ppermute | solution.py:1724
  115.2 35.6 %collective-permute-start.16 = (bf16[4,96,768]{2,1,0:T(8,128)(2,1)}, bf16[4,96,768]{2,1,0:T(8,128)(2,1)}, u32[]{:S(2)}, u32[]{:S(2)}) collective-permute-start(bf16[4,96,768]{2,1,0:T(8,128)(2,1)} %get-tuple-element.160), channel_id=1, source_target_pairs={{0,1},{1,0},{2,3},{3,2},{4,5},{5,4},{6,7},{7,6},{8,9},{9,8},{10,11... | collective-permute-start | bytes 1769480 | tf_op jit(solution)/shard_map/ppermute | solution.py:1724
  117.0 28.1 %collective-permute-start.26 = (bf16[4,96,960]{2,1,0:T(8,128)(2,1)}, bf16[4,96,960]{2,1,0:T(8,128)(2,1)S(1)}, u32[]{:S(2)}, u32[]{:S(2)}) collective-permute-start(bf16[4,96,960]{2,1,0:T(8,128)(2,1)} %get-tuple-element.199), channel_id=1, source_target_pairs={{0,2},{1,3},{2,0},{3,1},{4,6},{5,7},{6,4},{7,5},{8,10},{9,11},{10,... | collective-permute-start | bytes 2211848 | tf_op jit(solution)/shard_map/ppermute | solution.py:1724
  131.6 6.7 %collective-permute-start.20 = (bf16[1,576,128]{2,1,0:T(8,128)(2,1)S(1)}, bf16[1,576,128]{2,1,0:T(8,128)(2,1)S(1)}, u32[]{:S(2)}, u32[]{:S(2)}) collective-permute-start(bf16[1,576,128]{2,1,0:T(8,128)(2,1)S(1)} %dynamic-slice_convert_fusion), channel_id=1, source_target_pairs={{0,16},{8,24},{16,0},{24,8},{1,17},{9,25},{17,1},{25,9},{2,18},{10... | collective-permute-start | bytes 442376 | tf_op jit(solution)/shard_map/ppermute | solution.py:1724
  133.6 5.4 %collective-permute-start.22 = (f32[1,96,128]{2,1,0:T(8,128)S(1)}, f32[1,96,128]{2,1,0:T(8,128)S(1)}, u32[]{:S(2)}, u32[]{:S(2)}) collective-permute-start(f32[1,96,128]{2,1,0:T(8,128)S(1)} %get-tuple-element.212), channel_id=1, source_target_pairs={{0,16},{8,24},{16,0},{24,8},{1,17},{9,25},{17,1},{25,9},{2,18},{10... | collective-permute-start | bytes 147464 | tf_op jit(solution)/shard_map/ppermute | solution.py:1724
  141.4 33.4 %all-to-all-start.3 = ((bf16[8,184,128]{2,1,0:T(8,128)(2,1)}), bf16[8,184,128]{2,1,0:T(8,128)(2,1)S(1)}, u32[]{:S(2)}, u32[]{:S(2)}) async-start(bf16[8,184,128]{2,1,0:T(8,128)(2,1)} %get-tuple-element.177), calls=%async_computation.3 | async-start | bytes 753664 | tf_op jit(solution)/shard_map/all_to_all | solution.py:2170
  148.7 12.1 %collective-permute-start.27 = (bf16[2,96,960]{2,1,0:T(8,128)(2,1)}, bf16[2,96,960]{2,1,0:T(8,128)(2,1)S(1)}, u32[]{:S(2)}, u32[]{:S(2)}) collective-permute-start(bf16[2,96,960]{2,1,0:T(8,128)(2,1)} %get-tuple-element.201), channel_id=1, source_target_pairs={{0,1},{1,0},{2,3},{3,2},{4,5},{5,4},{6,7},{7,6},{8,9},{9,8},{10,11... | collective-permute-start | bytes 1105928 | tf_op jit(solution)/shard_map/ppermute | solution.py:1724
  153.2 13.3 %collective-permute-start.17 = (bf16[2,96,768]{2,1,0:T(8,128)(2,1)}, bf16[2,96,768]{2,1,0:T(8,128)(2,1)S(1)}, u32[]{:S(2)}, u32[]{:S(2)}) collective-permute-start(bf16[2,96,768]{2,1,0:T(8,128)(2,1)} %get-tuple-element.162), channel_id=1, source_target_pairs={{0,2},{1,3},{2,0},{3,1},{4,6},{5,7},{6,4},{7,5},{8,10},{9,11},{10,... | collective-permute-start | bytes 884744 | tf_op jit(solution)/shard_map/ppermute | solution.py:1724
  163.7 17.3 %collective-permute-start.28 = (bf16[1,96,960]{2,1,0:T(8,128)(2,1)}, bf16[1,96,960]{2,1,0:T(8,128)(2,1)S(1)}, u32[]{:S(2)}, u32[]{:S(2)}) collective-permute-start(bf16[1,96,960]{2,1,0:T(8,128)(2,1)} %get-tuple-element.203), channel_id=1, source_target_pairs={{0,4},{1,5},{2,6},{3,7},{4,0},{5,1},{6,2},{7,3},{8,12},{9,13},{10,... | collective-permute-start | bytes 552968 | tf_op jit(solution)/shard_map/ppermute | solution.py:1724
  169.1 11.9 %collective-permute-start.18 = (bf16[1,96,768]{2,1,0:T(8,128)(2,1)}, bf16[1,96,768]{2,1,0:T(8,128)(2,1)S(1)}, u32[]{:S(2)}, u32[]{:S(2)}) collective-permute-start(bf16[1,96,768]{2,1,0:T(8,128)(2,1)} %get-tuple-element.163), channel_id=1, source_target_pairs={{0,4},{1,5},{2,6},{3,7},{4,0},{5,1},{6,2},{7,3},{8,12},{9,13},{10,... | collective-permute-start | bytes 442376 | tf_op jit(solution)/shard_map/ppermute | solution.py:1724
  183.8 11.2 %collective-permute-start.30 = (bf16[96,1792]{1,0:T(8,128)(2,1)}, bf16[96,1792]{1,0:T(8,128)(2,1)S(1)}, u32[]{:S(2)}, u32[]{:S(2)}) collective-permute-start(bf16[96,1792]{1,0:T(8,128)(2,1)} %last_fold.1.refs_1_), channel_id=1, source_target_pairs={{0,16},{8,24},{16,0},{24,8},{1,17},{9,25},{17,1},{25,9},{2,18},{10... | collective-permute-start | bytes 1032200 | tf_op jit(solution)/shard_map/ppermute | solution.py:1724
  184.3 13.1 %collective-permute-start.24 = (bf16[880,128]{1,0:T(8,128)(2,1)}, bf16[880,128]{1,0:T(8,128)(2,1)S(1)}, u32[]{:S(2)}, u32[]{:S(2)}) collective-permute-start(bf16[880,128]{1,0:T(8,128)(2,1)} %merge.1.refs_1_), channel_id=1, source_target_pairs={{0,16},{8,24},{16,0},{24,8},{1,17},{9,25},{17,1},{25,9},{2,18},{10... | collective-permute-start | bytes 675848 | tf_op jit(solution)/shard_map/ppermute | solution.py:1724
  185.8 16.7 %collective-permute-start.29 = (bf16[96,1792]{1,0:T(8,128)(2,1)}, bf16[96,1792]{1,0:T(8,128)(2,1)S(1)}, u32[]{:S(2)}, u32[]{:S(2)}) collective-permute-start(bf16[96,1792]{1,0:T(8,128)(2,1)} %last_fold.1.refs_1_), channel_id=1, source_target_pairs={{0,8},{8,0},{16,24},{24,16},{1,9},{9,1},{17,25},{25,17},{2,10},{10... | collective-permute-start | bytes 1032200 | tf_op jit(solution)/shard_map/ppermute | solution.py:1724
  195.0 7.5 %collective-permute-start.31 = (bf16[96,1792]{1,0:T(8,128)(2,1)S(1)}, bf16[96,1792]{1,0:T(8,128)(2,1)S(1)}, u32[]{:S(2)}, u32[]{:S(2)}) collective-permute-start(bf16[96,1792]{1,0:T(8,128)(2,1)S(1)} %collective-permute-done.30.refs_3_), channel_id=1, source_target_pairs={{0,8},{8,0},{16,24},{24,16},{1,9},{9,1},{17,25},{25,17},{2,10},{10... | collective-permute-start | bytes 1032200 | tf_op jit(solution)/shard_map/ppermute | solution.py:1724
  (36 other events, 210.2 us)

commit v3 on v2

--- a/solution.py
+++ b/solution.py
@@ -447,6 +447,7 @@
 BLOCK = 256
 WAVE_BLOCK = 256
 PAD = 8
+CHUNK = 64
 DENSE_LIMIT = 2048
 ROW_AT = {
     "pre_gain": 0,
@@ -526,19 +527,32 @@
     return rows % 8 == 0 and (tokens - rows) * blocks == rows and (tokens - rows) % 8 == 0
 
 
+def split_low(value):
+    high = value.astype(jnp.bfloat16)
+    return high, (value - high.astype(jnp.float32)).astype(jnp.bfloat16)
+
+
+def three_products(dot, left_side, right_side):
+    left_high, left_rest = split_low(left_side)
+    right_high, right_rest = split_low(right_side)
+    return dot(left_high, right_high) + dot(left_high, right_rest) + dot(left_rest, right_high)
+
+
+def fine_nn(left_side, right_side):
+    return three_products(plain_dot, left_side, right_side)
+
+
+def fine_nt(left_side, right_side):
+    return three_products(right_dot, left_side, right_side)
+
+
+def fine_tn(left_side, right_side):
+    return three_products(left_dot, left_side, right_side)
+
+
 def exact_nn(left_side, right_side):
     return jnp.dot(
         left_side, right_side, precision=highest_accuracy, preferred_element_type=jnp.float32
-    )
-
-
-def exact_nt(left_side, right_side):
-    return lax.dot_general(
-        left_side,
-        right_side,
-        (((1,), (1,)), ((), ())),
-        precision=highest_accuracy,
-        preferred_element_type=jnp.float32,
     )
 
 
@@ -792,10 +806,10 @@
         layer_in, times = feature_block(index * BLOCK, BLOCK, length, feat_count)
         for layer, weight in enumerate((pos_weight, inner_weight, third_weight)):
             matrix = doubled(weight[...].astype(f32))
-            inner = exact_nn(layer_in, matrix) + twice(vectors[layer : layer + 1, :])
+            inner = fine_nn(layer_in, matrix) + twice(vectors[layer : layer + 1, :])
             layer_in, cosine = sine_pair(freq * inner)
             waves_out[layer, here, :] = jnp.concatenate([layer_in, cosine], axis=1)
-        both = exact_nn(layer_in, doubled(weights[...]))
+        both = fine_nn(layer_in, doubled(weights[...]))
         cols = 2 * LANES
         for part, rows in enumerate((here, there)):
             kernels = both[:, part * cols : (part + 1) * cols]
@@ -806,7 +820,7 @@
             rest[rows, :] = (kernels - upper.astype(f32)).astype(low)
         return carry
 
-    lax.fori_loop(0, half // BLOCK, network, 0)
+    lax.fori_loop(0, half // BLOCK, network, 0, unroll=True)
     for copy in loads:
         copy.wait()
 
@@ -825,7 +839,7 @@
                 spectrum_out[side, lower, cols] = imag * (1.0 / length)
         return carry
 
-    lax.fori_loop(0, half // WAVE_BLOCK, spectra, 0)
+    lax.fori_loop(0, half // WAVE_BLOCK, spectra, 0, unroll=True)
 
 
 def butterfly(even, odd, turn, upper, lower):
@@ -844,17 +858,17 @@
     return even, (first[0] - second[0], first[1] + second[1])
 
 
-def short_mix(rows, projected, group):
+def short_mix(rows, projected, index, group):
     cols = slice(group * LANES, (group + 1) * LANES)
-    length = projected.shape[1] - PAD
-    now, last = slice(PAD, PAD + length), slice(PAD - 1, PAD - 1 + length)
+    here = pl.ds(pl.multiple_of(index * CHUNK, CHUNK), CHUNK + PAD)
+    even, odd = projected[0, here, cols], projected[1, here, cols]
     taps = [row_of(rows, "taps", 3 * tap + group) for tap in range(3)]
     shift = row_of(rows, "tap_bias", group)
-    odd_last = projected[1, last, cols]
-    even_now = projected[0, now, cols]
-    even = taps[0] * projected[0, last, cols] + taps[1] * odd_last + taps[2] * even_now + shift
-    odd = taps[0] * odd_last + taps[1] * even_now + taps[2] * projected[1, now, cols] + shift
-    return even, odd
+    last = slice(PAD - 1, PAD - 1 + CHUNK)
+    return (
+        taps[0] * even[last] + taps[1] * odd[last] + taps[2] * even[PAD:] + shift,
+        taps[0] * odd[last] + taps[1] * even[PAD:] + taps[2] * odd[PAD:] + shift,
+    )
 
 
 def spread_rows(tile, held, target):
@@ -896,13 +910,13 @@
         store_inverse(reals, imags, block_rows(index, WAVE_BLOCK), 0, parts)
         return carry
 
-    lax.fori_loop(0, half // WAVE_BLOCK, ahead, 0)
+    lax.fori_loop(0, half // WAVE_BLOCK, ahead, 0, unroll=True)
 
     def behind(index, carry):
         finish(block_rows(index, WAVE_BLOCK), inverse_block(wave, reals, imags, index))
         return carry
 
-    lax.fori_loop(0, half // WAVE_BLOCK, behind, 0)
+    lax.fori_loop(0, half // WAVE_BLOCK, behind, 0, unroll=True)
 
 
 def correlate(wave, turn, signal, spectrum, cols, kept, reals, imags, finish):
@@ -923,7 +937,7 @@
             store_inverse(reals, imags, here, 2 * number, parts)
         return carry
 
-    lax.fori_loop(0, half // WAVE_BLOCK, ahead, 0)
+    lax.fori_loop(0, half // WAVE_BLOCK, ahead, 0, unroll=True)
 
     def behind(index, carry):
         both = inverse_block(wave, reals, imags, index)
@@ -931,7 +945,7 @@
         return finish(block_rows(index, WAVE_BLOCK), both[:, :wide], kernel, carry)
 
     zero = jnp.zeros((1, wide), jnp.float32)
-    return lax.fori_loop(0, half // WAVE_BLOCK, behind, zero)
+    return lax.fori_loop(0, half // WAVE_BLOCK, behind, zero, unroll=True)
 
 
 def front_kernel(parts, index, *refs):
@@ -946,6 +960,7 @@
         gated_out,
         product_wave_out,
         gated_wave_out,
+        mixed_out,
         mixer_out,
         held,
         reals,
@@ -956,6 +971,7 @@
         projected,
         product_wave,
         gated_wave,
+        mixed,
         mixer,
         sems,
     ) = refs[5 + parts :]
@@ -977,6 +993,7 @@
                 (projected, projected_out),
                 (product_wave, product_wave_out),
                 (gated_wave, gated_wave_out),
+                (mixed, mixed_out),
             ]
         )
     ]
@@ -996,13 +1013,22 @@
         projected[odd, PAD:, :] = plain_dot(held[block_rows(odd, half), :], weight[...]) + in_bias
         return carry
 
-    lax.fori_loop(0, 2, project, 0)
+    lax.fori_loop(0, 2, project, 0, unroll=True)
     stores[1].start()
-    mixed = [short_mix(rows, projected, group) for group in range(3)]
-    for odd in range(2):
-        cols = slice(odd * LANES, (odd + 1) * LANES)
-        product_out[:, cols] = (mixed[0][odd] * mixed[1][odd]).astype(low)
-        gate_out[:, cols] = mixed[2][odd].astype(low)
+
+    def mix(step, carry):
+        here = block_rows(step, CHUNK)
+        value, gate_one, gate_two = (short_mix(rows, projected, step, group) for group in range(3))
+        for odd in range(2):
+            cols = slice(odd * LANES, (odd + 1) * LANES)
+            mixed[0, here, cols] = value[odd]
+            mixed[1, here, cols] = gate_one[odd]
+            product_out[here, cols] = (value[odd] * gate_one[odd]).astype(low)
+            gate_out[here, cols] = gate_two[odd].astype(low)
+        return carry
+
+    lax.fori_loop(0, half // CHUNK, mix, 0)
+    stores[4].start()
     skips = [twice(row_of(rows, "skips", order)) for order in range(2)]
 
     def first(here, convolved):
@@ -1024,8 +1050,8 @@
     stores[3].start()
     for part in range(parts):
         at = slice(part * count, (part + 1) * count)
-        tiles = [mixer[at, odd * LANES : odd * LANES + channels].astype(f32) for odd in range(2)]
-        mixer_out[part] = dense_rows(jnp.concatenate(tiles, axis=0)).astype(low)
+        tiles = [mixer[at, odd * LANES : odd * LANES + channels] for odd in range(2)]
+        mixer_out[part] = dense_rows(jnp.concatenate(tiles, axis=0))
     for copy in stores:
         copy.wait()
 
@@ -1044,6 +1070,7 @@
     spectrum_in,
     wave_in,
     projected_in,
+    mixed_in,
     packed_out,
     padded_out,
     grad_kernel_out,
@@ -1059,6 +1086,7 @@
     product_wave,
     gated_wave,
     projected,
+    mixed,
     shifted,
     sems,
 ):
@@ -1075,17 +1103,18 @@
                 (gated_wave_in, gated_wave),
                 (product_wave_in, product_wave),
                 (projected_in, projected),
+                (mixed_in, mixed),
             ]
         )
     ]
     for copy in loads:
         copy.start()
-    padding = jnp.zeros((count, LANES - channels), f32)
+    padding = jnp.zeros((count, LANES - channels), low)
     for part in range(parts):
-        tile = loose_rows(grad_mixer[part].astype(f32), 2 * count, channels)
+        tile = loose_rows(grad_mixer[part], 2 * count, channels)
         here = slice(part * count, (part + 1) * count)
         pieces = [tile[:count], padding, tile[count:], padding]
-        grad_mix[here, :] = jnp.concatenate(pieces, axis=1).astype(low)
+        grad_mix[here, :] = jnp.concatenate(pieces, axis=1)
     skips = [twice(row_of(rows, "skips", order)) for order in range(2)]
 
     def store_kernel(here, order, kernel):
@@ -1120,43 +1149,67 @@
     sums_out[15:16, :] = skip_first[:, :LANES] + skip_first[:, LANES:]
     sums_out[16:17, :] = skip_second[:, :LANES] + skip_second[:, LANES:]
     sums_out[17:24, :] = jnp.zeros((7, LANES), f32)
-    loads[4].wait()
-    now, last, after = slice(PAD, PAD + half), slice(PAD - 1, PAD - 1 + half), slice(1, 1 + half)
-
-    def total(value):
-        return jnp.sum(value, axis=0, keepdims=True)
-
-    shifted[:, half:, :] = jnp.zeros((2, PAD, LANES), f32)
-    for group in range(3):
-        here = slice(group * LANES, (group + 1) * LANES)
-        sides = [slice(odd * LANES, (odd + 1) * LANES) for odd in range(2)]
-        if group == 2:
-            mixed = [grad_gate[:, side].astype(f32) for side in sides]
-        else:
-            others = short_mix(rows, projected, 1 - group)
-            mixed = [grad_value[:, side].astype(f32) * other for side, other in zip(sides, others)]
-        shifted[0, :half, :], shifted[1, :half, :] = mixed
-        even, odd = mixed
-        taps = [row_of(rows, "taps", 3 * tap + group) for tap in range(3)]
-        odd_last, even_now = projected[1, last, here], projected[0, now, here]
-        moved = (
-            total(even * projected[0, last, here] + odd * odd_last),
-            total(even * odd_last + odd * even_now),
-            total(even * even_now + odd * projected[1, now, here]),
-        )
-        for tap in range(3):
-            at = 3 * tap + group
-            sums_out[at : at + 1, :] = moved[tap]
-        sums_out[9 + group : 10 + group, :] = total(even + odd)
-        even_next, odd_next = shifted[0, after, :], shifted[1, after, :]
-        grads = (
-            taps[0] * even_next + taps[1] * odd + taps[2] * even,
-            taps[0] * odd_next + taps[1] * even_next + taps[2] * odd,
-        )
-        grads = [grad.astype(low) for grad in grads]
-        for place, grad in enumerate(grads):
-            padded_out[place * half : (place + 1) * half, here] = grad
-        sums_out[12 + group : 13 + group, :] = total(grads[0].astype(f32) + grads[1].astype(f32))
+    for copy in loads[4:]:
+        copy.wait()
+    shifted[:, :, half:, :] = jnp.zeros((3, 2, PAD, LANES), f32)
+    sides = [slice(odd * LANES, (odd + 1) * LANES) for odd in range(2)]
+
+    def folded(value):
+        return jnp.sum(value.reshape(CHUNK // 8, 8, LANES), axis=0)
+
+    def taps_back(step, totals):
+        here = block_rows(step, CHUNK)
+        window = pl.ds(pl.multiple_of(step * CHUNK, CHUNK), CHUNK + PAD)
+        last = slice(PAD - 1, PAD - 1 + CHUNK)
+        totals = list(totals)
+        for group in range(3):
+            cols = slice(group * LANES, (group + 1) * LANES)
+            if group == 2:
+                even, odd = (grad_gate[here, side].astype(f32) for side in sides)
+            else:
+                even, odd = (
+                    grad_value[here, side].astype(f32) * mixed[1 - group, here, side]
+                    for side in sides
+                )
+            shifted[group, 0, here, :], shifted[group, 1, here, :] = even, odd
+            even_rows, odd_rows = projected[0, window, cols], projected[1, window, cols]
+            terms = (
+                even * even_rows[last] + odd * odd_rows[last],
+                even * odd_rows[last] + odd * even_rows[PAD:],
+                even * even_rows[PAD:] + odd * odd_rows[PAD:],
+                even + odd,
+            )
+            for number, term in enumerate(terms):
+                totals[3 * number + group] = totals[3 * number + group] + folded(term)
+        return tuple(totals)
+
+    zero = jnp.zeros((8, LANES), f32)
+    totals = lax.fori_loop(0, half // CHUNK, taps_back, (zero,) * 12)
+
+    def project_back(step, totals):
+        window = pl.ds(pl.multiple_of(step * CHUNK, CHUNK), CHUNK + PAD)
+        following = slice(1, 1 + CHUNK)
+        totals = list(totals)
+        for group in range(3):
+            cols = slice(group * LANES, (group + 1) * LANES)
+            even, odd = shifted[group, 0, window, :], shifted[group, 1, window, :]
+            taps = [row_of(rows, "taps", 3 * tap + group) for tap in range(3)]
+            now = slice(0, CHUNK)
+            grads = (
+                taps[0] * even[following] + taps[1] * odd[now] + taps[2] * even[now],
+                taps[0] * odd[following] + taps[1] * even[following] + taps[2] * odd[now],
+            )
+            grads = [grad.astype(low) for grad in grads]
+            for place, grad in enumerate(grads):
+                at = pl.ds(pl.multiple_of(place * half + step * CHUNK, CHUNK), CHUNK)
+                padded_out[at, cols] = grad
+            wide = grads[0].astype(f32) + grads[1].astype(f32)
+            totals[group] = totals[group] + folded(wide)
+        return tuple(totals)
+
+    totals = totals + lax.fori_loop(0, half // CHUNK, project_back, (zero,) * 3)
+    for number, value in enumerate(totals):
+        sums_out[number : number + 1, :] = jnp.sum(value, axis=0, keepdims=True)
     dense = packed_out.shape[1] // 3
 
     def pack(part, carry):
@@ -1165,10 +1218,10 @@
             tiles = [
                 padded_out[
                     pl.ds(pl.multiple_of(odd * half + part * count, count), count), cols
-                ].astype(f32)
+                ]
                 for odd in range(2)
             ]
-            packed = dense_rows(jnp.concatenate(tiles, axis=0)).astype(low)
+            packed = dense_rows(jnp.concatenate(tiles, axis=0))
             packed_out[part, group * dense : (group + 1) * dense, :] = packed
         return carry
 
@@ -1246,9 +1299,9 @@
         for copy in loads(place):
             copy.start()
     tiles = [
-        loose_rows(received[part].astype(f32), tok_count, channels) for part in range(parts)
+        loose_rows(received[part], tok_count, channels) for part in range(parts)
     ]
-    mixer = jnp.concatenate(tiles, axis=1).astype(low)
+    mixer = jnp.concatenate(tiles, axis=1)
     load_out.wait()
     branch = plain_dot(mixer, out_w[...]) + row_of(rows, "out_bias")
     residual[...] = tokens[...].astype(f32) + branch
@@ -1277,17 +1330,17 @@
         flow[...] += right_dot(grad_upper, up_w[place])
         return carry
 
-    lax.fori_loop(0, quarters, body, 0)
+    lax.fori_loop(0, quarters, body, 0, unroll=2)
     spread_rows(residual[...] + total[...] + row_of(rows, "down_bias"), held, outputs_out)
     _, unit, inv_std = norm_forward(residual[...], gain, bias)
     grad_norm, grad_gain, grad_bias = norm_backward(flow[...], unit, inv_std, gain)
     grad_residual = top[...].astype(f32) + grad_norm
     residual_out[...] = grad_residual
     grad_branch = grad_residual.astype(low)
-    grad_mixer = right_dot(grad_branch, out_w[...])
+    grad_mixer = right_dot(grad_branch, out_w[...]).astype(low)
     for part in range(parts):
         tile = grad_mixer[:, part * channels : (part + 1) * channels]
-        send_out[part] = dense_rows(tile).astype(low)
+        send_out[part] = dense_rows(tile)
     wide_branch = grad_branch.astype(f32)
     vectors = [
         jnp.sum(wide_branch, axis=0, keepdims=True),
@@ -1314,8 +1367,8 @@
         for part in range(parts):
             at = part * per_part + place * step
             inside = at % quarter
-            tiles.append(act[at // quarter, :, inside : inside + step].astype(f32))
-        act_parts[place] = jnp.concatenate(tiles, axis=1).astype(low)
+            tiles.append(act[at // quarter, :, inside : inside + step])
+        act_parts[place] = jnp.concatenate(tiles, axis=1)
     for bits in range(batch):
         place = batch_index[0] ^ bits
         parts_out[bits][:, :quarter] = upper_grad[place]
@@ -1336,7 +1389,7 @@
 
 
 def flip(tile):
-    return tile.astype(jnp.float32).T.astype(jnp.bfloat16)
+    return tile.T
 
 
 def weight_kernel(batch, orders, index, *refs):
@@ -1396,13 +1449,13 @@
     for group in range(3):
         tiles = [
             loose_rows(
-                received[part, group * dense : (group + 1) * dense, :].astype(f32),
+                received[part, group * dense : (group + 1) * dense, :],
                 tok_count,
                 channels,
             )
             for part in range(parts)
         ]
-        joined[:, group * width : (group + 1) * width] = jnp.concatenate(tiles, axis=1).astype(low)
+        joined[:, group * width : (group + 1) * width] = jnp.concatenate(tiles, axis=1)
     gain = row_of(rows, "pre_gain")
     bias = row_of(rows, "pre_bias")
     _, unit, inv_std = norm_forward(tokens[...].astype(f32), gain, bias)
@@ -1494,21 +1547,21 @@
             rate_total[...] = rate_total[...] - decayed
             windowed.append(grads * jnp.exp(-rates[...] * time))
         windowed = jnp.concatenate(windowed, axis=1)
-        weight_total[...] = weight_total[...] + exact_tdot(waves[2, here, :LANES], windowed)
-        flow = exact_nt(windowed, weight_pair)
+        weight_total[...] = weight_total[...] + fine_tn(waves[2, here, :LANES], windowed)
+        flow = fine_nt(windowed, weight_pair)
         for layer in (2, 1, 0):
             slope = flow * waves[layer, here, LANES:]
             below = waves[layer - 1, here, :LANES] if layer else features
             count = below.shape[1]
-            pairs[layer, :count, :] = pairs[layer, :count, :] + exact_tdot(below, slope)
+            pairs[layer, :count, :] = pairs[layer, :count, :] + fine_tn(below, slope)
             row = slice(LANES, LANES + 1)
             pairs[layer, row, :] = pairs[layer, row, :] + jnp.sum(slope, axis=0, keepdims=True)
             if layer:
                 weight = inner_weight if layer == 1 else third_weight
-                flow = exact_nt(slope * freq_pair, doubled(weight[...].astype(f32)))
+                flow = fine_nt(slope * freq_pair, doubled(weight[...].astype(f32)))
         return carry
 
-    lax.fori_loop(0, blocks // 2, body, 0)
+    lax.fori_loop(0, blocks // 2, body, 0, unroll=True)
     grad_freq = jnp.zeros_like(freq)
     at, bias_at = 0, 2 * fhid + feat_count
     for layer, weight in ((2, third_weight), (1, inner_weight), (0, pos_weight)):
@@ -1524,11 +1577,12 @@
     shared[bias_at + 3 : bias_at + 4, :] = grad_freq
     pair_load.wait()
     small_out[...] = jnp.zeros_like(small_out)
-    ones = jnp.ones((8, in_local.shape[1]), f32)
-    in_wide = in_local[...].astype(f32)
-    gain = exact_nt(ones, in_wide * pair_sums[...])[0:1]
+    ones = jnp.ones((16, in_local.shape[1]), jnp.bfloat16)
+    high, rest = split_low(in_local[...].astype(f32) * pair_sums[...])
+    gain = (right_dot(ones, high) + right_dot(ones, rest))[0:1]
     column_sums = jnp.concatenate([sums[12 + group : 13 + group, :] for group in range(3)], axis=1)
-    bias = exact_nt(jnp.broadcast_to(column_sums, ones.shape), in_wide)[0:1]
+    high, rest = split_low(jnp.broadcast_to(column_sums, ones.shape))
+    bias = (right_dot(high, in_local[...]) + right_dot(rest, in_local[...]))[0:1]
     everywhere = small_out.at[:, :SHARED_ROWS, :]
     per = width // LANES
     gain = (gain - row_of(norm_rows, "pre_bias") * bias) / row_of(norm_rows, "pre_gain")
@@ -1762,11 +1816,6 @@
         total = keep + got.astype(jnp.float32)
         left.remove(bits)
     return total[0]
-
-
-def split_low(value):
-    high = value.astype(jnp.bfloat16)
-    return high, (value - high.astype(jnp.float32)).astype(jnp.bfloat16)
 
 
 def dense_device(
@@ -1907,9 +1956,6 @@
         ],
         name="filters",
     )
-    tops = over_batch(grad_top)
-    spectrum, *tops = lax.optimization_barrier((spectrum, *tops))
-
     dense = tok_count * channels // LANES
     (
         normed,
@@ -1920,6 +1966,7 @@
         gated,
         product_wave,
         gated_wave,
+        mixed,
         mixer_chan,
     ) = call_kernel(
         lambda *refs: front_kernel(seq_parts, *refs),
@@ -1932,13 +1979,14 @@
             ((half, 2 * LANES), low),
             ((2, length, LANES), f32),
             ((2, length, LANES), f32),
+            ((2, half, 2 * LANES), f32),
             ((seq_parts, dense, LANES), low),
         ],
         [seq_scalar]
         + [chunks[part] for part in range(seq_parts)]
         + [in_local, rows_local, wave, turn, spectrum],
         micros=13,
-        spaces="s" + "v" * seq_parts + "vvhhh" + "hhvvvvhhv",
+        spaces="s" + "v" * seq_parts + "vvhhh" + "hhvvvvhhhv",
         scratch=[
             ((length, width), low),
             ((half, 2 * LANES), low),
@@ -1949,12 +1997,15 @@
             ((2, PAD + half, wide), f32),
             ((2, length, LANES), f32),
             ((2, length, LANES), f32),
+            ((2, half, 2 * LANES), f32),
             ((half, 2 * LANES), low),
-            7,
+            8,
         ],
         name="front",
     )
+    tops = over_batch(grad_top)
     mixer_back = lax.all_to_all(mixer_chan, "seq", 0, 0, tiled=True)
+    mixer_back, *tops = lax.optimization_barrier((mixer_back, *tops))
 
     quarter = hidden_units // batch_parts
     branch_quarter = width // batch_parts
@@ -2047,9 +2098,10 @@
             spectrum,
             wave,
             projected,
+            mixed,
         ],
         micros=15,
-        spaces="v" * 7 + "h" * 5 + "vvvv",
+        spaces="v" * 7 + "h" * 6 + "vvvv",
         scratch=[((half, 2 * LANES), low)] * 4
         + [
             ((half, 4 * LANES), low),
@@ -2059,8 +2111,9 @@
             ((2, length, LANES), f32),
             ((2, length, LANES), f32),
             ((2, PAD + half, wide), f32),
-            ((2, half + PAD, LANES), f32),
-            5,
+            ((2, half, 2 * LANES), f32),
+            ((3, 2, half + PAD, LANES), f32),
+            6,
         ],
         name="back",
     )
@@ -2203,19 +2256,6 @@
         [up_keep, up_got, rest_keep, rest_got],
         micros=1,
         name="last_fold",
-    )
-    final_down, final_up, final_out = call_kernel(
-        lambda *refs: collect_kernel(batch_parts, *refs),
-        [
-            ((batch_parts * rows_each, width), f32),
-            ((rows_each, hidden_units), f32),
-            ((rows_each, width), f32),
-        ],
-        [batch_scalar] + over_batch(weights_done),
-        micros=3,
-        spaces="s" + "v" * (batch_parts + 3),
-        scratch=[((batch_parts, rows_each, total), low)],
-        name="collect",
     )
     (
         final_in,
@@ -2273,6 +2313,30 @@
         ],
         name="finish",
     )
+    entries = {0: weights_done, batch_parts // 2: swapped(weights_done, "batch", batch_parts // 2)}
+    entries[batch_parts // 2], final_in = lax.optimization_barrier(
+        (entries[batch_parts // 2], final_in)
+    )
+    bits = batch_parts // 4
+    while bits:
+        entries.update(
+            {place ^ bits: swapped(member, "batch", bits) for place, member in entries.items()}
+        )
+        bits //= 2
+    entries = [entries[place] for place in range(batch_parts)]
+    final_down, final_up, final_out = call_kernel(
+        lambda *refs: collect_kernel(batch_parts, *refs),
+        [
+            ((batch_parts * rows_each, width), f32),
+            ((rows_each, hidden_units), f32),
+            ((rows_each, width), f32),
+        ],
+        [batch_scalar] + entries,
+        micros=3,
+        spaces="s" + "v" * (batch_parts + 3),
+        scratch=[((batch_parts, rows_each, total), low)],
+        name="collect",
+    )
     return (
         outputs[None],
         grad_inputs[None],

time: 208 us -> 192 us (0.923)
  waiting for transfers between devices: 49.4 us -> 40.3 us
  Pallas kernels: 91.7 us -> 84.3 us
    ppermute x32, waiting for transfers between devices: 36.3 us -> 28.8 us  [swapped(): lax.ppermute(value, axis, [(source, source ^ bits) for source in range(co...]
    pallas_call x18, Pallas kernels: 91.7 us -> 84.3 us  [call_kernel(): pl.pallas_call(kernel, out_shape=shapes, in_specs=specs[:len(args)], out_...]
    unnamed x64 -> x66, local copies, waits for them, and re-layouts: 8.61 us -> 8.28 us
  transfers between devices with their start and end apart: 36 -> 36, of which waited for: 12 -> 15; matrix products, arithmetic and copies ran while one was open for 4% -> 4% of each run, Pallas kernels for 31% -> 36%
where the time goes in v3:
time: 192 us; the launch traced here: 191 us
  Pallas kernels  84.3 us (44%)
  starting transfers between devices  48.8 us (25%)
  waiting for transfers between devices  40.3 us (21%)
  local copies, waits for them, and re-layouts  12.4 us (6%)
  matrix products  2.13 us (1%)
    pallas_call x18, Pallas kernels, call_kernel(): pl.pallas_call(kernel, out_shape=shapes, in_specs=specs[:len(args)], out_...  84.3 us
    ppermute x32, starting transfers between devices, swapped(): lax.ppermute(value, axis, [(source, source ^ bits) for source in range(co...  30 us
    ppermute x32, waiting for transfers between devices, swapped(): lax.ppermute(value, axis, [(source, source ^ bits) for source in range(co...  28.8 us
    unnamed x66, local copies, waits for them, and re-layouts  8.28 us
    all_to_all x1, starting transfers between devices, dense_device(): mixer_back = lax.all_to_all(mixer_chan, 'seq', 0, 0, tiled=True)  7.93 us
    all_to_all x1, waiting for transfers between devices, dense_device(): mixer_back = lax.all_to_all(mixer_chan, 'seq', 0, 0, tiled=True)  6.06 us
    all_to_all x1, waiting for transfers between devices, dense_device(): grad_mixer_chan = lax.all_to_all(grad_mixer, 'seq', 0, 0, tiled=True)  5.43 us
  transfers between devices with their start and end apart: 36, of which 15 were waited for; matrix products, arithmetic and copies ran while one was open for 4% of the time, Pallas kernels for 36%

profile of v3, /device:TPU:0, one launch (start us, length us, event | category | flops | bytes accessed | tf_op | source)
XLA Modules:
  0.0 190.6 jit_solution(13040526176924901056)
XLA Ops:
  0.7 2.1 %norm.1 = (bf16[128,768]{1,0:T(8,128)(2,1)}, bf16[128,768]{1,0:T(8,128)(2,1)}, bf16[128,768]{1,0:T(8,128)(2,1)}) custom-call(bf16[128,768]{1,0:T(8,128)(2,1)} %bitcast.46, bf16[128,768]{1,0:T(8,128)(2,1)} %bitcast.47, bf16[768]{0:T(1024)(128)(2,1)} %refs_1_.1, bf16[768]{0:T(1024)(128)(2,1)} %refs_2_.1), custom_call_target="tpu_custom_call" | custom-call | flops 1 | bytes 3000000 | tf_op jit(solution)/shard_map/norm/pallas_call | solution.py:473
  2.7 3.0 %collective-permute-start.1 = (bf16[128,768]{1,0:T(8,128)(2,1)}, bf16[128,768]{1,0:T(8,128)(2,1)S(1)}, u32[]{:S(2)}, u32[]{:S(2)}) collective-permute-start(bf16[128,768]{1,0:T(8,128)(2,1)} %get-tuple-element.122.refs_1_), channel_id=1, source_target_pairs={{0,2},{1,3},{2,0},{3,1},{4,6},{5,7},{6,4},{7,5},{8,10},{9,11},{10,... | collective-permute-start | bytes 589832 | tf_op jit(solution)/shard_map/ppermute | solution.py:1778
  5.7 2.6 %collective-permute-start.2 = (bf16[128,768]{1,0:T(8,128)(2,1)}, bf16[128,768]{1,0:T(8,128)(2,1)S(1)}, u32[]{:S(2)}, u32[]{:S(2)}) collective-permute-start(bf16[128,768]{1,0:T(8,128)(2,1)} %get-tuple-element.122.refs_1_), channel_id=1, source_target_pairs={{0,4},{1,5},{2,6},{3,7},{4,0},{5,1},{6,2},{7,3},{8,12},{9,13},{10,... | collective-permute-start | bytes 589832 | tf_op jit(solution)/shard_map/ppermute | solution.py:1778
  10.1 5.6 %waves.1 = (bf16[1024,512]{1,0:T(8,128)(2,1)}, f32[1024,128]{1,0:T(8,128)}, f32[32,768]{1,0:T(8,128)}, bf16[768,384]{1,0:T(8,128)(2,1)}, f32[32,128]{1,0:T(8,128...) custom-call(s32[1]{0:T(128)} %bitcast.4.refs_0_, bf16[768]{0:T(1024)(128)(2,1)} %refs_1_.1, ...), custom_call_target="tpu_custom_call" | custom-call | flops 1 | bytes 25500000 | tf_op jit(solution)/shard_map/waves/pallas_call | solution.py:473
  15.8 7.4 %collective-permute-done.2.refs_5_ = bf16[128,768]{1,0:T(8,128)(2,1)S(1)} collective-permute-done((bf16[128,768]{1,0:T(8,128)(2,1)}, bf16[128,768]{1,0:T(8,128)(2,1)S(1)}, u32[]{:S(2)}, u32[]{:S(2)}) %collective-permute-start.2) | collective-permute-done | bytes 196640 | tf_op jit(solution)/shard_map/ppermute | solution.py:1778
  28.2 6.5 %filters.1 = (f32[2,1024,256]{2,1,0:T(8,128)}, f32[1024,256]{1,0:T(8,128)}, f32[3,512,256]{2,1,0:T(8,128)}) custom-call(bf16[33,64]{1,0:T(8,128)(2,1)} %pos_weight.3, bf16[64,64]{1,0:T(8,128)(2,1)} %inner_weight.3, bf16[64,64]{1,0:T(8,128)(2,1)} %third_weight.3, f32[4,64]{1,0:T(4,128)} %get-tuple-element.131.vectors, f32[64,256]{1,0:T(8,128)} %get-tuple-element.132.weights, ...), custom_call_target="tpu_custom_call" | custom-call | flops 1 | bytes 39000000 | tf_op jit(solution)/shard_map/filters/pallas_call | solution.py:473
  36.4 9.3 %front.1 = (bf16[1024,768]{1,0:T(8,128)(2,1)}, f32[2,520,384]{2,1,0:T(8,128)}, bf16[512,256]{1,0:T(8,128)(2,1)}, bf16[512,256]{1,0:T(8,128)(2,1)}, bf16[512,256]...) custom-call(s32[1]{0:T(128)} %bitcast.1.refs_0_, ...), custom_call_target="tpu_custom_call" | custom-call | flops 1 | bytes 39000000 | tf_op jit(solution)/shard_map/front/pallas_call | solution.py:473
  45.7 7.9 %all-to-all-start = ((bf16[8,96,128]{2,1,0:T(8,128)(2,1)}), bf16[8,96,128]{2,1,0:T(8,128)(2,1)S(1)}, u32[]{:S(2)}, u32[]{:S(2)}) async-start(bf16[8,96,128]{2,1,0:T(8,128)(2,1)} %get-tuple-element.135), calls=%async_computation | async-start | bytes 393216 | tf_op jit(solution)/shard_map/all_to_all | solution.py:2007
  55.3 6.1 %all-to-all-done.refs_1_ = bf16[8,96,128]{2,1,0:T(8,128)(2,1)S(1)} async-done(((bf16[8,96,128]{2,1,0:T(8,128)(2,1)}), bf16[8,96,128]{2,1,0:T(8,128)(2,1)S(1)}, u32[]{:S(2)}, u32[]{:S(2)}) %all-to-all-start) | async-done | bytes 196640 | tf_op jit(solution)/shard_map/all_to_all | solution.py:2007
  62.1 10.8 %middle.1 = (f32[128,768]{1,0:T(8,128)}, f32[128,768]{1,0:T(8,128)}, bf16[8,96,128]{2,1,0:T(8,128)(2,1)}, f32[48,128]{1,0:T(8,128)}, bf16[128,1536]{1,0:T(8,128)...) custom-call(s32[1]{0:T(128)} %bitcast.refs_0_, ...), custom_call_target="tpu_custom_call" | custom-call | flops 1 | bytes 33000000 | tf_op jit(solution)/shard_map/middle/pallas_call | solution.py:473
  74.4 3.4 %all-to-all-start.1 = ((bf16[8,96,128]{2,1,0:T(8,128)(2,1)}), bf16[8,96,128]{2,1,0:T(8,128)(2,1)S(1)}, u32[]{:S(2)}, u32[]{:S(2)}) async-start(bf16[8,96,128]{2,1,0:T(8,128)(2,1)} %get-tuple-element.142), calls=%async_computation.1 | async-start | bytes 393216 | tf_op jit(solution)/shard_map/all_to_all | solution.py:2074
  80.1 5.4 %all-to-all-done.1.refs_0_ = bf16[8,96,128]{2,1,0:T(8,128)(2,1)S(1)} async-done(((bf16[8,96,128]{2,1,0:T(8,128)(2,1)}), bf16[8,96,128]{2,1,0:T(8,128)(2,1)S(1)}, u32[]{:S(2)}, u32[]{:S(2)}) %all-to-all-start.1) | async-done | bytes 196640 | tf_op jit(solution)/shard_map/all_to_all | solution.py:2074
  86.2 11.3 %back.1 = (bf16[8,288,128]{2,1,0:T(8,128)(2,1)}, bf16[1024,384]{1,0:T(8,128)(2,1)}, f32[2,512,256]{2,1,0:T(8,128)}, f32[24,128]{1,0:T(8,128)}) custom-call(bf16[8,96,128]{2,1,0:T(8,128)(2,1)} %copy-done.8, bf16[512,256]{1,0:T(8,128)(2,1)} %get-tuple-element.143.refs_1_, bf16[512,256]{1,0:T(8,128)(2,1)} %get-tuple-element.144.refs_2_, ...), custom_call_target="tpu_custom_call" | custom-call | flops 1 | bytes 45000000 | tf_op jit(solution)/shard_map/back/pallas_call | solution.py:473
  97.5 3.8 %all-to-all-start.2 = ((bf16[8,288,128]{2,1,0:T(8,128)(2,1)}), bf16[8,288,128]{2,1,0:T(8,128)(2,1)S(1)}, u32[]{:S(2)}, u32[]{:S(2)}) async-start(bf16[8,288,128]{2,1,0:T(8,128)(2,1)} %get-tuple-element.175), calls=%async_computation.2 | async-start | bytes 1179648 | tf_op jit(solution)/shard_map/all_to_all | solution.py:2120
  102.0 2.1 %fusion.1.pair_in = f32[768,384]{1,0:T(8,128)S(1)} fusion(bf16[1024,768]{1,0:T(8,128)(2,1)S(1)} %copy-done.32, bf16[1024,384]{1,0:T(8,128)(2,1)} %get-tuple-element.151), kind=kOutput, calls=%fused_computation.10 | convolution fusion | flops 603979776 | bytes 3538944 | tf_op jit(solution)/shard_map/dot_general | solution.py:36
  105.8 5.5 %weights.1 = (f32[4,96,768]{2,1,0:T(8,128)}, bf16[4,96,768]{2,1,0:T(8,128)(2,1)}, f32[4,96,960]{2,1,0:T(8,128)}, bf16[4,96,960]{2,1,0:T(8,128)(2,1)}) custom-call(s32[2]{0:T(128)} %pad_add_fusion.refs_0_, bf16[128,1536]{1,0:T(8,128)(2,1)} %get-tuple-element.152.refs_1_, bf16[128,1536]{1,0:T(8,128)(2,1)} %collective-permute-done.10.refs_2_, ...), custom_call_target="tpu_custom_call" | custom-call | flops 1 | bytes 18000000 | tf_op jit(solution)/shard_map/weights/pallas_call | solution.py:473
  115.0 7.2 %chain.1 = f32[4,96,128]{2,1,0:T(8,128)} custom-call(f32[32,768]{1,0:T(8,128)} %get-tuple-element.139.refs_4_.norm_rows.rows, bf16[768,384]{1,0:T(8,128)(2,1)} %get-tuple-element.127.refs_9_.in_local, f32[24,128]{1,0:T(8,128)} %get-tuple-element.169.sums, f32[48,128]{1,0:T(8,128)} %get-tuple-element.170.middle_sums, bf16[33,64]{1,0:T(8,128)(2,1)} %pos_weight.3, ...), custom_call_target="tpu_custom_call" | custom-call | flops 1 | bytes 36000000 | tf_op jit(solution)/shard_map/chain/pallas_call | solution.py:473
  127.9 3.2 %collective-permute-done.20 = bf16[1,576,128]{2,1,0:T(8,128)(2,1)S(1)} collective-permute-done((bf16[1,576,128]{2,1,0:T(8,128)(2,1)S(1)}, bf16[1,576,128]{2,1,0:T(8,128)(2,1)S(1)}, u32[]{:S(2)}, u32[]{:S(2)}) %collective-permute-start.20) | collective-permute-done | bytes 147488 | tf_op jit(solution)/shard_map/ppermute | solution.py:1778
  134.2 3.7 %all-to-all-start.3 = ((bf16[8,184,128]{2,1,0:T(8,128)(2,1)}), bf16[8,184,128]{2,1,0:T(8,128)(2,1)S(1)}, u32[]{:S(2)}, u32[]{:S(2)}) async-start(bf16[8,184,128]{2,1,0:T(8,128)(2,1)} %get-tuple-element.181), calls=%async_computation.3 | async-start | bytes 753664 | tf_op jit(solution)/shard_map/all_to_all | solution.py:2223
  138.8 2.7 %fold.6 = (f32[2,96,960]{2,1,0:T(8,128)}, bf16[2,96,960]{2,1,0:T(8,128)(2,1)}) custom-call(s32[1]{0:T(128)} %bitcast.10.refs_0_, f32[4,96,960]{2,1,0:T(8,128)} %get-tuple-element.188.refs_1_, bf16[4,96,960]{2,1,0:T(8,128)(2,1)} %copy-done.6), custom_call_target="tpu_custom_call" | custom-call | flops 1 | bytes 3000000 | tf_op jit(solution)/shard_map/fold/pallas_call | solution.py:473
  141.5 2.0 %collective-permute-start.27 = (bf16[2,96,960]{2,1,0:T(8,128)(2,1)}, bf16[2,96,960]{2,1,0:T(8,128)(2,1)S(1)}, u32[]{:S(2)}, u32[]{:S(2)}) collective-permute-start(bf16[2,96,960]{2,1,0:T(8,128)(2,1)} %get-tuple-element.191), channel_id=1, source_target_pairs={{0,1},{1,0},{2,3},{3,2},{4,5},{5,4},{6,7},{7,6},{8,9},{9,8},{10,11... | collective-permute-start | bytes 1105928 | tf_op jit(solution)/shard_map/ppermute | solution.py:1778
  143.5 2.4 %fold.4 = (f32[2,96,768]{2,1,0:T(8,128)}, bf16[2,96,768]{2,1,0:T(8,128)(2,1)}) custom-call(s32[1]{0:T(128)} %bitcast.7.refs_0_, f32[4,96,768]{2,1,0:T(8,128)} %get-tuple-element.163.refs_1_, bf16[4,96,768]{2,1,0:T(8,128)(2,1)} %collective-permute-done.16.refs_2_), custom_call_target="tpu_custom_call" | custom-call | flops 1 | bytes 3000000 | tf_op jit(solution)/shard_map/fold/pallas_call | solution.py:473
  147.4 6.2 %collective-permute-done.27.refs_2_ = bf16[2,96,960]{2,1,0:T(8,128)(2,1)S(1)} collective-permute-done((bf16[2,96,960]{2,1,0:T(8,128)(2,1)}, bf16[2,96,960]{2,1,0:T(8,128)(2,1)S(1)}, u32[]{:S(2)}, u32[]{:S(2)}) %collective-permute-start.27) | collective-permute-done | bytes 368672 | tf_op jit(solution)/shard_map/ppermute | solution.py:1778
  154.3 2.1 %fold.7 = (f32[1,96,960]{2,1,0:T(8,128)}, bf16[1,96,960]{2,1,0:T(8,128)(2,1)}) custom-call(s32[1]{0:T(128)} %bitcast.6.refs_0_, f32[2,96,960]{2,1,0:T(8,128)} %get-tuple-element.190.refs_1_, bf16[2,96,960]{2,1,0:T(8,128)(2,1)} %copy-done.10), custom_call_target="tpu_custom_call" | custom-call | flops 1 | bytes 3000000 | tf_op jit(solution)/shard_map/fold/pallas_call | solution.py:473
  156.4 2.7 %collective-permute-start.28 = (bf16[1,96,960]{2,1,0:T(8,128)(2,1)}, bf16[1,96,960]{2,1,0:T(8,128)(2,1)S(1)}, u32[]{:S(2)}, u32[]{:S(2)}) collective-permute-start(bf16[1,96,960]{2,1,0:T(8,128)(2,1)} %get-tuple-element.193), channel_id=1, source_target_pairs={{0,4},{1,5},{2,6},{3,7},{4,0},{5,1},{6,2},{7,3},{8,12},{9,13},{10,... | collective-permute-start | bytes 552968 | tf_op jit(solution)/shard_map/ppermute | solution.py:1778
  159.9 1.9 %fold.5 = (f32[1,96,768]{2,1,0:T(8,128)}, bf16[1,96,768]{2,1,0:T(8,128)(2,1)}) custom-call(s32[1]{0:T(128)} %bitcast.6.refs_0_, f32[2,96,768]{2,1,0:T(8,128)} %get-tuple-element.165.refs_1_, bf16[2,96,768]{2,1,0:T(8,128)(2,1)} %copy-done.14), custom_call_target="tpu_custom_call" | custom-call | flops 1 | bytes 3000000 | tf_op jit(solution)/shard_map/fold/pallas_call | solution.py:473
  165.1 5.5 %final.1 = f32[128,768]{1,0:T(8,128)} custom-call(bf16[8,288,128]{2,1,0:T(8,128)(2,1)} %copy-done.2, bf16[128,768]{1,0:T(8,128)(2,1)} %get-tuple-element.138.refs_2_.tokens, f32[128,768]{1,0:T(8,128)} %get-tuple-element.180.residual, f32[32,768]{1,0:T(8,128)} %get-tuple-element.139.refs_4_.norm_rows.rows, bf16[768,2304]{1,0:T(8,128)(2,1)} %weight_in.1), custom_call_target="tpu_custom_call" | custom-call | flops 1 | bytes 16500000 | tf_op jit(solution)/shard_map/final/pallas_call | solution.py:473
  170.6 3.1 %collective-permute-done.18.up_got = bf16[1,96,768]{2,1,0:T(8,128)(2,1)S(1)} collective-permute-done((bf16[1,96,768]{2,1,0:T(8,128)(2,1)}, bf16[1,96,768]{2,1,0:T(8,128)(2,1)S(1)}, u32[]{:S(2)}, u32[]{:S(2)}) %collective-permute-start.18) | collective-permute-done | bytes 147488 | tf_op jit(solution)/shard_map/ppermute | solution.py:1778
  174.5 2.0 %last_fold.1.refs_1_ = bf16[96,1792]{1,0:T(8,128)(2,1)} custom-call(f32[1,96,768]{2,1,0:T(8,128)} %get-tuple-element.186.up_keep, bf16[1,96,768]{2,1,0:T(8,128)(2,1)} %copy-done.30, f32[1,96,960]{2,1,0:T(8,128)} %get-tuple-element.192.rest_keep, bf16[1,96,960]{2,1,0:T(8,128)(2,1)} %copy-done.28), custom_call_target="tpu_custom_call" | custom-call | flops 1 | bytes 3000000 | tf_op jit(solution)/shard_map/last_fold/pallas_call | solution.py:473
  179.9 2.9 %finish.1 = (f32[96,2304]{1,0:T(8,128)}, f32[768]{0:T(1024)}, f32[768]{0:T(1024)}, f32[768]{0:T(1024)}, f32[768]{0:T(1024)}, /*index=5*/f32[768]{0:T(1024)}, f32...) custom-call(s32[1]{0:T(128)} %bitcast.refs_0_, ...), custom_call_target="tpu_custom_call" | custom-call | flops 1 | bytes 9000000 | tf_op jit(solution)/shard_map/finish/pallas_call | solution.py:473
  182.7 2.5 %collective-permute-done.29.refs_3_ = bf16[96,1792]{1,0:T(8,128)(2,1)S(1)} collective-permute-done((bf16[96,1792]{1,0:T(8,128)(2,1)}, bf16[96,1792]{1,0:T(8,128)(2,1)S(1)}, u32[]{:S(2)}, u32[]{:S(2)}) %collective-permute-start.29) | collective-permute-done | bytes 344096 | tf_op jit(solution)/shard_map/ppermute | solution.py:1778
  187.7 3.0 %collect.1 = (f32[384,768]{1,0:T(8,128)}, f32[96,3072]{1,0:T(8,128)}, f32[96,768]{1,0:T(8,128)}) custom-call(s32[1]{0:T(128)} %bitcast.refs_0_, bf16[96,1792]{1,0:T(8,128)(2,1)} %last_fold.1.refs_1_, bf16[96,1792]{1,0:T(8,128)(2,1)} %copy-done.12, bf16[96,1792]{1,0:T(8,128)(2,1)} %copy-done.11, bf16[96,1792]{1,0:T(8,128)(2,1)} %copy-done.13), custom_call_target="tpu_custom_call" | custom-call | flops 1 | bytes 9000000 | tf_op jit(solution)/shard_map/collect/pallas_call | solution.py:473
  (135 shorter events, 43.6 us)
Async XLA Ops:
  2.7 13.0 %collective-permute-start.1 = (bf16[128,768]{1,0:T(8,128)(2,1)}, bf16[128,768]{1,0:T(8,128)(2,1)S(1)}, u32[]{:S(2)}, u32[]{:S(2)}) collective-permute-start(bf16[128,768]{1,0:T(8,128)(2,1)} %get-tuple-element.122.refs_1_), channel_id=1, source_target_pairs={{0,2},{1,3},{2,0},{3,1},{4,6},{5,7},{6,4},{7,5},{8,10},{9,11},{10,... | collective-permute-start | bytes 589832 | tf_op jit(solution)/shard_map/ppermute | solution.py:1778
  5.7 17.4 %collective-permute-start.2 = (bf16[128,768]{1,0:T(8,128)(2,1)}, bf16[128,768]{1,0:T(8,128)(2,1)S(1)}, u32[]{:S(2)}, u32[]{:S(2)}) collective-permute-start(bf16[128,768]{1,0:T(8,128)(2,1)} %get-tuple-element.122.refs_1_), channel_id=1, source_target_pairs={{0,4},{1,5},{2,6},{3,7},{4,0},{5,1},{6,2},{7,3},{8,12},{9,13},{10,... | collective-permute-start | bytes 589832 | tf_op jit(solution)/shard_map/ppermute | solution.py:1778
  8.3 14.8 %collective-permute-start.3 = (bf16[128,768]{1,0:T(8,128)(2,1)}, bf16[128,768]{1,0:T(8,128)(2,1)S(1)}, u32[]{:S(2)}, u32[]{:S(2)}) collective-permute-start(bf16[128,768]{1,0:T(8,128)(2,1)} %get-tuple-element.122.refs_1_), channel_id=1, source_target_pairs={{0,6},{1,7},{2,4},{3,5},{4,2},{5,3},{6,0},{7,1},{8,14},{9,15},{10,... | collective-permute-start | bytes 589832 | tf_op jit(solution)/shard_map/ppermute | solution.py:1778
  8.3 26.4 %collective-permute-start = (bf16[128,768]{1,0:T(8,128)(2,1)}, bf16[128,768]{1,0:T(8,128)(2,1)S(1)}, u32[]{:S(2)}, u32[]{:S(2)}) collective-permute-start(bf16[128,768]{1,0:T(8,128)(2,1)} %get-tuple-element.122.refs_1_), channel_id=1, source_target_pairs={{0,1},{1,0},{2,3},{3,2},{4,5},{5,4},{6,7},{7,6},{8,9},{9,8},{10,11... | collective-permute-start | bytes 589832 | tf_op jit(solution)/shard_map/ppermute | solution.py:1778
  23.1 11.6 %collective-permute-start.4 = (bf16[128,768]{1,0:T(8,128)(2,1)S(1)}, bf16[128,768]{1,0:T(8,128)(2,1)S(1)}, u32[]{:S(2)}, u32[]{:S(2)}) collective-permute-start(bf16[128,768]{1,0:T(8,128)(2,1)S(1)} %collective-permute-done.1.refs_3_), channel_id=1, source_target_pairs={{0,1},{1,0},{2,3},{3,2},{4,5},{5,4},{6,7},{7,6},{8,9},{9,8},{10,11... | collective-permute-start | bytes 589832 | tf_op jit(solution)/shard_map/ppermute | solution.py:1778
  24.7 10.1 %collective-permute-start.5 = (bf16[128,768]{1,0:T(8,128)(2,1)S(1)}, bf16[128,768]{1,0:T(8,128)(2,1)S(1)}, u32[]{:S(2)}, u32[]{:S(2)}) collective-permute-start(bf16[128,768]{1,0:T(8,128)(2,1)S(1)} %collective-permute-done.2.refs_5_), channel_id=1, source_target_pairs={{0,1},{1,0},{2,3},{3,2},{4,5},{5,4},{6,7},{7,6},{8,9},{9,8},{10,11... | collective-permute-start | bytes 589832 | tf_op jit(solution)/shard_map/ppermute | solution.py:1778
  25.2 10.5 %collective-permute-start.6 = (bf16[128,768]{1,0:T(8,128)(2,1)S(1)}, bf16[128,768]{1,0:T(8,128)(2,1)S(1)}, u32[]{:S(2)}, u32[]{:S(2)}) collective-permute-start(bf16[128,768]{1,0:T(8,128)(2,1)S(1)} %collective-permute-done.3.refs_7_), channel_id=1, source_target_pairs={{0,1},{1,0},{2,3},{3,2},{4,5},{5,4},{6,7},{7,6},{8,9},{9,8},{10,11... | collective-permute-start | bytes 589832 | tf_op jit(solution)/shard_map/ppermute | solution.py:1778
  26.7 26.9 %collective-permute-start.8 = (bf16[128,768]{1,0:T(8,128)(2,1)S(1)}, bf16[128,768]{1,0:T(8,128)(2,1)S(1)}, u32[]{:S(2)}, u32[]{:S(2)}) collective-permute-start(bf16[128,768]{1,0:T(8,128)(2,1)S(1)} %copy-done.7), channel_id=1, source_target_pairs={{0,16},{8,24},{16,0},{24,8},{1,17},{9,25},{17,1},{25,9},{2,18},{10... | collective-permute-start | bytes 589832 | tf_op jit(solution)/shard_map/ppermute | solution.py:1778
  45.7 15.7 %all-to-all-start = ((bf16[8,96,128]{2,1,0:T(8,128)(2,1)}), bf16[8,96,128]{2,1,0:T(8,128)(2,1)S(1)}, u32[]{:S(2)}, u32[]{:S(2)}) async-start(bf16[8,96,128]{2,1,0:T(8,128)(2,1)} %get-tuple-element.135), calls=%async_computation | async-start | bytes 393216 | tf_op jit(solution)/shard_map/all_to_all | solution.py:2007
  53.6 1.7 collective-permute-start.9
  72.9 28.4 %collective-permute-start.11 = (bf16[128,1536]{1,0:T(8,128)(2,1)}, bf16[128,1536]{1,0:T(8,128)(2,1)}, u32[]{:S(2)}, u32[]{:S(2)}) collective-permute-start(bf16[128,1536]{1,0:T(8,128)(2,1)} %get-tuple-element.152.refs_1_), channel_id=1, source_target_pairs={{0,16},{8,24},{16,0},{24,8},{1,17},{9,25},{17,1},{25,9},{2,18},{10... | collective-permute-start | bytes 1179656 | tf_op jit(solution)/shard_map/ppermute | solution.py:1778
  74.4 11.1 %all-to-all-start.1 = ((bf16[8,96,128]{2,1,0:T(8,128)(2,1)}), bf16[8,96,128]{2,1,0:T(8,128)(2,1)S(1)}, u32[]{:S(2)}, u32[]{:S(2)}) async-start(bf16[8,96,128]{2,1,0:T(8,128)(2,1)} %get-tuple-element.142), calls=%async_computation.1 | async-start | bytes 393216 | tf_op jit(solution)/shard_map/all_to_all | solution.py:2074
  77.8 27.9 %collective-permute-start.13 = (bf16[128,1792]{1,0:T(8,128)(2,1)}, bf16[128,1792]{1,0:T(8,128)(2,1)}, u32[]{:S(2)}, u32[]{:S(2)}) collective-permute-start(bf16[128,1792]{1,0:T(8,128)(2,1)} %get-tuple-element.158), channel_id=1, source_target_pairs={{0,8},{8,0},{16,24},{24,16},{1,9},{9,1},{17,25},{25,17},{2,10},{10... | collective-permute-start | bytes 1376264 | tf_op jit(solution)/shard_map/ppermute | solution.py:1778
  77.9 27.9 %collective-permute-start.14 = (bf16[128,1792]{1,0:T(8,128)(2,1)}, bf16[128,1792]{1,0:T(8,128)(2,1)}, u32[]{:S(2)}, u32[]{:S(2)}) collective-permute-start(bf16[128,1792]{1,0:T(8,128)(2,1)} %get-tuple-element.159), channel_id=1, source_target_pairs={{0,16},{8,24},{16,0},{24,8},{1,17},{9,25},{17,1},{25,9},{2,18},{10... | collective-permute-start | bytes 1376264 | tf_op jit(solution)/shard_map/ppermute | solution.py:1778
  78.5 27.3 %collective-permute-start.15 = (bf16[128,1792]{1,0:T(8,128)(2,1)}, bf16[128,1792]{1,0:T(8,128)(2,1)}, u32[]{:S(2)}, u32[]{:S(2)}) collective-permute-start(bf16[128,1792]{1,0:T(8,128)(2,1)} %get-tuple-element.160), channel_id=1, source_target_pairs={{0,24},{8,16},{16,8},{24,0},{1,25},{9,17},{17,9},{25,1},{2,26},{10... | collective-permute-start | bytes 1376264 | tf_op jit(solution)/shard_map/ppermute | solution.py:1778
  79.8 26.0 %collective-permute-start.10 = (bf16[128,1536]{1,0:T(8,128)(2,1)}, bf16[128,1536]{1,0:T(8,128)(2,1)}, u32[]{:S(2)}, u32[]{:S(2)}) collective-permute-start(bf16[128,1536]{1,0:T(8,128)(2,1)} %get-tuple-element.152.refs_1_), channel_id=1, source_target_pairs={{0,8},{8,0},{16,24},{24,16},{1,9},{9,1},{17,25},{25,17},{2,10},{10... | collective-permute-start | bytes 1179656 | tf_op jit(solution)/shard_map/ppermute | solution.py:1778
  97.5 25.8 %all-to-all-start.2 = ((bf16[8,288,128]{2,1,0:T(8,128)(2,1)}), bf16[8,288,128]{2,1,0:T(8,128)(2,1)S(1)}, u32[]{:S(2)}, u32[]{:S(2)}) async-start(bf16[8,288,128]{2,1,0:T(8,128)(2,1)} %get-tuple-element.175), calls=%async_computation.2 | async-start | bytes 1179648 | tf_op jit(solution)/shard_map/all_to_all | solution.py:2120
  101.3 4.5 %collective-permute-start.12 = (bf16[128,1536]{1,0:T(8,128)(2,1)}, bf16[128,1536]{1,0:T(8,128)(2,1)}, u32[]{:S(2)}, u32[]{:S(2)}) collective-permute-start(bf16[128,1536]{1,0:T(8,128)(2,1)} %collective-permute-done.11.refs_3_), channel_id=1, source_target_pairs={{0,8},{8,0},{16,24},{24,16},{1,9},{9,1},{17,25},{25,17},{2,10},{10... | collective-permute-start | bytes 1179656 | tf_op jit(solution)/shard_map/ppermute | solution.py:1778
  111.3 10.9 %collective-permute-start.19 = (bf16[2,576,128]{2,1,0:T(8,128)(2,1)S(1)}, bf16[2,576,128]{2,1,0:T(8,128)(2,1)}, u32[]{:S(2)}, u32[]{:S(2)}) collective-permute-start(bf16[2,576,128]{2,1,0:T(8,128)(2,1)S(1)} %fusion), channel_id=1, source_target_pairs={{0,8},{8,0},{16,24},{24,16},{1,9},{9,1},{17,25},{25,17},{2,10},{10... | collective-permute-start | bytes 884744 | tf_op jit(solution)/shard_map/ppermute | solution.py:1778
  111.9 31.6 %collective-permute-start.16 = (bf16[4,96,768]{2,1,0:T(8,128)(2,1)}, bf16[4,96,768]{2,1,0:T(8,128)(2,1)}, u32[]{:S(2)}, u32[]{:S(2)}) collective-permute-start(bf16[4,96,768]{2,1,0:T(8,128)(2,1)} %get-tuple-element.164), channel_id=1, source_target_pairs={{0,1},{1,0},{2,3},{3,2},{4,5},{5,4},{6,7},{7,6},{8,9},{9,8},{10,11... | collective-permute-start | bytes 1769480 | tf_op jit(solution)/shard_map/ppermute | solution.py:1778
  113.5 24.3 %collective-permute-start.26 = (bf16[4,96,960]{2,1,0:T(8,128)(2,1)}, bf16[4,96,960]{2,1,0:T(8,128)(2,1)S(1)}, u32[]{:S(2)}, u32[]{:S(2)}) collective-permute-start(bf16[4,96,960]{2,1,0:T(8,128)(2,1)} %get-tuple-element.189), channel_id=1, source_target_pairs={{0,2},{1,3},{2,0},{3,1},{4,6},{5,7},{6,4},{7,5},{8,10},{9,11},{10,... | collective-permute-start | bytes 2211848 | tf_op jit(solution)/shard_map/ppermute | solution.py:1778
  124.4 6.7 %collective-permute-start.20 = (bf16[1,576,128]{2,1,0:T(8,128)(2,1)S(1)}, bf16[1,576,128]{2,1,0:T(8,128)(2,1)S(1)}, u32[]{:S(2)}, u32[]{:S(2)}) collective-permute-start(bf16[1,576,128]{2,1,0:T(8,128)(2,1)S(1)} %dynamic-slice_convert_fusion), channel_id=1, source_target_pairs={{0,16},{8,24},{16,0},{24,8},{1,17},{9,25},{17,1},{25,9},{2,18},{10... | collective-permute-start | bytes 442376 | tf_op jit(solution)/shard_map/ppermute | solution.py:1778
  126.3 5.4 %collective-permute-start.22 = (f32[1,96,128]{2,1,0:T(8,128)S(1)}, f32[1,96,128]{2,1,0:T(8,128)S(1)}, u32[]{:S(2)}, u32[]{:S(2)}) collective-permute-start(f32[1,96,128]{2,1,0:T(8,128)S(1)} %get-tuple-element.218), channel_id=1, source_target_pairs={{0,16},{8,24},{16,0},{24,8},{1,17},{9,25},{17,1},{25,9},{2,18},{10... | collective-permute-start | bytes 147464 | tf_op jit(solution)/shard_map/ppermute | solution.py:1778
  134.2 27.8 %all-to-all-start.3 = ((bf16[8,184,128]{2,1,0:T(8,128)(2,1)}), bf16[8,184,128]{2,1,0:T(8,128)(2,1)S(1)}, u32[]{:S(2)}, u32[]{:S(2)}) async-start(bf16[8,184,128]{2,1,0:T(8,128)(2,1)} %get-tuple-element.181), calls=%async_computation.3 | async-start | bytes 753664 | tf_op jit(solution)/shard_map/all_to_all | solution.py:2223
  141.5 12.1 %collective-permute-start.27 = (bf16[2,96,960]{2,1,0:T(8,128)(2,1)}, bf16[2,96,960]{2,1,0:T(8,128)(2,1)S(1)}, u32[]{:S(2)}, u32[]{:S(2)}) collective-permute-start(bf16[2,96,960]{2,1,0:T(8,128)(2,1)} %get-tuple-element.191), channel_id=1, source_target_pairs={{0,1},{1,0},{2,3},{3,2},{4,5},{5,4},{6,7},{7,6},{8,9},{9,8},{10,11... | collective-permute-start | bytes 1105928 | tf_op jit(solution)/shard_map/ppermute | solution.py:1778
  145.9 13.2 %collective-permute-start.17 = (bf16[2,96,768]{2,1,0:T(8,128)(2,1)}, bf16[2,96,768]{2,1,0:T(8,128)(2,1)S(1)}, u32[]{:S(2)}, u32[]{:S(2)}) collective-permute-start(bf16[2,96,768]{2,1,0:T(8,128)(2,1)} %get-tuple-element.166), channel_id=1, source_target_pairs={{0,2},{1,3},{2,0},{3,1},{4,6},{5,7},{6,4},{7,5},{8,10},{9,11},{10,... | collective-permute-start | bytes 884744 | tf_op jit(solution)/shard_map/ppermute | solution.py:1778
  156.4 17.3 %collective-permute-start.28 = (bf16[1,96,960]{2,1,0:T(8,128)(2,1)}, bf16[1,96,960]{2,1,0:T(8,128)(2,1)S(1)}, u32[]{:S(2)}, u32[]{:S(2)}) collective-permute-start(bf16[1,96,960]{2,1,0:T(8,128)(2,1)} %get-tuple-element.193), channel_id=1, source_target_pairs={{0,4},{1,5},{2,6},{3,7},{4,0},{5,1},{6,2},{7,3},{8,12},{9,13},{10,... | collective-permute-start | bytes 552968 | tf_op jit(solution)/shard_map/ppermute | solution.py:1778
  161.8 11.9 %collective-permute-start.18 = (bf16[1,96,768]{2,1,0:T(8,128)(2,1)}, bf16[1,96,768]{2,1,0:T(8,128)(2,1)S(1)}, u32[]{:S(2)}, u32[]{:S(2)}) collective-permute-start(bf16[1,96,768]{2,1,0:T(8,128)(2,1)} %get-tuple-element.167), channel_id=1, source_target_pairs={{0,4},{1,5},{2,6},{3,7},{4,0},{5,1},{6,2},{7,3},{8,12},{9,13},{10,... | collective-permute-start | bytes 442376 | tf_op jit(solution)/shard_map/ppermute | solution.py:1778
  164.5 12.5 %collective-permute-start.24 = (bf16[880,128]{1,0:T(8,128)(2,1)}, bf16[880,128]{1,0:T(8,128)(2,1)S(1)}, u32[]{:S(2)}, u32[]{:S(2)}) collective-permute-start(bf16[880,128]{1,0:T(8,128)(2,1)} %merge.1.refs_1_), channel_id=1, source_target_pairs={{0,16},{8,24},{16,0},{24,8},{1,17},{9,25},{17,1},{25,9},{2,18},{10... | collective-permute-start | bytes 675848 | tf_op jit(solution)/shard_map/ppermute | solution.py:1778
  176.5 8.8 %collective-permute-start.29 = (bf16[96,1792]{1,0:T(8,128)(2,1)}, bf16[96,1792]{1,0:T(8,128)(2,1)S(1)}, u32[]{:S(2)}, u32[]{:S(2)}) collective-permute-start(bf16[96,1792]{1,0:T(8,128)(2,1)} %last_fold.1.refs_1_), channel_id=1, source_target_pairs={{0,16},{8,24},{16,0},{24,8},{1,17},{9,25},{17,1},{25,9},{2,18},{10... | collective-permute-start | bytes 1032200 | tf_op jit(solution)/shard_map/ppermute | solution.py:1778
  177.0 1.8 collective-permute-start.25
  177.5 7.7 %collective-permute-start.30 = (bf16[96,1792]{1,0:T(8,128)(2,1)}, bf16[96,1792]{1,0:T(8,128)(2,1)S(1)}, u32[]{:S(2)}, u32[]{:S(2)}) collective-permute-start(bf16[96,1792]{1,0:T(8,128)(2,1)} %last_fold.1.refs_1_), channel_id=1, source_target_pairs={{0,8},{8,0},{16,24},{24,16},{1,9},{9,1},{17,25},{25,17},{2,10},{10... | collective-permute-start | bytes 1032200 | tf_op jit(solution)/shard_map/ppermute | solution.py:1778
  (37 other events, 196.8 us)

commit v4 on v3

--- a/solution.py
+++ b/solution.py
@@ -2068,7 +2068,8 @@
             [bit_of(bits), keep, got],
             micros=1,
             spaces="svvvv",
-            name="fold",
+            limit=12,
+        name="fold",
         )
 
     grad_mixer_chan = lax.all_to_all(grad_mixer, "seq", 0, 0, tiled=True)
@@ -2213,6 +2214,7 @@
             swapped(small_send, "batch", batch_bits[-1])[0],
         ],
         micros=2,
+        limit=12,
         name="spread",
     )
     up_keep, up_send = next_fold(up_keep, up_got, orders[0], 1)
@@ -2241,6 +2243,7 @@
         [((seq_parts * in_count + 2 * done_rows, LANES), low)],
         [mixed_got, small],
         micros=2,
+        limit=12,
         name="merge",
     )
     up_keep, up_send = next_fold(up_keep, up_got, orders[0], 2)
@@ -2255,6 +2258,7 @@
         [((rows_each, total), low)],
         [up_keep, up_got, rest_keep, rest_got],
         micros=1,
+        limit=12,
         name="last_fold",
     )
     (
@@ -2311,6 +2315,7 @@
             ((batch_parts,) + last.shape, low),
             ((batch_parts, done_rows, LANES), f32),
         ],
+        limit=12,
         name="finish",
     )
     entries = {0: weights_done, batch_parts // 2: swapped(weights_done, "batch", batch_parts // 2)}
@@ -2335,6 +2340,7 @@
         micros=3,
         spaces="s" + "v" * (batch_parts + 3),
         scratch=[((batch_parts, rows_each, total), low)],
+        limit=12,
         name="collect",
     )
     return (

time: 192 us -> 183 us (0.953)
  Pallas kernels: 84.3 us -> 71.8 us
  waiting for transfers between devices: 40.3 us -> 49.7 us
  local copies, waits for them, and re-layouts: 12.4 us -> 7.21 us
    pallas_call x18, Pallas kernels: 84.3 us -> 71.8 us  [call_kernel(): pl.pallas_call(kernel, out_shape=shapes, in_specs=specs[:len(args)], out_...]
    ppermute x32, waiting for transfers between devices: 28.8 us -> 38.2 us  [swapped(): lax.ppermute(value, axis, [(source, source ^ bits) for source in range(co...]
    unnamed x66 -> x46, local copies, waits for them, and re-layouts: 8.28 us -> 4.36 us
  transfers between devices with their start and end apart: 36 -> 36, of which waited for: 15 -> 15; matrix products, arithmetic and copies ran while one was open for 4% -> 3% of each run, Pallas kernels for 36% -> 31%
where the time goes in v4:
time: 183 us; the launch traced here: 182 us
  Pallas kernels  71.8 us (39%)
  waiting for transfers between devices  49.7 us (27%)
  starting transfers between devices  49.2 us (27%)
  local copies, waits for them, and re-layouts  7.21 us (4%)
  matrix products  2.61 us (1%)
    pallas_call x18, Pallas kernels, call_kernel(): pl.pallas_call(kernel, out_shape=shapes, in_specs=specs[:len(args)], out_...  71.8 us
    ppermute x32, waiting for transfers between devices, swapped(): lax.ppermute(value, axis, [(source, source ^ bits) for source in range(co...  38.2 us
    ppermute x32, starting transfers between devices, swapped(): lax.ppermute(value, axis, [(source, source ^ bits) for source in range(co...  30.3 us
    all_to_all x1, starting transfers between devices, dense_device(): mixer_back = lax.all_to_all(mixer_chan, 'seq', 0, 0, tiled=True)  7.93 us
    all_to_all x1, waiting for transfers between devices, dense_device(): mixer_back = lax.all_to_all(mixer_chan, 'seq', 0, 0, tiled=True)  6.06 us
    all_to_all x1, waiting for transfers between devices, dense_device(): grad_mixer_chan = lax.all_to_all(grad_mixer, 'seq', 0, 0, tiled=True)  5.43 us
    unnamed x46, local copies, waits for them, and re-layouts  4.36 us
    all_to_all x1, starting transfers between devices, dense_device(): mixed_got = lax.all_to_all(mixed_send, 'seq', 0, 0, tiled=True)  3.8 us
  transfers between devices with their start and end apart: 36, of which 15 were waited for; matrix products, arithmetic and copies ran while one was open for 3% of the time, Pallas kernels for 31%

profile of v4, /device:TPU:0, one launch (start us, length us, event | category | flops | bytes accessed | tf_op | source)
XLA Modules:
  0.0 182.2 jit_solution(16837332617458964465)
XLA Ops:
  0.7 2.1 %norm.1 = (bf16[128,768]{1,0:T(8,128)(2,1)}, bf16[128,768]{1,0:T(8,128)(2,1)}, bf16[128,768]{1,0:T(8,128)(2,1)}) custom-call(bf16[128,768]{1,0:T(8,128)(2,1)} %bitcast.48, bf16[128,768]{1,0:T(8,128)(2,1)} %bitcast.49, bf16[768]{0:T(1024)(128)(2,1)} %refs_1_.1, bf16[768]{0:T(1024)(128)(2,1)} %refs_2_.1), custom_call_target="tpu_custom_call" | custom-call | flops 1 | bytes 3000000 | tf_op jit(solution)/shard_map/norm/pallas_call | solution.py:473
  2.7 3.0 %collective-permute-start.1 = (bf16[128,768]{1,0:T(8,128)(2,1)}, bf16[128,768]{1,0:T(8,128)(2,1)S(1)}, u32[]{:S(2)}, u32[]{:S(2)}) collective-permute-start(bf16[128,768]{1,0:T(8,128)(2,1)} %get-tuple-element.122.refs_1_), channel_id=1, source_target_pairs={{0,2},{1,3},{2,0},{3,1},{4,6},{5,7},{6,4},{7,5},{8,10},{9,11},{10,... | collective-permute-start | bytes 589832 | tf_op jit(solution)/shard_map/ppermute | solution.py:1778
  5.7 2.6 %collective-permute-start.2 = (bf16[128,768]{1,0:T(8,128)(2,1)}, bf16[128,768]{1,0:T(8,128)(2,1)S(1)}, u32[]{:S(2)}, u32[]{:S(2)}) collective-permute-start(bf16[128,768]{1,0:T(8,128)(2,1)} %get-tuple-element.122.refs_1_), channel_id=1, source_target_pairs={{0,4},{1,5},{2,6},{3,7},{4,0},{5,1},{6,2},{7,3},{8,12},{9,13},{10,... | collective-permute-start | bytes 589832 | tf_op jit(solution)/shard_map/ppermute | solution.py:1778
  8.3 1.7 collective-permute-start
  10.1 5.6 %waves.1 = (bf16[1024,512]{1,0:T(8,128)(2,1)}, f32[1024,128]{1,0:T(8,128)}, f32[32,768]{1,0:T(8,128)}, bf16[768,384]{1,0:T(8,128)(2,1)}, f32[32,128]{1,0:T(8,128...) custom-call(s32[1]{0:T(128)} %bitcast.4.refs_0_, bf16[768]{0:T(1024)(128)(2,1)} %refs_1_.1, ...), custom_call_target="tpu_custom_call" | custom-call | flops 1 | bytes 25500000 | tf_op jit(solution)/shard_map/waves/pallas_call | solution.py:473
  15.7 7.4 %collective-permute-done.2.refs_5_ = bf16[128,768]{1,0:T(8,128)(2,1)S(1)} collective-permute-done((bf16[128,768]{1,0:T(8,128)(2,1)}, bf16[128,768]{1,0:T(8,128)(2,1)S(1)}, u32[]{:S(2)}, u32[]{:S(2)}) %collective-permute-start.2) | collective-permute-done | bytes 196640 | tf_op jit(solution)/shard_map/ppermute | solution.py:1778
  28.2 6.5 %filters.1 = (f32[2,1024,256]{2,1,0:T(8,128)}, f32[1024,256]{1,0:T(8,128)}, f32[3,512,256]{2,1,0:T(8,128)}) custom-call(bf16[33,64]{1,0:T(8,128)(2,1)} %pos_weight.3, bf16[64,64]{1,0:T(8,128)(2,1)} %inner_weight.3, bf16[64,64]{1,0:T(8,128)(2,1)} %third_weight.3, f32[4,64]{1,0:T(4,128)} %get-tuple-element.131.vectors, f32[64,256]{1,0:T(8,128)} %get-tuple-element.132.weights, ...), custom_call_target="tpu_custom_call" | custom-call | flops 1 | bytes 39000000 | tf_op jit(solution)/shard_map/filters/pallas_call | solution.py:473
  36.4 9.3 %front.1 = (bf16[1024,768]{1,0:T(8,128)(2,1)}, f32[2,520,384]{2,1,0:T(8,128)}, bf16[512,256]{1,0:T(8,128)(2,1)}, bf16[512,256]{1,0:T(8,128)(2,1)}, bf16[512,256]...) custom-call(s32[1]{0:T(128)} %bitcast.1.refs_0_, ...), custom_call_target="tpu_custom_call" | custom-call | flops 1 | bytes 39000000 | tf_op jit(solution)/shard_map/front/pallas_call | solution.py:473
  45.7 7.9 %all-to-all-start = ((bf16[8,96,128]{2,1,0:T(8,128)(2,1)}), bf16[8,96,128]{2,1,0:T(8,128)(2,1)S(1)}, u32[]{:S(2)}, u32[]{:S(2)}) async-start(bf16[8,96,128]{2,1,0:T(8,128)(2,1)} %get-tuple-element.135), calls=%async_computation | async-start | bytes 393216 | tf_op jit(solution)/shard_map/all_to_all | solution.py:2007
  55.3 6.1 %all-to-all-done.refs_1_ = bf16[8,96,128]{2,1,0:T(8,128)(2,1)S(1)} async-done(((bf16[8,96,128]{2,1,0:T(8,128)(2,1)}), bf16[8,96,128]{2,1,0:T(8,128)(2,1)S(1)}, u32[]{:S(2)}, u32[]{:S(2)}) %all-to-all-start) | async-done | bytes 196640 | tf_op jit(solution)/shard_map/all_to_all | solution.py:2007
  62.0 10.8 %middle.1 = (f32[128,768]{1,0:T(8,128)}, f32[128,768]{1,0:T(8,128)}, bf16[8,96,128]{2,1,0:T(8,128)(2,1)}, f32[48,128]{1,0:T(8,128)}, bf16[128,1536]{1,0:T(8,128)...) custom-call(s32[1]{0:T(128)} %bitcast.refs_0_, ...), custom_call_target="tpu_custom_call" | custom-call | flops 1 | bytes 33000000 | tf_op jit(solution)/shard_map/middle/pallas_call | solution.py:473
  74.4 3.4 %all-to-all-start.1 = ((bf16[8,96,128]{2,1,0:T(8,128)(2,1)}), bf16[8,96,128]{2,1,0:T(8,128)(2,1)S(1)}, u32[]{:S(2)}, u32[]{:S(2)}) async-start(bf16[8,96,128]{2,1,0:T(8,128)(2,1)} %get-tuple-element.142), calls=%async_computation.1 | async-start | bytes 393216 | tf_op jit(solution)/shard_map/all_to_all | solution.py:2075
  80.1 5.4 %all-to-all-done.1.refs_0_ = bf16[8,96,128]{2,1,0:T(8,128)(2,1)S(1)} async-done(((bf16[8,96,128]{2,1,0:T(8,128)(2,1)}), bf16[8,96,128]{2,1,0:T(8,128)(2,1)S(1)}, u32[]{:S(2)}, u32[]{:S(2)}) %all-to-all-start.1) | async-done | bytes 196640 | tf_op jit(solution)/shard_map/all_to_all | solution.py:2075
  86.2 11.2 %back.1 = (bf16[8,288,128]{2,1,0:T(8,128)(2,1)}, bf16[1024,384]{1,0:T(8,128)(2,1)}, f32[2,512,256]{2,1,0:T(8,128)}, f32[24,128]{1,0:T(8,128)}) custom-call(bf16[8,96,128]{2,1,0:T(8,128)(2,1)} %copy-done.11, bf16[512,256]{1,0:T(8,128)(2,1)} %get-tuple-element.143.refs_1_, bf16[512,256]{1,0:T(8,128)(2,1)} %get-tuple-element.144.refs_2_, ...), custom_call_target="tpu_custom_call" | custom-call | flops 1 | bytes 45000000 | tf_op jit(solution)/shard_map/back/pallas_call | solution.py:473
  97.4 3.8 %all-to-all-start.2 = ((bf16[8,288,128]{2,1,0:T(8,128)(2,1)}), bf16[8,288,128]{2,1,0:T(8,128)(2,1)S(1)}, u32[]{:S(2)}, u32[]{:S(2)}) async-start(bf16[8,288,128]{2,1,0:T(8,128)(2,1)} %get-tuple-element.175), calls=%async_computation.2 | async-start | bytes 1179648 | tf_op jit(solution)/shard_map/all_to_all | solution.py:2121
  101.9 2.6 %fusion.1.pair_in = f32[768,384]{1,0:T(8,128)S(1)} fusion(bf16[1024,768]{1,0:T(8,128)(2,1)} %get-tuple-element.141, bf16[1024,384]{1,0:T(8,128)(2,1)} %get-tuple-element.151), kind=kOutput, calls=%fused_computation.10 | convolution fusion | flops 603979776 | bytes 3538944 | tf_op jit(solution)/shard_map/dot_general | solution.py:36
  106.2 5.5 %weights.1 = (f32[4,96,768]{2,1,0:T(8,128)}, bf16[4,96,768]{2,1,0:T(8,128)(2,1)}, f32[4,96,960]{2,1,0:T(8,128)}, bf16[4,96,960]{2,1,0:T(8,128)(2,1)}) custom-call(s32[2]{0:T(128)} %pad_add_fusion.refs_0_, bf16[128,1536]{1,0:T(8,128)(2,1)} %get-tuple-element.152.refs_1_, bf16[128,1536]{1,0:T(8,128)(2,1)} %collective-permute-done.10.refs_2_, ...), custom_call_target="tpu_custom_call" | custom-call | flops 1 | bytes 18000000 | tf_op jit(solution)/shard_map/weights/pallas_call | solution.py:473
  112.3 1.6 collective-permute-start.16
  115.4 7.2 %chain.1 = f32[4,96,128]{2,1,0:T(8,128)} custom-call(f32[32,768]{1,0:T(8,128)} %get-tuple-element.139.refs_4_.norm_rows.rows, bf16[768,384]{1,0:T(8,128)(2,1)} %get-tuple-element.127.refs_9_.in_local, f32[24,128]{1,0:T(8,128)} %get-tuple-element.169.sums, f32[48,128]{1,0:T(8,128)} %get-tuple-element.170.middle_sums, bf16[33,64]{1,0:T(8,128)(2,1)} %pos_weight.3, ...), custom_call_target="tpu_custom_call" | custom-call | flops 1 | bytes 36000000 | tf_op jit(solution)/shard_map/chain/pallas_call | solution.py:473
  126.1 4.5 %collective-permute-done.20 = bf16[1,576,128]{2,1,0:T(8,128)(2,1)S(1)} collective-permute-done((bf16[1,576,128]{2,1,0:T(8,128)(2,1)S(1)}, bf16[1,576,128]{2,1,0:T(8,128)(2,1)S(1)}, u32[]{:S(2)}, u32[]{:S(2)}) %collective-permute-start.20) | collective-permute-done | bytes 147488 | tf_op jit(solution)/shard_map/ppermute | solution.py:1778
  132.7 3.8 %all-to-all-start.3 = ((bf16[8,184,128]{2,1,0:T(8,128)(2,1)}), bf16[8,184,128]{2,1,0:T(8,128)(2,1)S(1)}, u32[]{:S(2)}, u32[]{:S(2)}) async-start(bf16[8,184,128]{2,1,0:T(8,128)(2,1)} %get-tuple-element.181), calls=%async_computation.3 | async-start | bytes 753664 | tf_op jit(solution)/shard_map/all_to_all | solution.py:2225
  136.5 2.0 %fold.6 = (f32[2,96,960]{2,1,0:T(8,128)S(1)}, bf16[2,96,960]{2,1,0:T(8,128)(2,1)}) custom-call(s32[1]{0:T(128)} %bitcast.10.refs_0_, f32[4,96,960]{2,1,0:T(8,128)S(1)} %copy-done, bf16[4,96,960]{2,1,0:T(8,128)(2,1)} %collective-permute-done.26.refs_2_), custom_call_target="tpu_custom_call" | custom-call | flops 1 | bytes 3000000 | tf_op jit(solution)/shard_map/fold/pallas_call | solution.py:473
  139.3 2.0 %collective-permute-start.27 = (bf16[2,96,960]{2,1,0:T(8,128)(2,1)}, bf16[2,96,960]{2,1,0:T(8,128)(2,1)S(1)}, u32[]{:S(2)}, u32[]{:S(2)}) collective-permute-start(bf16[2,96,960]{2,1,0:T(8,128)(2,1)} %get-tuple-element.191), channel_id=1, source_target_pairs={{0,1},{1,0},{2,3},{3,2},{4,5},{5,4},{6,7},{7,6},{8,9},{9,8},{10,11... | collective-permute-start | bytes 1105928 | tf_op jit(solution)/shard_map/ppermute | solution.py:1778
  141.4 1.9 %fold.4 = (f32[2,96,768]{2,1,0:T(8,128)S(1)}, bf16[2,96,768]{2,1,0:T(8,128)(2,1)}) custom-call(s32[1]{0:T(128)} %bitcast.7.refs_0_, f32[4,96,768]{2,1,0:T(8,128)S(1)} %copy-done.1, bf16[4,96,768]{2,1,0:T(8,128)(2,1)} %collective-permute-done.16.refs_2_), custom_call_target="tpu_custom_call" | custom-call | flops 1 | bytes 3000000 | tf_op jit(solution)/shard_map/fold/pallas_call | solution.py:473
  144.7 7.5 %collective-permute-done.27.refs_2_ = bf16[2,96,960]{2,1,0:T(8,128)(2,1)S(1)} collective-permute-done((bf16[2,96,960]{2,1,0:T(8,128)(2,1)}, bf16[2,96,960]{2,1,0:T(8,128)(2,1)S(1)}, u32[]{:S(2)}, u32[]{:S(2)}) %collective-permute-start.27) | collective-permute-done | bytes 368672 | tf_op jit(solution)/shard_map/ppermute | solution.py:1778
  152.2 2.3 %collective-permute-start.28 = (bf16[1,96,960]{2,1,0:T(8,128)(2,1)S(1)}, bf16[1,96,960]{2,1,0:T(8,128)(2,1)S(1)}, u32[]{:S(2)}, u32[]{:S(2)}) collective-permute-start(bf16[1,96,960]{2,1,0:T(8,128)(2,1)S(1)} %get-tuple-element.193), channel_id=1, source_target_pairs={{0,4},{1,5},{2,6},{3,7},{4,0},{5,1},{6,2},{7,3},{8,12},{9,13},{10,... | collective-permute-start | bytes 552968 | tf_op jit(solution)/shard_map/ppermute | solution.py:1778
  156.8 5.5 %final.1 = f32[128,768]{1,0:T(8,128)} custom-call(bf16[8,288,128]{2,1,0:T(8,128)(2,1)} %copy-done.8, bf16[128,768]{1,0:T(8,128)(2,1)} %get-tuple-element.138.refs_2_.tokens, f32[128,768]{1,0:T(8,128)} %get-tuple-element.180.residual, f32[32,768]{1,0:T(8,128)} %get-tuple-element.139.refs_4_.norm_rows.rows, bf16[768,2304]{1,0:T(8,128)(2,1)} %weight_in.1), custom_call_target="tpu_custom_call" | custom-call | flops 1 | bytes 16500000 | tf_op jit(solution)/shard_map/final/pallas_call | solution.py:473
  162.3 7.6 %collective-permute-done.18.up_got = bf16[1,96,768]{2,1,0:T(8,128)(2,1)S(1)} collective-permute-done((bf16[1,96,768]{2,1,0:T(8,128)(2,1)S(1)}, bf16[1,96,768]{2,1,0:T(8,128)(2,1)S(1)}, u32[]{:S(2)}, u32[]{:S(2)}) %collective-permute-start.18) | collective-permute-done | bytes 147488 | tf_op jit(solution)/shard_map/ppermute | solution.py:1778
  172.4 1.6 finish.1
  174.0 4.9 %collective-permute-done.29.refs_3_ = bf16[96,1792]{1,0:T(8,128)(2,1)S(1)} collective-permute-done((bf16[96,1792]{1,0:T(8,128)(2,1)S(1)}, bf16[96,1792]{1,0:T(8,128)(2,1)S(1)}, u32[]{:S(2)}, u32[]{:S(2)}) %collective-permute-start.29) | collective-permute-done | bytes 344096 | tf_op jit(solution)/shard_map/ppermute | solution.py:1778
  178.9 1.6 collective-permute-done.31.refs_4_
  180.5 1.7 collect.1
  (115 shorter events, 30.6 us)
Async XLA Ops:
  2.7 13.0 %collective-permute-start.1 = (bf16[128,768]{1,0:T(8,128)(2,1)}, bf16[128,768]{1,0:T(8,128)(2,1)S(1)}, u32[]{:S(2)}, u32[]{:S(2)}) collective-permute-start(bf16[128,768]{1,0:T(8,128)(2,1)} %get-tuple-element.122.refs_1_), channel_id=1, source_target_pairs={{0,2},{1,3},{2,0},{3,1},{4,6},{5,7},{6,4},{7,5},{8,10},{9,11},{10,... | collective-permute-start | bytes 589832 | tf_op jit(solution)/shard_map/ppermute | solution.py:1778
  5.7 17.4 %collective-permute-start.2 = (bf16[128,768]{1,0:T(8,128)(2,1)}, bf16[128,768]{1,0:T(8,128)(2,1)S(1)}, u32[]{:S(2)}, u32[]{:S(2)}) collective-permute-start(bf16[128,768]{1,0:T(8,128)(2,1)} %get-tuple-element.122.refs_1_), channel_id=1, source_target_pairs={{0,4},{1,5},{2,6},{3,7},{4,0},{5,1},{6,2},{7,3},{8,12},{9,13},{10,... | collective-permute-start | bytes 589832 | tf_op jit(solution)/shard_map/ppermute | solution.py:1778
  8.3 14.8 %collective-permute-start.3 = (bf16[128,768]{1,0:T(8,128)(2,1)}, bf16[128,768]{1,0:T(8,128)(2,1)S(1)}, u32[]{:S(2)}, u32[]{:S(2)}) collective-permute-start(bf16[128,768]{1,0:T(8,128)(2,1)} %get-tuple-element.122.refs_1_), channel_id=1, source_target_pairs={{0,6},{1,7},{2,4},{3,5},{4,2},{5,3},{6,0},{7,1},{8,14},{9,15},{10,... | collective-permute-start | bytes 589832 | tf_op jit(solution)/shard_map/ppermute | solution.py:1778
  8.3 26.4 %collective-permute-start = (bf16[128,768]{1,0:T(8,128)(2,1)}, bf16[128,768]{1,0:T(8,128)(2,1)S(1)}, u32[]{:S(2)}, u32[]{:S(2)}) collective-permute-start(bf16[128,768]{1,0:T(8,128)(2,1)} %get-tuple-element.122.refs_1_), channel_id=1, source_target_pairs={{0,1},{1,0},{2,3},{3,2},{4,5},{5,4},{6,7},{7,6},{8,9},{9,8},{10,11... | collective-permute-start | bytes 589832 | tf_op jit(solution)/shard_map/ppermute | solution.py:1778
  23.1 11.6 %collective-permute-start.4 = (bf16[128,768]{1,0:T(8,128)(2,1)S(1)}, bf16[128,768]{1,0:T(8,128)(2,1)S(1)}, u32[]{:S(2)}, u32[]{:S(2)}) collective-permute-start(bf16[128,768]{1,0:T(8,128)(2,1)S(1)} %collective-permute-done.1.refs_3_), channel_id=1, source_target_pairs={{0,1},{1,0},{2,3},{3,2},{4,5},{5,4},{6,7},{7,6},{8,9},{9,8},{10,11... | collective-permute-start | bytes 589832 | tf_op jit(solution)/shard_map/ppermute | solution.py:1778
  24.7 10.1 %collective-permute-start.5 = (bf16[128,768]{1,0:T(8,128)(2,1)S(1)}, bf16[128,768]{1,0:T(8,128)(2,1)S(1)}, u32[]{:S(2)}, u32[]{:S(2)}) collective-permute-start(bf16[128,768]{1,0:T(8,128)(2,1)S(1)} %collective-permute-done.2.refs_5_), channel_id=1, source_target_pairs={{0,1},{1,0},{2,3},{3,2},{4,5},{5,4},{6,7},{7,6},{8,9},{9,8},{10,11... | collective-permute-start | bytes 589832 | tf_op jit(solution)/shard_map/ppermute | solution.py:1778
  25.2 10.5 %collective-permute-start.6 = (bf16[128,768]{1,0:T(8,128)(2,1)S(1)}, bf16[128,768]{1,0:T(8,128)(2,1)S(1)}, u32[]{:S(2)}, u32[]{:S(2)}) collective-permute-start(bf16[128,768]{1,0:T(8,128)(2,1)S(1)} %collective-permute-done.3.refs_7_), channel_id=1, source_target_pairs={{0,1},{1,0},{2,3},{3,2},{4,5},{5,4},{6,7},{7,6},{8,9},{9,8},{10,11... | collective-permute-start | bytes 589832 | tf_op jit(solution)/shard_map/ppermute | solution.py:1778
  26.7 26.9 %collective-permute-start.8 = (bf16[128,768]{1,0:T(8,128)(2,1)S(1)}, bf16[128,768]{1,0:T(8,128)(2,1)S(1)}, u32[]{:S(2)}, u32[]{:S(2)}) collective-permute-start(bf16[128,768]{1,0:T(8,128)(2,1)S(1)} %copy-done.10), channel_id=1, source_target_pairs={{0,16},{8,24},{16,0},{24,8},{1,17},{9,25},{17,1},{25,9},{2,18},{10... | collective-permute-start | bytes 589832 | tf_op jit(solution)/shard_map/ppermute | solution.py:1778
  45.7 15.7 %all-to-all-start = ((bf16[8,96,128]{2,1,0:T(8,128)(2,1)}), bf16[8,96,128]{2,1,0:T(8,128)(2,1)S(1)}, u32[]{:S(2)}, u32[]{:S(2)}) async-start(bf16[8,96,128]{2,1,0:T(8,128)(2,1)} %get-tuple-element.135), calls=%async_computation | async-start | bytes 393216 | tf_op jit(solution)/shard_map/all_to_all | solution.py:2007
  53.6 1.7 collective-permute-start.9
  72.9 28.4 %collective-permute-start.11 = (bf16[128,1536]{1,0:T(8,128)(2,1)}, bf16[128,1536]{1,0:T(8,128)(2,1)}, u32[]{:S(2)}, u32[]{:S(2)}) collective-permute-start(bf16[128,1536]{1,0:T(8,128)(2,1)} %get-tuple-element.152.refs_1_), channel_id=1, source_target_pairs={{0,16},{8,24},{16,0},{24,8},{1,17},{9,25},{17,1},{25,9},{2,18},{10... | collective-permute-start | bytes 1179656 | tf_op jit(solution)/shard_map/ppermute | solution.py:1778
  74.4 11.1 %all-to-all-start.1 = ((bf16[8,96,128]{2,1,0:T(8,128)(2,1)}), bf16[8,96,128]{2,1,0:T(8,128)(2,1)S(1)}, u32[]{:S(2)}, u32[]{:S(2)}) async-start(bf16[8,96,128]{2,1,0:T(8,128)(2,1)} %get-tuple-element.142), calls=%async_computation.1 | async-start | bytes 393216 | tf_op jit(solution)/shard_map/all_to_all | solution.py:2075
  77.8 28.3 %collective-permute-start.13 = (bf16[128,1792]{1,0:T(8,128)(2,1)}, bf16[128,1792]{1,0:T(8,128)(2,1)}, u32[]{:S(2)}, u32[]{:S(2)}) collective-permute-start(bf16[128,1792]{1,0:T(8,128)(2,1)} %get-tuple-element.158), channel_id=1, source_target_pairs={{0,8},{8,0},{16,24},{24,16},{1,9},{9,1},{17,25},{25,17},{2,10},{10... | collective-permute-start | bytes 1376264 | tf_op jit(solution)/shard_map/ppermute | solution.py:1778
  77.9 28.3 %collective-permute-start.14 = (bf16[128,1792]{1,0:T(8,128)(2,1)}, bf16[128,1792]{1,0:T(8,128)(2,1)}, u32[]{:S(2)}, u32[]{:S(2)}) collective-permute-start(bf16[128,1792]{1,0:T(8,128)(2,1)} %get-tuple-element.159), channel_id=1, source_target_pairs={{0,16},{8,24},{16,0},{24,8},{1,17},{9,25},{17,1},{25,9},{2,18},{10... | collective-permute-start | bytes 1376264 | tf_op jit(solution)/shard_map/ppermute | solution.py:1778
  78.5 27.7 %collective-permute-start.15 = (bf16[128,1792]{1,0:T(8,128)(2,1)}, bf16[128,1792]{1,0:T(8,128)(2,1)}, u32[]{:S(2)}, u32[]{:S(2)}) collective-permute-start(bf16[128,1792]{1,0:T(8,128)(2,1)} %get-tuple-element.160), channel_id=1, source_target_pairs={{0,24},{8,16},{16,8},{24,0},{1,25},{9,17},{17,9},{25,1},{2,26},{10... | collective-permute-start | bytes 1376264 | tf_op jit(solution)/shard_map/ppermute | solution.py:1778
  79.8 26.4 %collective-permute-start.10 = (bf16[128,1536]{1,0:T(8,128)(2,1)}, bf16[128,1536]{1,0:T(8,128)(2,1)}, u32[]{:S(2)}, u32[]{:S(2)}) collective-permute-start(bf16[128,1536]{1,0:T(8,128)(2,1)} %get-tuple-element.152.refs_1_), channel_id=1, source_target_pairs={{0,8},{8,0},{16,24},{24,16},{1,9},{9,1},{17,25},{25,17},{2,10},{10... | collective-permute-start | bytes 1179656 | tf_op jit(solution)/shard_map/ppermute | solution.py:1778
  97.4 25.3 %all-to-all-start.2 = ((bf16[8,288,128]{2,1,0:T(8,128)(2,1)}), bf16[8,288,128]{2,1,0:T(8,128)(2,1)S(1)}, u32[]{:S(2)}, u32[]{:S(2)}) async-start(bf16[8,288,128]{2,1,0:T(8,128)(2,1)} %get-tuple-element.175), calls=%async_computation.2 | async-start | bytes 1179648 | tf_op jit(solution)/shard_map/all_to_all | solution.py:2121
  101.2 5.0 %collective-permute-start.12 = (bf16[128,1536]{1,0:T(8,128)(2,1)}, bf16[128,1536]{1,0:T(8,128)(2,1)}, u32[]{:S(2)}, u32[]{:S(2)}) collective-permute-start(bf16[128,1536]{1,0:T(8,128)(2,1)} %collective-permute-done.11.refs_3_), channel_id=1, source_target_pairs={{0,8},{8,0},{16,24},{24,16},{1,9},{9,1},{17,25},{25,17},{2,10},{10... | collective-permute-start | bytes 1179656 | tf_op jit(solution)/shard_map/ppermute | solution.py:1778
  111.7 10.9 %collective-permute-start.19 = (bf16[2,576,128]{2,1,0:T(8,128)(2,1)S(1)}, bf16[2,576,128]{2,1,0:T(8,128)(2,1)S(1)}, u32[]{:S(2)}, u32[]{:S(2)}) collective-permute-start(bf16[2,576,128]{2,1,0:T(8,128)(2,1)S(1)} %fusion), channel_id=1, source_target_pairs={{0,8},{8,0},{16,24},{24,16},{1,9},{9,1},{17,25},{25,17},{2,10},{10... | collective-permute-start | bytes 884744 | tf_op jit(solution)/shard_map/ppermute | solution.py:1778
  112.3 29.1 %collective-permute-start.16 = (bf16[4,96,768]{2,1,0:T(8,128)(2,1)}, bf16[4,96,768]{2,1,0:T(8,128)(2,1)}, u32[]{:S(2)}, u32[]{:S(2)}) collective-permute-start(bf16[4,96,768]{2,1,0:T(8,128)(2,1)} %get-tuple-element.164), channel_id=1, source_target_pairs={{0,1},{1,0},{2,3},{3,2},{4,5},{5,4},{6,7},{7,6},{8,9},{9,8},{10,11... | collective-permute-start | bytes 1769480 | tf_op jit(solution)/shard_map/ppermute | solution.py:1778
  113.9 22.5 %collective-permute-start.26 = (bf16[4,96,960]{2,1,0:T(8,128)(2,1)}, bf16[4,96,960]{2,1,0:T(8,128)(2,1)}, u32[]{:S(2)}, u32[]{:S(2)}) collective-permute-start(bf16[4,96,960]{2,1,0:T(8,128)(2,1)} %get-tuple-element.189), channel_id=1, source_target_pairs={{0,2},{1,3},{2,0},{3,1},{4,6},{5,7},{6,4},{7,5},{8,10},{9,11},{10,... | collective-permute-start | bytes 2211848 | tf_op jit(solution)/shard_map/ppermute | solution.py:1778
  123.9 6.7 %collective-permute-start.20 = (bf16[1,576,128]{2,1,0:T(8,128)(2,1)S(1)}, bf16[1,576,128]{2,1,0:T(8,128)(2,1)S(1)}, u32[]{:S(2)}, u32[]{:S(2)}) collective-permute-start(bf16[1,576,128]{2,1,0:T(8,128)(2,1)S(1)} %dynamic-slice_convert_fusion), channel_id=1, source_target_pairs={{0,16},{8,24},{16,0},{24,8},{1,17},{9,25},{17,1},{25,9},{2,18},{10... | collective-permute-start | bytes 442376 | tf_op jit(solution)/shard_map/ppermute | solution.py:1778
  125.2 6.1 %collective-permute-start.22 = (f32[1,96,128]{2,1,0:T(8,128)S(1)}, f32[1,96,128]{2,1,0:T(8,128)S(1)}, u32[]{:S(2)}, u32[]{:S(2)}) collective-permute-start(f32[1,96,128]{2,1,0:T(8,128)S(1)} %get-tuple-element.218), channel_id=1, source_target_pairs={{0,16},{8,24},{16,0},{24,8},{1,17},{9,25},{17,1},{25,9},{2,18},{10... | collective-permute-start | bytes 147464 | tf_op jit(solution)/shard_map/ppermute | solution.py:1778
  132.7 22.7 %all-to-all-start.3 = ((bf16[8,184,128]{2,1,0:T(8,128)(2,1)}), bf16[8,184,128]{2,1,0:T(8,128)(2,1)S(1)}, u32[]{:S(2)}, u32[]{:S(2)}) async-start(bf16[8,184,128]{2,1,0:T(8,128)(2,1)} %get-tuple-element.181), calls=%async_computation.3 | async-start | bytes 753664 | tf_op jit(solution)/shard_map/all_to_all | solution.py:2225
  139.3 12.8 %collective-permute-start.27 = (bf16[2,96,960]{2,1,0:T(8,128)(2,1)}, bf16[2,96,960]{2,1,0:T(8,128)(2,1)S(1)}, u32[]{:S(2)}, u32[]{:S(2)}) collective-permute-start(bf16[2,96,960]{2,1,0:T(8,128)(2,1)} %get-tuple-element.191), channel_id=1, source_target_pairs={{0,1},{1,0},{2,3},{3,2},{4,5},{5,4},{6,7},{7,6},{8,9},{9,8},{10,11... | collective-permute-start | bytes 1105928 | tf_op jit(solution)/shard_map/ppermute | solution.py:1778
  143.2 11.3 %collective-permute-start.17 = (bf16[2,96,768]{2,1,0:T(8,128)(2,1)}, bf16[2,96,768]{2,1,0:T(8,128)(2,1)S(1)}, u32[]{:S(2)}, u32[]{:S(2)}) collective-permute-start(bf16[2,96,768]{2,1,0:T(8,128)(2,1)} %get-tuple-element.166), channel_id=1, source_target_pairs={{0,2},{1,3},{2,0},{3,1},{4,6},{5,7},{6,4},{7,5},{8,10},{9,11},{10,... | collective-permute-start | bytes 884744 | tf_op jit(solution)/shard_map/ppermute | solution.py:1778
  152.2 17.7 %collective-permute-start.28 = (bf16[1,96,960]{2,1,0:T(8,128)(2,1)S(1)}, bf16[1,96,960]{2,1,0:T(8,128)(2,1)S(1)}, u32[]{:S(2)}, u32[]{:S(2)}) collective-permute-start(bf16[1,96,960]{2,1,0:T(8,128)(2,1)S(1)} %get-tuple-element.193), channel_id=1, source_target_pairs={{0,4},{1,5},{2,6},{3,7},{4,0},{5,1},{6,2},{7,3},{8,12},{9,13},{10,... | collective-permute-start | bytes 552968 | tf_op jit(solution)/shard_map/ppermute | solution.py:1778
  154.6 15.3 %collective-permute-start.18 = (bf16[1,96,768]{2,1,0:T(8,128)(2,1)S(1)}, bf16[1,96,768]{2,1,0:T(8,128)(2,1)S(1)}, u32[]{:S(2)}, u32[]{:S(2)}) collective-permute-start(bf16[1,96,768]{2,1,0:T(8,128)(2,1)S(1)} %get-tuple-element.167), channel_id=1, source_target_pairs={{0,4},{1,5},{2,6},{3,7},{4,0},{5,1},{6,2},{7,3},{8,12},{9,13},{10,... | collective-permute-start | bytes 442376 | tf_op jit(solution)/shard_map/ppermute | solution.py:1778
  156.2 14.4 %collective-permute-start.24 = (bf16[880,128]{1,0:T(8,128)(2,1)S(1)}, bf16[880,128]{1,0:T(8,128)(2,1)S(1)}, u32[]{:S(2)}, u32[]{:S(2)}) collective-permute-start(bf16[880,128]{1,0:T(8,128)(2,1)S(1)} %merge.1.refs_1_), channel_id=1, source_target_pairs={{0,16},{8,24},{16,0},{24,8},{1,17},{9,25},{17,1},{25,9},{2,18},{10... | collective-permute-start | bytes 675848 | tf_op jit(solution)/shard_map/ppermute | solution.py:1778
  170.0 8.9 %collective-permute-start.29 = (bf16[96,1792]{1,0:T(8,128)(2,1)S(1)}, bf16[96,1792]{1,0:T(8,128)(2,1)S(1)}, u32[]{:S(2)}, u32[]{:S(2)}) collective-permute-start(bf16[96,1792]{1,0:T(8,128)(2,1)S(1)} %last_fold.1.refs_1_), channel_id=1, source_target_pairs={{0,16},{8,24},{16,0},{24,8},{1,17},{9,25},{17,1},{25,9},{2,18},{10... | collective-permute-start | bytes 1032200 | tf_op jit(solution)/shard_map/ppermute | solution.py:1778
  170.6 1.8 collective-permute-start.25
  171.1 7.8 %collective-permute-start.30 = (bf16[96,1792]{1,0:T(8,128)(2,1)S(1)}, bf16[96,1792]{1,0:T(8,128)(2,1)S(1)}, u32[]{:S(2)}, u32[]{:S(2)}) collective-permute-start(bf16[96,1792]{1,0:T(8,128)(2,1)S(1)} %last_fold.1.refs_1_), channel_id=1, source_target_pairs={{0,8},{8,0},{16,24},{24,16},{1,9},{9,1},{17,25},{25,17},{2,10},{10... | collective-permute-start | bytes 1032200 | tf_op jit(solution)/shard_map/ppermute | solution.py:1778
  (27 other events, 183.2 us)

commit v5 on v4

--- a/solution.py
+++ b/solution.py
@@ -954,14 +954,18 @@
     (
         normed_out,
         projected_out,
+        product_hbm,
+        gate_hbm,
+        after_hbm,
+        gated_hbm,
+        product_wave_out,
+        gated_wave_out,
+        mixed_out,
+        mixer_out,
         product_out,
         gate_out,
         after_out,
         gated_out,
-        product_wave_out,
-        gated_wave_out,
-        mixed_out,
-        mixer_out,
         held,
         reals,
         imags,
@@ -994,6 +998,10 @@
                 (product_wave, product_wave_out),
                 (gated_wave, gated_wave_out),
                 (mixed, mixed_out),
+                (product_out, product_hbm),
+                (gate_out, gate_hbm),
+                (after_out, after_hbm),
+                (gated_out, gated_hbm),
             ]
         )
     ]
@@ -1028,7 +1036,8 @@
         return carry
 
     lax.fori_loop(0, half // CHUNK, mix, 0)
-    stores[4].start()
+    for copy in stores[4:7]:
+        copy.start()
     skips = [twice(row_of(rows, "skips", order)) for order in range(2)]
 
     def first(here, convolved):
@@ -1045,7 +1054,8 @@
         copy.wait()
     cols = [slice(order * LANES, (order + 1) * LANES) for order in range(2)]
     convolve(wave, turn, product_out, spectrum, cols[0], product_wave, reals, imags, first)
-    stores[2].start()
+    for copy in (stores[2], stores[7], stores[8]):
+        copy.start()
     convolve(wave, turn, gated_out, spectrum, cols[1], gated_wave, reals, imags, second)
     stores[3].start()
     for part in range(parts):
@@ -1059,12 +1069,12 @@
 def back_kernel(
     channels,
     grad_mixer,
-    product_ref,
-    gate_ref,
-    after_ref,
-    gated_ref,
     rows,
-    turn,
+    product_in,
+    gate_in,
+    after_in,
+    gated_in,
+    turn_in,
     product_wave_in,
     gated_wave_in,
     spectrum_in,
@@ -1079,6 +1089,11 @@
     grad_after,
     grad_value,
     grad_gate,
+    product_ref,
+    gate_ref,
+    after_ref,
+    gated_ref,
+    turn,
     reals,
     imags,
     wave,
@@ -1099,8 +1114,13 @@
         for place, (source, target) in enumerate(
             [
                 (wave_in, wave),
+                (turn_in, turn),
                 (spectrum_in, spectrum),
                 (gated_wave_in, gated_wave),
+                (gate_in, gate_ref),
+                (after_in, after_ref),
+                (gated_in, gated_ref),
+                (product_in, product_ref),
                 (product_wave_in, product_wave),
                 (projected_in, projected),
                 (mixed_in, mixed),
@@ -1137,19 +1157,20 @@
         return total + jnp.sum(top * product_ref[here, :].astype(f32), axis=0, keepdims=True)
 
     cols = [slice(order * LANES, (order + 1) * LANES) for order in range(2)]
-    for copy in loads[:3]:
+    for copy in loads[:7]:
         copy.wait()
     skip_second = correlate(
         wave, turn, grad_mix, spectrum, cols[1], gated_wave, reals, imags, first
     )
-    loads[3].wait()
+    for copy in loads[7:9]:
+        copy.wait()
     skip_first = correlate(
         wave, turn, grad_after, spectrum, cols[0], product_wave, reals, imags, second
     )
     sums_out[15:16, :] = skip_first[:, :LANES] + skip_first[:, LANES:]
     sums_out[16:17, :] = skip_second[:, :LANES] + skip_second[:, LANES:]
     sums_out[17:24, :] = jnp.zeros((7, LANES), f32)
-    for copy in loads[4:]:
+    for copy in loads[9:]:
         copy.wait()
     shifted[:, :, half:, :] = jnp.zeros((3, 2, PAD, LANES), f32)
     sides = [slice(odd * LANES, (odd + 1) * LANES) for odd in range(2)]
@@ -1330,7 +1351,7 @@
         flow[...] += right_dot(grad_upper, up_w[place])
         return carry
 
-    lax.fori_loop(0, quarters, body, 0, unroll=2)
+    lax.fori_loop(0, quarters, body, 0, unroll=True)
     spread_rows(residual[...] + total[...] + row_of(rows, "down_bias"), held, outputs_out)
     _, unit, inv_std = norm_forward(residual[...], gain, bias)
     grad_norm, grad_gain, grad_bias = norm_backward(flow[...], unit, inv_std, gain)
@@ -1923,11 +1944,13 @@
         ],
         name="waves",
     )
-    even = [chunks[bits] for bits in range(2, seq_parts, 2)]
-    wave, *even = lax.optimization_barrier((wave, *even))
-    for bits in range(0, seq_parts, 2):
-        if bits:
-            chunks[bits] = even[bits // 2 - 1]
+    early = [bits for bits in (0, 2) if bits < seq_parts]
+    for bits in early:
+        chunks[bits + 1] = swapped(chunks[bits], "seq", 1)
+    places = sorted(place for place in chunks if place)
+    wave, *gathered = lax.optimization_barrier((wave, *[chunks[place] for place in places]))
+    chunks.update(zip(places, gathered))
+    for bits in range(4, seq_parts, 2):
         chunks[bits + 1] = swapped(chunks[bits], "seq", 1)
     spectrum, kernels, filter_waves = call_kernel(
         filter_kernel,
@@ -1986,8 +2009,9 @@
         + [chunks[part] for part in range(seq_parts)]
         + [in_local, rows_local, wave, turn, spectrum],
         micros=13,
-        spaces="s" + "v" * seq_parts + "vvhhh" + "hhvvvvhhhv",
-        scratch=[
+        spaces="s" + "v" * seq_parts + "vvhhh" + "hhhhhhhhhv",
+        scratch=[((half, 2 * LANES), low)] * 4
+        + [
             ((length, width), low),
             ((half, 2 * LANES), low),
             ((half, 2 * LANES), low),
@@ -1999,7 +2023,7 @@
             ((2, length, LANES), f32),
             ((2, half, 2 * LANES), f32),
             ((half, 2 * LANES), low),
-            8,
+            12,
         ],
         name="front",
     )
@@ -2088,11 +2112,11 @@
         ],
         [
             grad_mixer_chan,
+            rows_local,
             product,
             gate,
             after,
             gated,
-            rows_local,
             turn,
             product_wave,
             gated_wave,
@@ -2102,9 +2126,10 @@
             mixed,
         ],
         micros=15,
-        spaces="v" * 7 + "h" * 6 + "vvvv",
-        scratch=[((half, 2 * LANES), low)] * 4
+        spaces="vv" + "h" * 11 + "vvvv",
+        scratch=[((half, 2 * LANES), low)] * 8
         + [
+            ((length, LANES), f32),
             ((half, 4 * LANES), low),
             ((half, 4 * LANES), low),
             ((length, half), low),
@@ -2114,7 +2139,7 @@
             ((2, PAD + half, wide), f32),
             ((2, half, 2 * LANES), f32),
             ((3, 2, half + PAD, LANES), f32),
-            6,
+            11,
         ],
         name="back",
     )

time: 183 us -> 179 us (0.978)
  waiting for transfers between devices: 49.7 us -> 46.3 us
    ppermute x32, waiting for transfers between devices: 38.2 us -> 34.8 us  [swapped(): lax.ppermute(value, axis, [(source, source ^ bits) for source in range(co...]
    all_to_all x1, starting transfers between devices: 7.93 us -> 5.36 us  [dense_device(): mixer_back = lax.all_to_all(mixer_chan, 'seq', 0, 0, tiled=True)]
    ppermute x32, starting transfers between devices: 30.3 us -> 32.3 us  [swapped(): lax.ppermute(value, axis, [(source, source ^ bits) for source in range(co...]
  transfers between devices with their start and end apart: 36 -> 36, of which waited for: 15 -> 15; matrix products, arithmetic and copies ran while one was open for 3% -> 3% of each run, Pallas kernels for 31% -> 32%
where the time goes in v5:
time: 179 us; the launch traced here: 178 us
  Pallas kernels  71.3 us (40%)
  starting transfers between devices  48.6 us (27%)
  waiting for transfers between devices  46.3 us (26%)
  local copies, waits for them, and re-layouts  7.27 us (4%)
  matrix products  2.6 us (1%)
    pallas_call x18, Pallas kernels, call_kernel(): pl.pallas_call(kernel, out_shape=shapes, in_specs=specs[:len(args)], out_...  71.3 us
    ppermute x32, waiting for transfers between devices, swapped(): lax.ppermute(value, axis, [(source, source ^ bits) for source in range(co...  34.8 us
    ppermute x32, starting transfers between devices, swapped(): lax.ppermute(value, axis, [(source, source ^ bits) for source in range(co...  32.3 us
    all_to_all x1, waiting for transfers between devices, dense_device(): mixer_back = lax.all_to_all(mixer_chan, 'seq', 0, 0, tiled=True)  6.06 us
    all_to_all x1, waiting for transfers between devices, dense_device(): grad_mixer_chan = lax.all_to_all(grad_mixer, 'seq', 0, 0, tiled=True)  5.43 us
    all_to_all x1, starting transfers between devices, dense_device(): mixer_back = lax.all_to_all(mixer_chan, 'seq', 0, 0, tiled=True)  5.36 us
    unnamed x46, local copies, waits for them, and re-layouts  4.41 us
    all_to_all x1, starting transfers between devices, dense_device(): mixed_got = lax.all_to_all(mixed_send, 'seq', 0, 0, tiled=True)  3.8 us
  transfers between devices with their start and end apart: 36, of which 15 were waited for; matrix products, arithmetic and copies ran while one was open for 3% of the time, Pallas kernels for 32%

profile of v5, /device:TPU:0, one launch (start us, length us, event | category | flops | bytes accessed | tf_op | source)
XLA Modules:
  0.0 177.9 jit_solution(10911922360786782315)
XLA Ops:
  0.7 2.1 %norm.1 = (bf16[128,768]{1,0:T(8,128)(2,1)}, bf16[128,768]{1,0:T(8,128)(2,1)}, bf16[128,768]{1,0:T(8,128)(2,1)}) custom-call(bf16[128,768]{1,0:T(8,128)(2,1)} %bitcast.48, bf16[128,768]{1,0:T(8,128)(2,1)} %bitcast.49, bf16[768]{0:T(1024)(128)(2,1)} %refs_1_.1, bf16[768]{0:T(1024)(128)(2,1)} %refs_2_.1), custom_call_target="tpu_custom_call" | custom-call | flops 1 | bytes 3000000 | tf_op jit(solution)/shard_map/norm/pallas_call | solution.py:473
  2.7 3.0 %collective-permute-start.1 = (bf16[128,768]{1,0:T(8,128)(2,1)}, bf16[128,768]{1,0:T(8,128)(2,1)S(1)}, u32[]{:S(2)}, u32[]{:S(2)}) collective-permute-start(bf16[128,768]{1,0:T(8,128)(2,1)} %get-tuple-element.124.refs_1_), channel_id=1, source_target_pairs={{0,2},{1,3},{2,0},{3,1},{4,6},{5,7},{6,4},{7,5},{8,10},{9,11},{10,... | collective-permute-start | bytes 589832 | tf_op jit(solution)/shard_map/ppermute | solution.py:1799
  7.3 2.6 %collective-permute-start.3 = (bf16[128,768]{1,0:T(8,128)(2,1)}, bf16[128,768]{1,0:T(8,128)(2,1)S(1)}, u32[]{:S(2)}, u32[]{:S(2)}) collective-permute-start(bf16[128,768]{1,0:T(8,128)(2,1)} %get-tuple-element.124.refs_1_), channel_id=1, source_target_pairs={{0,4},{1,5},{2,6},{3,7},{4,0},{5,1},{6,2},{7,3},{8,12},{9,13},{10,... | collective-permute-start | bytes 589832 | tf_op jit(solution)/shard_map/ppermute | solution.py:1799
  10.1 2.9 %collective-permute-done.1.refs_3_ = bf16[128,768]{1,0:T(8,128)(2,1)S(1)} collective-permute-done((bf16[128,768]{1,0:T(8,128)(2,1)}, bf16[128,768]{1,0:T(8,128)(2,1)S(1)}, u32[]{:S(2)}, u32[]{:S(2)}) %collective-permute-start.1) | collective-permute-done | bytes 196640 | tf_op jit(solution)/shard_map/ppermute | solution.py:1799
  13.0 2.7 %collective-permute-start.2 = (bf16[128,768]{1,0:T(8,128)(2,1)S(1)}, bf16[128,768]{1,0:T(8,128)(2,1)S(1)}, u32[]{:S(2)}, u32[]{:S(2)}) collective-permute-start(bf16[128,768]{1,0:T(8,128)(2,1)S(1)} %collective-permute-done.1.refs_3_), channel_id=1, source_target_pairs={{0,1},{1,0},{2,3},{3,2},{4,5},{5,4},{6,7},{7,6},{8,9},{9,8},{10,11... | collective-permute-start | bytes 589832 | tf_op jit(solution)/shard_map/ppermute | solution.py:1799
  15.7 5.6 %waves.1 = (bf16[1024,512]{1,0:T(8,128)(2,1)}, f32[1024,128]{1,0:T(8,128)}, f32[32,768]{1,0:T(8,128)}, bf16[768,384]{1,0:T(8,128)(2,1)}, f32[32,128]{1,0:T(8,128...) custom-call(s32[1]{0:T(128)} %bitcast.4.refs_0_, bf16[768]{0:T(1024)(128)(2,1)} %refs_1_.1, ...), custom_call_target="tpu_custom_call" | custom-call | flops 1 | bytes 25500000 | tf_op jit(solution)/shard_map/waves/pallas_call | solution.py:473
  21.3 3.3 %collective-permute-done.3.refs_5_ = bf16[128,768]{1,0:T(8,128)(2,1)S(1)} collective-permute-done((bf16[128,768]{1,0:T(8,128)(2,1)}, bf16[128,768]{1,0:T(8,128)(2,1)S(1)}, u32[]{:S(2)}, u32[]{:S(2)}) %collective-permute-start.3) | collective-permute-done | bytes 196640 | tf_op jit(solution)/shard_map/ppermute | solution.py:1799
  28.2 6.5 %filters.1 = (f32[2,1024,256]{2,1,0:T(8,128)}, f32[1024,256]{1,0:T(8,128)}, f32[3,512,256]{2,1,0:T(8,128)}) custom-call(bf16[33,64]{1,0:T(8,128)(2,1)} %pos_weight.3, bf16[64,64]{1,0:T(8,128)(2,1)} %inner_weight.3, bf16[64,64]{1,0:T(8,128)(2,1)} %third_weight.3, f32[4,64]{1,0:T(4,128)} %get-tuple-element.135.vectors, f32[64,256]{1,0:T(8,128)} %get-tuple-element.136.weights, ...), custom_call_target="tpu_custom_call" | custom-call | flops 1 | bytes 39000000 | tf_op jit(solution)/shard_map/filters/pallas_call | solution.py:473
  35.5 9.1 %front.1 = (bf16[1024,768]{1,0:T(8,128)(2,1)}, f32[2,520,384]{2,1,0:T(8,128)}, bf16[512,256]{1,0:T(8,128)(2,1)}, bf16[512,256]{1,0:T(8,128)(2,1)}, bf16[512,256]...) custom-call(s32[1]{0:T(128)} %bitcast.1.refs_0_, ...), custom_call_target="tpu_custom_call" | custom-call | flops 1 | bytes 39000000 | tf_op jit(solution)/shard_map/front/pallas_call | solution.py:473
  44.6 5.4 %all-to-all-start = ((bf16[8,96,128]{2,1,0:T(8,128)(2,1)}), bf16[8,96,128]{2,1,0:T(8,128)(2,1)S(1)}, u32[]{:S(2)}, u32[]{:S(2)}) async-start(bf16[8,96,128]{2,1,0:T(8,128)(2,1)} %get-tuple-element.139), calls=%async_computation | async-start | bytes 393216 | tf_op jit(solution)/shard_map/all_to_all | solution.py:2031
  51.7 6.1 %all-to-all-done.refs_1_ = bf16[8,96,128]{2,1,0:T(8,128)(2,1)S(1)} async-done(((bf16[8,96,128]{2,1,0:T(8,128)(2,1)}), bf16[8,96,128]{2,1,0:T(8,128)(2,1)S(1)}, u32[]{:S(2)}, u32[]{:S(2)}) %all-to-all-start) | async-done | bytes 196640 | tf_op jit(solution)/shard_map/all_to_all | solution.py:2031
  58.4 10.5 %middle.1 = (f32[128,768]{1,0:T(8,128)}, f32[128,768]{1,0:T(8,128)}, bf16[8,96,128]{2,1,0:T(8,128)(2,1)}, f32[48,128]{1,0:T(8,128)}, bf16[128,1536]{1,0:T(8,128)...) custom-call(s32[1]{0:T(128)} %bitcast.refs_0_, ...), custom_call_target="tpu_custom_call" | custom-call | flops 1 | bytes 33000000 | tf_op jit(solution)/shard_map/middle/pallas_call | solution.py:473
  70.2 3.4 %all-to-all-start.1 = ((bf16[8,96,128]{2,1,0:T(8,128)(2,1)}), bf16[8,96,128]{2,1,0:T(8,128)(2,1)S(1)}, u32[]{:S(2)}, u32[]{:S(2)}) async-start(bf16[8,96,128]{2,1,0:T(8,128)(2,1)} %get-tuple-element.146), calls=%async_computation.1 | async-start | bytes 393216 | tf_op jit(solution)/shard_map/all_to_all | solution.py:2099
  75.8 5.4 %all-to-all-done.1.refs_0_ = bf16[8,96,128]{2,1,0:T(8,128)(2,1)S(1)} async-done(((bf16[8,96,128]{2,1,0:T(8,128)(2,1)}), bf16[8,96,128]{2,1,0:T(8,128)(2,1)S(1)}, u32[]{:S(2)}, u32[]{:S(2)}) %all-to-all-start.1) | async-done | bytes 196640 | tf_op jit(solution)/shard_map/all_to_all | solution.py:2099
  82.0 11.2 %back.1 = (bf16[8,288,128]{2,1,0:T(8,128)(2,1)}, bf16[1024,384]{1,0:T(8,128)(2,1)}, f32[2,512,256]{2,1,0:T(8,128)}, f32[24,128]{1,0:T(8,128)}) custom-call(bf16[8,96,128]{2,1,0:T(8,128)(2,1)} %copy-done.11, f32[32,128]{1,0:T(8,128)} %get-tuple-element.132.refs_10_.refs_1_, bf16[512,256]{1,0:T(8,128)(2,1)} %get-tuple-element.147.refs_2_, ...), custom_call_target="tpu_custom_call" | custom-call | flops 1 | bytes 45000000 | tf_op jit(solution)/shard_map/back/pallas_call | solution.py:473
  93.1 3.8 %all-to-all-start.2 = ((bf16[8,288,128]{2,1,0:T(8,128)(2,1)}), bf16[8,288,128]{2,1,0:T(8,128)(2,1)S(1)}, u32[]{:S(2)}, u32[]{:S(2)}) async-start(bf16[8,288,128]{2,1,0:T(8,128)(2,1)} %get-tuple-element.179), calls=%async_computation.2 | async-start | bytes 1179648 | tf_op jit(solution)/shard_map/all_to_all | solution.py:2146
  97.6 2.6 %fusion.1.pair_in = f32[768,384]{1,0:T(8,128)S(1)} fusion(bf16[1024,768]{1,0:T(8,128)(2,1)} %get-tuple-element.145, bf16[1024,384]{1,0:T(8,128)(2,1)} %get-tuple-element.155), kind=kOutput, calls=%fused_computation.10 | convolution fusion | flops 603979776 | bytes 3538944 | tf_op jit(solution)/shard_map/dot_general | solution.py:36
  101.9 5.5 %weights.1 = (f32[4,96,768]{2,1,0:T(8,128)}, bf16[4,96,768]{2,1,0:T(8,128)(2,1)}, f32[4,96,960]{2,1,0:T(8,128)}, bf16[4,96,960]{2,1,0:T(8,128)(2,1)}) custom-call(s32[2]{0:T(128)} %pad_add_fusion.refs_0_, bf16[128,1536]{1,0:T(8,128)(2,1)} %get-tuple-element.156.refs_1_, bf16[128,1536]{1,0:T(8,128)(2,1)} %collective-permute-done.10.refs_2_, ...), custom_call_target="tpu_custom_call" | custom-call | flops 1 | bytes 18000000 | tf_op jit(solution)/shard_map/weights/pallas_call | solution.py:473
  108.0 1.6 collective-permute-start.16
  111.1 7.2 %chain.1 = f32[4,96,128]{2,1,0:T(8,128)} custom-call(f32[32,768]{1,0:T(8,128)} %get-tuple-element.143.refs_4_.norm_rows.rows, bf16[768,384]{1,0:T(8,128)(2,1)} %get-tuple-element.131.refs_9_.in_local, f32[24,128]{1,0:T(8,128)} %get-tuple-element.173.sums, f32[48,128]{1,0:T(8,128)} %get-tuple-element.174.middle_sums, bf16[33,64]{1,0:T(8,128)(2,1)} %pos_weight.3, ...), custom_call_target="tpu_custom_call" | custom-call | flops 1 | bytes 36000000 | tf_op jit(solution)/shard_map/chain/pallas_call | solution.py:473
  121.9 4.4 %collective-permute-done.20 = bf16[1,576,128]{2,1,0:T(8,128)(2,1)S(1)} collective-permute-done((bf16[1,576,128]{2,1,0:T(8,128)(2,1)S(1)}, bf16[1,576,128]{2,1,0:T(8,128)(2,1)S(1)}, u32[]{:S(2)}, u32[]{:S(2)}) %collective-permute-start.20) | collective-permute-done | bytes 147488 | tf_op jit(solution)/shard_map/ppermute | solution.py:1799
  128.3 3.8 %all-to-all-start.3 = ((bf16[8,184,128]{2,1,0:T(8,128)(2,1)}), bf16[8,184,128]{2,1,0:T(8,128)(2,1)S(1)}, u32[]{:S(2)}, u32[]{:S(2)}) async-start(bf16[8,184,128]{2,1,0:T(8,128)(2,1)} %get-tuple-element.185), calls=%async_computation.3 | async-start | bytes 753664 | tf_op jit(solution)/shard_map/all_to_all | solution.py:2250
  132.1 2.0 %fold.6 = (f32[2,96,960]{2,1,0:T(8,128)S(1)}, bf16[2,96,960]{2,1,0:T(8,128)(2,1)}) custom-call(s32[1]{0:T(128)} %bitcast.10.refs_0_, f32[4,96,960]{2,1,0:T(8,128)S(1)} %copy-done, bf16[4,96,960]{2,1,0:T(8,128)(2,1)} %collective-permute-done.26.refs_2_), custom_call_target="tpu_custom_call" | custom-call | flops 1 | bytes 3000000 | tf_op jit(solution)/shard_map/fold/pallas_call | solution.py:473
  135.0 2.0 %collective-permute-start.27 = (bf16[2,96,960]{2,1,0:T(8,128)(2,1)}, bf16[2,96,960]{2,1,0:T(8,128)(2,1)S(1)}, u32[]{:S(2)}, u32[]{:S(2)}) collective-permute-start(bf16[2,96,960]{2,1,0:T(8,128)(2,1)} %get-tuple-element.195), channel_id=1, source_target_pairs={{0,1},{1,0},{2,3},{3,2},{4,5},{5,4},{6,7},{7,6},{8,9},{9,8},{10,11... | collective-permute-start | bytes 1105928 | tf_op jit(solution)/shard_map/ppermute | solution.py:1799
  137.0 1.9 %fold.4 = (f32[2,96,768]{2,1,0:T(8,128)S(1)}, bf16[2,96,768]{2,1,0:T(8,128)(2,1)}) custom-call(s32[1]{0:T(128)} %bitcast.7.refs_0_, f32[4,96,768]{2,1,0:T(8,128)S(1)} %copy-done.1, bf16[4,96,768]{2,1,0:T(8,128)(2,1)} %collective-permute-done.16.refs_2_), custom_call_target="tpu_custom_call" | custom-call | flops 1 | bytes 3000000 | tf_op jit(solution)/shard_map/fold/pallas_call | solution.py:473
  140.4 7.5 %collective-permute-done.27.refs_2_ = bf16[2,96,960]{2,1,0:T(8,128)(2,1)S(1)} collective-permute-done((bf16[2,96,960]{2,1,0:T(8,128)(2,1)}, bf16[2,96,960]{2,1,0:T(8,128)(2,1)S(1)}, u32[]{:S(2)}, u32[]{:S(2)}) %collective-permute-start.27) | collective-permute-done | bytes 368672 | tf_op jit(solution)/shard_map/ppermute | solution.py:1799
  147.9 2.3 %collective-permute-start.28 = (bf16[1,96,960]{2,1,0:T(8,128)(2,1)S(1)}, bf16[1,96,960]{2,1,0:T(8,128)(2,1)S(1)}, u32[]{:S(2)}, u32[]{:S(2)}) collective-permute-start(bf16[1,96,960]{2,1,0:T(8,128)(2,1)S(1)} %get-tuple-element.197), channel_id=1, source_target_pairs={{0,4},{1,5},{2,6},{3,7},{4,0},{5,1},{6,2},{7,3},{8,12},{9,13},{10,... | collective-permute-start | bytes 552968 | tf_op jit(solution)/shard_map/ppermute | solution.py:1799
  152.9 5.5 %final.1 = f32[128,768]{1,0:T(8,128)} custom-call(bf16[8,288,128]{2,1,0:T(8,128)(2,1)} %copy-done.8, bf16[128,768]{1,0:T(8,128)(2,1)} %get-tuple-element.142.refs_2_.tokens, f32[128,768]{1,0:T(8,128)} %get-tuple-element.184.residual, f32[32,768]{1,0:T(8,128)} %get-tuple-element.143.refs_4_.norm_rows.rows, bf16[768,2304]{1,0:T(8,128)(2,1)} %weight_in.1), custom_call_target="tpu_custom_call" | custom-call | flops 1 | bytes 16500000 | tf_op jit(solution)/shard_map/final/pallas_call | solution.py:473
  158.4 7.2 %collective-permute-done.18.up_got = bf16[1,96,768]{2,1,0:T(8,128)(2,1)S(1)} collective-permute-done((bf16[1,96,768]{2,1,0:T(8,128)(2,1)S(1)}, bf16[1,96,768]{2,1,0:T(8,128)(2,1)S(1)}, u32[]{:S(2)}, u32[]{:S(2)}) %collective-permute-start.18) | collective-permute-done | bytes 147488 | tf_op jit(solution)/shard_map/ppermute | solution.py:1799
  170.0 4.5 %collective-permute-done.29.refs_3_ = bf16[96,1792]{1,0:T(8,128)(2,1)S(1)} collective-permute-done((bf16[96,1792]{1,0:T(8,128)(2,1)S(1)}, bf16[96,1792]{1,0:T(8,128)(2,1)S(1)}, u32[]{:S(2)}, u32[]{:S(2)}) %collective-permute-start.29) | collective-permute-done | bytes 344096 | tf_op jit(solution)/shard_map/ppermute | solution.py:1799
  174.6 1.6 collective-permute-done.31.refs_4_
  176.2 1.7 collect.1
  (115 shorter events, 32.1 us)
Async XLA Ops:
  2.7 10.3 %collective-permute-start.1 = (bf16[128,768]{1,0:T(8,128)(2,1)}, bf16[128,768]{1,0:T(8,128)(2,1)S(1)}, u32[]{:S(2)}, u32[]{:S(2)}) collective-permute-start(bf16[128,768]{1,0:T(8,128)(2,1)} %get-tuple-element.124.refs_1_), channel_id=1, source_target_pairs={{0,2},{1,3},{2,0},{3,1},{4,6},{5,7},{6,4},{7,5},{8,10},{9,11},{10,... | collective-permute-start | bytes 589832 | tf_op jit(solution)/shard_map/ppermute | solution.py:1799
  5.7 15.6 %collective-permute-start = (bf16[128,768]{1,0:T(8,128)(2,1)}, bf16[128,768]{1,0:T(8,128)(2,1)S(1)}, u32[]{:S(2)}, u32[]{:S(2)}) collective-permute-start(bf16[128,768]{1,0:T(8,128)(2,1)} %get-tuple-element.124.refs_1_), channel_id=1, source_target_pairs={{0,1},{1,0},{2,3},{3,2},{4,5},{5,4},{6,7},{7,6},{8,9},{9,8},{10,11... | collective-permute-start | bytes 589832 | tf_op jit(solution)/shard_map/ppermute | solution.py:1799
  7.3 17.4 %collective-permute-start.3 = (bf16[128,768]{1,0:T(8,128)(2,1)}, bf16[128,768]{1,0:T(8,128)(2,1)S(1)}, u32[]{:S(2)}, u32[]{:S(2)}) collective-permute-start(bf16[128,768]{1,0:T(8,128)(2,1)} %get-tuple-element.124.refs_1_), channel_id=1, source_target_pairs={{0,4},{1,5},{2,6},{3,7},{4,0},{5,1},{6,2},{7,3},{8,12},{9,13},{10,... | collective-permute-start | bytes 589832 | tf_op jit(solution)/shard_map/ppermute | solution.py:1799
  9.9 14.8 %collective-permute-start.4 = (bf16[128,768]{1,0:T(8,128)(2,1)}, bf16[128,768]{1,0:T(8,128)(2,1)S(1)}, u32[]{:S(2)}, u32[]{:S(2)}) collective-permute-start(bf16[128,768]{1,0:T(8,128)(2,1)} %get-tuple-element.124.refs_1_), channel_id=1, source_target_pairs={{0,6},{1,7},{2,4},{3,5},{4,2},{5,3},{6,0},{7,1},{8,14},{9,15},{10,... | collective-permute-start | bytes 589832 | tf_op jit(solution)/shard_map/ppermute | solution.py:1799
  13.0 11.6 %collective-permute-start.2 = (bf16[128,768]{1,0:T(8,128)(2,1)S(1)}, bf16[128,768]{1,0:T(8,128)(2,1)S(1)}, u32[]{:S(2)}, u32[]{:S(2)}) collective-permute-start(bf16[128,768]{1,0:T(8,128)(2,1)S(1)} %collective-permute-done.1.refs_3_), channel_id=1, source_target_pairs={{0,1},{1,0},{2,3},{3,2},{4,5},{5,4},{6,7},{7,6},{8,9},{9,8},{10,11... | collective-permute-start | bytes 589832 | tf_op jit(solution)/shard_map/ppermute | solution.py:1799
  24.6 10.1 %collective-permute-start.5 = (bf16[128,768]{1,0:T(8,128)(2,1)S(1)}, bf16[128,768]{1,0:T(8,128)(2,1)S(1)}, u32[]{:S(2)}, u32[]{:S(2)}) collective-permute-start(bf16[128,768]{1,0:T(8,128)(2,1)S(1)} %collective-permute-done.3.refs_5_), channel_id=1, source_target_pairs={{0,1},{1,0},{2,3},{3,2},{4,5},{5,4},{6,7},{7,6},{8,9},{9,8},{10,11... | collective-permute-start | bytes 589832 | tf_op jit(solution)/shard_map/ppermute | solution.py:1799
  25.2 9.5 %collective-permute-start.6 = (bf16[128,768]{1,0:T(8,128)(2,1)S(1)}, bf16[128,768]{1,0:T(8,128)(2,1)S(1)}, u32[]{:S(2)}, u32[]{:S(2)}) collective-permute-start(bf16[128,768]{1,0:T(8,128)(2,1)S(1)} %collective-permute-done.4.refs_7_), channel_id=1, source_target_pairs={{0,1},{1,0},{2,3},{3,2},{4,5},{5,4},{6,7},{7,6},{8,9},{9,8},{10,11... | collective-permute-start | bytes 589832 | tf_op jit(solution)/shard_map/ppermute | solution.py:1799
  26.7 23.3 %collective-permute-start.8 = (bf16[128,768]{1,0:T(8,128)(2,1)S(1)}, bf16[128,768]{1,0:T(8,128)(2,1)S(1)}, u32[]{:S(2)}, u32[]{:S(2)}) collective-permute-start(bf16[128,768]{1,0:T(8,128)(2,1)S(1)} %copy-done.10), channel_id=1, source_target_pairs={{0,16},{8,24},{16,0},{24,8},{1,17},{9,25},{17,1},{25,9},{2,18},{10... | collective-permute-start | bytes 589832 | tf_op jit(solution)/shard_map/ppermute | solution.py:1799
  44.6 13.1 %all-to-all-start = ((bf16[8,96,128]{2,1,0:T(8,128)(2,1)}), bf16[8,96,128]{2,1,0:T(8,128)(2,1)S(1)}, u32[]{:S(2)}, u32[]{:S(2)}) async-start(bf16[8,96,128]{2,1,0:T(8,128)(2,1)} %get-tuple-element.139), calls=%async_computation | async-start | bytes 393216 | tf_op jit(solution)/shard_map/all_to_all | solution.py:2031
  50.0 1.7 collective-permute-start.9
  69.0 27.9 %collective-permute-start.11 = (bf16[128,1536]{1,0:T(8,128)(2,1)}, bf16[128,1536]{1,0:T(8,128)(2,1)}, u32[]{:S(2)}, u32[]{:S(2)}) collective-permute-start(bf16[128,1536]{1,0:T(8,128)(2,1)} %get-tuple-element.156.refs_1_), channel_id=1, source_target_pairs={{0,16},{8,24},{16,0},{24,8},{1,17},{9,25},{17,1},{25,9},{2,18},{10... | collective-permute-start | bytes 1179656 | tf_op jit(solution)/shard_map/ppermute | solution.py:1799
  70.2 11.1 %all-to-all-start.1 = ((bf16[8,96,128]{2,1,0:T(8,128)(2,1)}), bf16[8,96,128]{2,1,0:T(8,128)(2,1)S(1)}, u32[]{:S(2)}, u32[]{:S(2)}) async-start(bf16[8,96,128]{2,1,0:T(8,128)(2,1)} %get-tuple-element.146), calls=%async_computation.1 | async-start | bytes 393216 | tf_op jit(solution)/shard_map/all_to_all | solution.py:2099
  73.6 28.3 %collective-permute-start.13 = (bf16[128,1792]{1,0:T(8,128)(2,1)}, bf16[128,1792]{1,0:T(8,128)(2,1)}, u32[]{:S(2)}, u32[]{:S(2)}) collective-permute-start(bf16[128,1792]{1,0:T(8,128)(2,1)} %get-tuple-element.162), channel_id=1, source_target_pairs={{0,8},{8,0},{16,24},{24,16},{1,9},{9,1},{17,25},{25,17},{2,10},{10... | collective-permute-start | bytes 1376264 | tf_op jit(solution)/shard_map/ppermute | solution.py:1799
  73.6 28.2 %collective-permute-start.14 = (bf16[128,1792]{1,0:T(8,128)(2,1)}, bf16[128,1792]{1,0:T(8,128)(2,1)}, u32[]{:S(2)}, u32[]{:S(2)}) collective-permute-start(bf16[128,1792]{1,0:T(8,128)(2,1)} %get-tuple-element.163), channel_id=1, source_target_pairs={{0,16},{8,24},{16,0},{24,8},{1,17},{9,25},{17,1},{25,9},{2,18},{10... | collective-permute-start | bytes 1376264 | tf_op jit(solution)/shard_map/ppermute | solution.py:1799
  74.6 27.2 %collective-permute-start.15 = (bf16[128,1792]{1,0:T(8,128)(2,1)}, bf16[128,1792]{1,0:T(8,128)(2,1)}, u32[]{:S(2)}, u32[]{:S(2)}) collective-permute-start(bf16[128,1792]{1,0:T(8,128)(2,1)} %get-tuple-element.164), channel_id=1, source_target_pairs={{0,24},{8,16},{16,8},{24,0},{1,25},{9,17},{17,9},{25,1},{2,26},{10... | collective-permute-start | bytes 1376264 | tf_op jit(solution)/shard_map/ppermute | solution.py:1799
  75.5 26.3 %collective-permute-start.10 = (bf16[128,1536]{1,0:T(8,128)(2,1)}, bf16[128,1536]{1,0:T(8,128)(2,1)}, u32[]{:S(2)}, u32[]{:S(2)}) collective-permute-start(bf16[128,1536]{1,0:T(8,128)(2,1)} %get-tuple-element.156.refs_1_), channel_id=1, source_target_pairs={{0,8},{8,0},{16,24},{24,16},{1,9},{9,1},{17,25},{25,17},{2,10},{10... | collective-permute-start | bytes 1179656 | tf_op jit(solution)/shard_map/ppermute | solution.py:1799
  93.1 25.3 %all-to-all-start.2 = ((bf16[8,288,128]{2,1,0:T(8,128)(2,1)}), bf16[8,288,128]{2,1,0:T(8,128)(2,1)S(1)}, u32[]{:S(2)}, u32[]{:S(2)}) async-start(bf16[8,288,128]{2,1,0:T(8,128)(2,1)} %get-tuple-element.179), calls=%async_computation.2 | async-start | bytes 1179648 | tf_op jit(solution)/shard_map/all_to_all | solution.py:2146
  96.9 5.0 %collective-permute-start.12 = (bf16[128,1536]{1,0:T(8,128)(2,1)}, bf16[128,1536]{1,0:T(8,128)(2,1)}, u32[]{:S(2)}, u32[]{:S(2)}) collective-permute-start(bf16[128,1536]{1,0:T(8,128)(2,1)} %collective-permute-done.11.refs_3_), channel_id=1, source_target_pairs={{0,8},{8,0},{16,24},{24,16},{1,9},{9,1},{17,25},{25,17},{2,10},{10... | collective-permute-start | bytes 1179656 | tf_op jit(solution)/shard_map/ppermute | solution.py:1799
  107.4 10.9 %collective-permute-start.19 = (bf16[2,576,128]{2,1,0:T(8,128)(2,1)S(1)}, bf16[2,576,128]{2,1,0:T(8,128)(2,1)S(1)}, u32[]{:S(2)}, u32[]{:S(2)}) collective-permute-start(bf16[2,576,128]{2,1,0:T(8,128)(2,1)S(1)} %fusion), channel_id=1, source_target_pairs={{0,8},{8,0},{16,24},{24,16},{1,9},{9,1},{17,25},{25,17},{2,10},{10... | collective-permute-start | bytes 884744 | tf_op jit(solution)/shard_map/ppermute | solution.py:1799
  108.0 29.1 %collective-permute-start.16 = (bf16[4,96,768]{2,1,0:T(8,128)(2,1)}, bf16[4,96,768]{2,1,0:T(8,128)(2,1)}, u32[]{:S(2)}, u32[]{:S(2)}) collective-permute-start(bf16[4,96,768]{2,1,0:T(8,128)(2,1)} %get-tuple-element.168), channel_id=1, source_target_pairs={{0,1},{1,0},{2,3},{3,2},{4,5},{5,4},{6,7},{7,6},{8,9},{9,8},{10,11... | collective-permute-start | bytes 1769480 | tf_op jit(solution)/shard_map/ppermute | solution.py:1799
  109.6 22.5 %collective-permute-start.26 = (bf16[4,96,960]{2,1,0:T(8,128)(2,1)}, bf16[4,96,960]{2,1,0:T(8,128)(2,1)}, u32[]{:S(2)}, u32[]{:S(2)}) collective-permute-start(bf16[4,96,960]{2,1,0:T(8,128)(2,1)} %get-tuple-element.193), channel_id=1, source_target_pairs={{0,2},{1,3},{2,0},{3,1},{4,6},{5,7},{6,4},{7,5},{8,10},{9,11},{10,... | collective-permute-start | bytes 2211848 | tf_op jit(solution)/shard_map/ppermute | solution.py:1799
  119.6 6.7 %collective-permute-start.20 = (bf16[1,576,128]{2,1,0:T(8,128)(2,1)S(1)}, bf16[1,576,128]{2,1,0:T(8,128)(2,1)S(1)}, u32[]{:S(2)}, u32[]{:S(2)}) collective-permute-start(bf16[1,576,128]{2,1,0:T(8,128)(2,1)S(1)} %dynamic-slice_convert_fusion), channel_id=1, source_target_pairs={{0,16},{8,24},{16,0},{24,8},{1,17},{9,25},{17,1},{25,9},{2,18},{10... | collective-permute-start | bytes 442376 | tf_op jit(solution)/shard_map/ppermute | solution.py:1799
  120.9 6.1 %collective-permute-start.22 = (f32[1,96,128]{2,1,0:T(8,128)S(1)}, f32[1,96,128]{2,1,0:T(8,128)S(1)}, u32[]{:S(2)}, u32[]{:S(2)}) collective-permute-start(f32[1,96,128]{2,1,0:T(8,128)S(1)} %get-tuple-element.222), channel_id=1, source_target_pairs={{0,16},{8,24},{16,0},{24,8},{1,17},{9,25},{17,1},{25,9},{2,18},{10... | collective-permute-start | bytes 147464 | tf_op jit(solution)/shard_map/ppermute | solution.py:1799
  128.3 22.7 %all-to-all-start.3 = ((bf16[8,184,128]{2,1,0:T(8,128)(2,1)}), bf16[8,184,128]{2,1,0:T(8,128)(2,1)S(1)}, u32[]{:S(2)}, u32[]{:S(2)}) async-start(bf16[8,184,128]{2,1,0:T(8,128)(2,1)} %get-tuple-element.185), calls=%async_computation.3 | async-start | bytes 753664 | tf_op jit(solution)/shard_map/all_to_all | solution.py:2250
  135.0 12.8 %collective-permute-start.27 = (bf16[2,96,960]{2,1,0:T(8,128)(2,1)}, bf16[2,96,960]{2,1,0:T(8,128)(2,1)S(1)}, u32[]{:S(2)}, u32[]{:S(2)}) collective-permute-start(bf16[2,96,960]{2,1,0:T(8,128)(2,1)} %get-tuple-element.195), channel_id=1, source_target_pairs={{0,1},{1,0},{2,3},{3,2},{4,5},{5,4},{6,7},{7,6},{8,9},{9,8},{10,11... | collective-permute-start | bytes 1105928 | tf_op jit(solution)/shard_map/ppermute | solution.py:1799
  138.9 11.3 %collective-permute-start.17 = (bf16[2,96,768]{2,1,0:T(8,128)(2,1)}, bf16[2,96,768]{2,1,0:T(8,128)(2,1)S(1)}, u32[]{:S(2)}, u32[]{:S(2)}) collective-permute-start(bf16[2,96,768]{2,1,0:T(8,128)(2,1)} %get-tuple-element.170), channel_id=1, source_target_pairs={{0,2},{1,3},{2,0},{3,1},{4,6},{5,7},{6,4},{7,5},{8,10},{9,11},{10,... | collective-permute-start | bytes 884744 | tf_op jit(solution)/shard_map/ppermute | solution.py:1799
  147.9 17.7 %collective-permute-start.28 = (bf16[1,96,960]{2,1,0:T(8,128)(2,1)S(1)}, bf16[1,96,960]{2,1,0:T(8,128)(2,1)S(1)}, u32[]{:S(2)}, u32[]{:S(2)}) collective-permute-start(bf16[1,96,960]{2,1,0:T(8,128)(2,1)S(1)} %get-tuple-element.197), channel_id=1, source_target_pairs={{0,4},{1,5},{2,6},{3,7},{4,0},{5,1},{6,2},{7,3},{8,12},{9,13},{10,... | collective-permute-start | bytes 552968 | tf_op jit(solution)/shard_map/ppermute | solution.py:1799
  150.3 15.3 %collective-permute-start.18 = (bf16[1,96,768]{2,1,0:T(8,128)(2,1)S(1)}, bf16[1,96,768]{2,1,0:T(8,128)(2,1)S(1)}, u32[]{:S(2)}, u32[]{:S(2)}) collective-permute-start(bf16[1,96,768]{2,1,0:T(8,128)(2,1)S(1)} %get-tuple-element.171), channel_id=1, source_target_pairs={{0,4},{1,5},{2,6},{3,7},{4,0},{5,1},{6,2},{7,3},{8,12},{9,13},{10,... | collective-permute-start | bytes 442376 | tf_op jit(solution)/shard_map/ppermute | solution.py:1799
  151.9 14.8 %collective-permute-start.24 = (bf16[880,128]{1,0:T(8,128)(2,1)S(1)}, bf16[880,128]{1,0:T(8,128)(2,1)S(1)}, u32[]{:S(2)}, u32[]{:S(2)}) collective-permute-start(bf16[880,128]{1,0:T(8,128)(2,1)S(1)} %merge.1.refs_1_), channel_id=1, source_target_pairs={{0,16},{8,24},{16,0},{24,8},{1,17},{9,25},{17,1},{25,9},{2,18},{10... | collective-permute-start | bytes 675848 | tf_op jit(solution)/shard_map/ppermute | solution.py:1799
  165.6 8.9 %collective-permute-start.29 = (bf16[96,1792]{1,0:T(8,128)(2,1)S(1)}, bf16[96,1792]{1,0:T(8,128)(2,1)S(1)}, u32[]{:S(2)}, u32[]{:S(2)}) collective-permute-start(bf16[96,1792]{1,0:T(8,128)(2,1)S(1)} %last_fold.1.refs_1_), channel_id=1, source_target_pairs={{0,16},{8,24},{16,0},{24,8},{1,17},{9,25},{17,1},{25,9},{2,18},{10... | collective-permute-start | bytes 1032200 | tf_op jit(solution)/shard_map/ppermute | solution.py:1799
  166.6 1.8 %collective-permute-start.25 = (bf16[880,128]{1,0:T(8,128)(2,1)S(1)}, bf16[880,128]{1,0:T(8,128)(2,1)S(1)}, u32[]{:S(2)}, u32[]{:S(2)}) collective-permute-start(bf16[880,128]{1,0:T(8,128)(2,1)S(1)} %collective-permute-done.24.refs_3_), channel_id=1, source_target_pairs={{0,8},{8,0},{16,24},{24,16},{1,9},{9,1},{17,25},{25,17},{2,10},{10... | collective-permute-start | bytes 675848 | tf_op jit(solution)/shard_map/ppermute | solution.py:1799
  167.1 7.4 %collective-permute-start.30 = (bf16[96,1792]{1,0:T(8,128)(2,1)S(1)}, bf16[96,1792]{1,0:T(8,128)(2,1)S(1)}, u32[]{:S(2)}, u32[]{:S(2)}) collective-permute-start(bf16[96,1792]{1,0:T(8,128)(2,1)S(1)} %last_fold.1.refs_1_), channel_id=1, source_target_pairs={{0,8},{8,0},{16,24},{24,16},{1,9},{9,1},{17,25},{25,17},{2,10},{10... | collective-permute-start | bytes 1032200 | tf_op jit(solution)/shard_map/ppermute | solution.py:1799
  (27 other events, 181.6 us)
